TPU v7x, 32 devices: a whole 2x2x4 slice. The times are simulated.
32 devices in a mesh: groups: 2 (over x), seq: 4 (over y, core), chan: 4 (over z).
Axes of the slice: x: 2, y: 2, z: 4, core: 2. Of those that a mesh axis runs over, the one named last changes fastest.
Arguments:
- dna_act: bfloat16 [6, 2048, 1280], P('groups', 'seq', 'chan'), parts along dimension 0, may hold values from -5 to 5
- conv_weight: bfloat16 [5, 1280, 1536], P(None, 'chan'), may hold values from -0.078125 to 0.078125
- head_weight: bfloat16 [7611, 1536], P(None, 'chan'), may hold values from -0.078125 to 0.078125
- track_ids: int32 [1024], P('groups'), parts along dimension 0, may hold values from 0 to 7610, as said below
- bin_mask: int32 [6, 1024], P('groups', ('seq', 'chan')), parts along dimension 0, may hold values 0 or 1
- counts: int32 [6, 1024, 512], P('groups', ('seq', 'chan')), parts along dimension 0, may hold values from 0 to 3
Outputs:
- grad_input: bfloat16 [6, 2048, 1280], P('groups', 'seq', 'chan'), parts along dimension 0
- grad_conv: float32 [10, 1280, 1536], P('groups', 'chan', 'seq'), parts along dimension 0
- grad_tracks: float32 [1024, 1536], P(('groups', 'seq'), 'chan'), parts along dimension 0
There are 2 independent parts, one for each index of `groups`. A program takes and returns all parts, laid end to end along the dimension named above; an argument that names none is the same for every part. Nothing has to cross between parts.
Inputs may be any that keep to these rules, and one draw needn't show every extreme that they name: `track_ids`: the 512 track numbers are distinct.
All inputs are finite; a program needn't handle non-finite values. No bound on the sum of `bin_mask` on one device may be relied on, other than what follows from the above.
Results may differ from a plain program's by a relative error of at most 0.011.
Values may be sent and summed in bfloat16 or wider, within the bound.
No kernel may reach another device: no remote copies, remote signals or barrier semaphores. Data moves between devices by JAX's collectives and lax.ppermute only.
A program may use at most 128 MiB of HBM per device.

v0:
```python
import jax
import jax.numpy as jnp
from jax import lax
from jax.experimental import pallas as pl
from jax.experimental.pallas import tpu as pltpu
from jax.sharding import PartitionSpec as P


KSIZE = 5
BF16 = jnp.bfloat16
F32 = jnp.float32

VMEM_LIMIT = 24 * 1024 * 1024


def shift_chan(values, step):
    count = lax.axis_size("chan")
    return lax.ppermute(values, "chan", [(i, (i + step) % count) for i in range(count)])


def swap_seq(values, bit):
    count = lax.axis_size("seq")
    return lax.ppermute(values, "seq", [(i, i ^ bit) for i in range(count)])


def edge_seq(values, step):
    count = lax.axis_size("seq")
    pairs = [(i, i + step) for i in range(count) if 0 <= i + step < count]
    return lax.ppermute(values, "seq", pairs)


def exact_gelu(values):
    return jax.nn.gelu(values, approximate=False)


def in_owner_order(pieces, axis):
    count = len(pieces)
    width = pieces[0].shape[axis]
    joined = jnp.concatenate([pieces[-p % count] for p in range(2 * count)], axis=axis)
    start = (count - lax.axis_index("chan")) * width
    return lax.dynamic_slice_in_dim(joined, start, count * width, axis)


def by_owner(values, axis):
    count = lax.axis_size("chan")
    owner = lax.axis_index("chan")
    width = values.shape[axis] // count
    return [
        lax.dynamic_slice_in_dim(values, (owner + s) % count * width, width, axis)
        for s in range(count)
    ]


def plain_prepare(dna_act, head, tail, conv_weight):
    seq_count, positions, channels = dna_act.shape
    bins = positions // 2
    raw = jnp.concatenate([head, dna_act, tail], axis=1).astype(F32)
    wide = exact_gelu(raw).astype(BF16).astype(F32)
    even = (wide.reshape(seq_count, bins + 2, 2, channels).sum(axis=2) * 0.5).astype(BF16)
    odd = wide[:, 1:-1].reshape(seq_count, bins + 1, 2, channels).sum(axis=2) * 0.5
    odd = odd.astype(BF16)
    windows = jnp.stack(
        [even[:, :bins], odd[:, :bins], even[:, 1:-1], odd[:, 1:], even[:, 2:]]
    )
    slope = jax.vjp(exact_gelu, dna_act.astype(F32))[1](jnp.ones(dna_act.shape, F32))[0]
    return windows, slope, conv_weight


def plain_project(pieces, conv_weight, slabs, after=None):
    chosen = in_owner_order(pieces, 1)
    proj = jnp.einsum("kid,md->kim", conv_weight, chosen, preferred_element_type=F32).astype(BF16)
    width = conv_weight.shape[2] // slabs
    slab = lax.axis_index("seq")
    parts = [
        lax.dynamic_slice_in_dim(chosen, (slab ^ t) * width, width, 1) for t in range(slabs)
    ]
    return proj, parts


def plain_partial(windows, projs, after=None):
    part = jnp.einsum(
        "ksni,kim->snm", windows, jnp.concatenate(projs, 2), preferred_element_type=F32
    )
    parts = by_owner(part, 1)
    return parts[0], [p.astype(BF16) for p in parts[1:]]


def plain_logit_grad(own, others, counts, mask, group, after=None):
    logits = own + sum(o.astype(F32) for o in others)
    block = own.shape[2] // len(group)
    slab = lax.axis_index("seq")
    target = jnp.concatenate(
        [lax.dynamic_slice_in_dim(counts, (slab ^ u) * block, block, 2) for u in group], axis=2
    )
    return (mask[:, :, :1] * (jnp.exp(logits) - target.astype(F32))).astype(BF16)


def plain_mark(after):
    return after[0]


def plain_turn(windows, parts, after=None):
    return windows, parts


def plain_outer(windows, pieces, group, after=None):
    grads = in_owner_order(pieces, 1)
    outer = jnp.einsum("ksni,snm->kim", windows, grads, preferred_element_type=F32)
    blocks = jnp.split(outer, len(group), axis=2)
    kept = blocks[0::2]
    sent = [b.astype(BF16) for b in blocks[1::2]]
    return grads, (grads[:, :1], grads[:, -1:]), kept, sent


def plain_back(grads, projs, edges, slope, after=None):
    _, bins, _ = grads[0].shape
    stacked = jnp.concatenate(projs, axis=2)
    block = projs[0].shape[2]
    slab = lax.axis_index("seq")
    slabs = len(projs)

    def reorder(edge, other):
        flip = slab ^ other
        return jnp.concatenate(
            [lax.dynamic_slice_in_dim(edge, (p ^ flip) * block, block, 2) for p in range(slabs)],
            axis=2,
        )

    from_next = reorder(edges[0], jnp.minimum(slab + 1, slabs - 1))
    from_prev = reorder(edges[1], jnp.maximum(slab - 1, 0))
    wide = jnp.concatenate([from_prev, jnp.concatenate(grads, 2), from_next], axis=1)
    back = jnp.einsum("snm,kim->ksni", wide, stacked, preferred_element_type=F32)
    mid, up, down = slice(1, bins + 1), slice(2, bins + 2), slice(0, bins)
    even = back[0][:, up] + back[1][:, mid] + back[2][:, mid] + back[3][:, down] + back[4][:, down]
    odd = back[0][:, up] + back[1][:, up] + back[2][:, mid] + back[3][:, mid] + back[4][:, down]
    grad_acts = jnp.stack([even, odd], axis=2).reshape(slope.shape) * 0.5
    return (grad_acts * slope).astype(BF16)


def plain_tracks(kept, other, conv_weight, after=None):
    total = (kept + other.astype(F32)).astype(BF16)
    part = jnp.einsum("kim,kid->md", total, conv_weight, preferred_element_type=F32)
    parts = by_owner(part, 1)
    return total, parts[0], [p.astype(BF16) for p in parts[1:]]


def plain_filters(totals, parts, after=None):
    return jnp.einsum(
        "kim,mo->kio",
        jnp.concatenate(totals, 2),
        jnp.concatenate(parts, 0),
        preferred_element_type=F32,
    )


def dot(lhs, rhs, dims=((1,), (0,))):
    return lax.dot_general(lhs, rhs, (dims, ((), ())), preferred_element_type=F32)


def struct(shape, dtype):
    return jax.ShapeDtypeStruct(shape, dtype)


def vmem(shape, dtype):
    return pltpu.VMEM(shape, dtype)


def lanes(index, width):
    return pl.ds(pl.multiple_of(index * width, 128), width)


def rows_of(index, height):
    return pl.ds(pl.multiple_of(index * height, 16), height)


def call(body, arrays, out_shape, scratch=(), after=None):
    where = jnp.stack([lax.axis_index("chan"), lax.axis_index("seq")]).astype(jnp.int32)
    local_spec = pl.BlockSpec(memory_space=pltpu.VMEM)
    specs = [pl.BlockSpec(memory_space=pltpu.SMEM)] + [local_spec] * len(arrays)
    count = len(arrays) + 1
    extra = list(after or ())
    specs = specs + [pl.BlockSpec(memory_space=pl.ANY)] * len(extra)

    def run(*refs):
        body(*refs[:count], *refs[len(specs) :])

    single = not isinstance(out_shape, (list, tuple))
    return pl.pallas_call(
        run,
        in_specs=specs,
        out_specs=local_spec if single else [local_spec] * len(out_shape),
        out_shape=out_shape,
        scratch_shapes=list(scratch),
        compiler_params=pltpu.CompilerParams(vmem_limit_bytes=VMEM_LIMIT),
    )(where, *arrays, *extra)


def lane_tiles(channels):
    return [(t, at, min(128, channels - at)) for t, at in enumerate(range(0, channels, 128))]


def kernel_prepare(dna_act, head, tail, conv_weight):
    seq_count, positions, channels = dna_act.shape
    bins = positions // 2
    tiles = lane_tiles(channels)

    def rounded_gelu(x):
        return (0.5 * x * (1.0 + lax.erf(x * 0.7071067811865476))).astype(BF16).astype(F32)

    def body(x_ref, head_ref, tail_ref, w_ref, win_ref, slope_ref, held_ref, wide, done):
        fetch = pltpu.make_async_copy(w_ref, held_ref, done)
        fetch.start()
        for q in range(seq_count):
            x = x_ref[q].T.astype(F32)
            cdf = 0.5 * (1.0 + lax.erf(x * 0.7071067811865476))
            slope_ref[q] = cdf + x * jnp.exp(-0.5 * x * x) * 0.3989422804014327
            acts = (x * cdf).astype(BF16).astype(F32)
            first = rounded_gelu(head_ref[q].astype(F32))
            last = rounded_gelu(tail_ref[q].astype(F32))
            for t, at, size in tiles:
                part = slice(at, at + size)
                wide[t, 8 : 8 + positions, :size] = acts[:, part]
                wide[t, 6:8, :size] = first[:, part]
                wide[t, 8 + positions : 10 + positions, :size] = last[:, part]
                reads = [
                    wide[t, pl.ds(6 + r, bins, stride=2), :][:, :size] for r in range(KSIZE + 1)
                ]
                for k in range(KSIZE):
                    win_ref[k, q, :, part] = ((reads[k] + reads[k + 1]) * 0.5).astype(BF16)
        fetch.wait()

    local_spec = pl.BlockSpec(memory_space=pltpu.VMEM)
    return pl.pallas_call(
        body,
        in_specs=[local_spec] * 3 + [pl.BlockSpec(memory_space=pltpu.HBM)],
        out_specs=[local_spec] * 3,
        out_shape=[
            vmem((KSIZE, seq_count, bins, channels), BF16),
            vmem(dna_act.shape, F32),
            vmem(conv_weight.shape, BF16),
        ],
        scratch_shapes=[
            pltpu.VMEM((len(tiles), positions + 16, 128), F32),
            pltpu.SemaphoreType.DMA(()),
        ],
        compiler_params=pltpu.CompilerParams(vmem_limit_bytes=VMEM_LIMIT),
    )(jnp.swapaxes(dna_act, 1, 2), head, tail, conv_weight)


def kernel_project(pieces, conv_weight, slabs, after):
    ksize, channels, out_width = conv_weight.shape
    block, cols = pieces[0].shape
    owners = len(pieces)
    width = out_width // slabs

    def body(where, *refs):
        piece_refs, (w_ref, proj_ref), part_refs = (
            refs[:owners], refs[owners : owners + 2], refs[owners + 2 : -1]
        )
        chosen = refs[-1]
        for s in range(owners):
            source = lax.rem(where[0] - s + owners, owners)
            chosen[:, lanes(source, cols)] = piece_refs[s][...]
        for t in range(slabs):
            part_refs[t][...] = chosen[:, lanes(where[1] ^ t, width)]
        turned = chosen[...].T
        for k in range(ksize):
            proj_ref[k] = dot(w_ref[k], turned).astype(BF16)

    outs = call(
        body,
        [*pieces, conv_weight],
        [struct((ksize, channels, block), BF16)] + [struct((block, width), BF16)] * slabs,
        [pltpu.VMEM((block, out_width), BF16)],
        after,
    )
    return outs[0], outs[1:]


def kernel_partial(windows, projs, after):
    ksize, seq_count, bins, _ = windows.shape
    owners = lax.axis_size("chan")
    rows = bins // owners
    block = projs[0].shape[2]
    wide = block * len(projs)

    def body(where, win_ref, *refs):
        proj_refs = refs[: len(projs)]
        out_refs, acc = refs[len(projs) : -1], refs[-1]
        for q in range(seq_count):
            total = None
            for k in range(ksize):
                term = dot(win_ref[k, q], jnp.concatenate([p[k] for p in proj_refs], axis=1))
                total = term if total is None else total + term
            acc[q] = total
            for s in range(owners):
                part = acc[q, rows_of(lax.rem(where[0] + s, owners), rows)]
                out_refs[s][q] = part.astype(out_refs[s].dtype)

    outs = call(
        body,
        [windows, *projs],
        [vmem((seq_count, rows, wide), F32)]
        + [struct((seq_count, rows, wide), BF16)] * (owners - 1),
        [pltpu.VMEM((seq_count, bins, wide), F32)],
        after,
    )
    return outs[0], outs[1:]


def kernel_mark(after):
    def body(where, out_ref):
        out_ref[...] = jnp.zeros((8, 128), jnp.int32) + where[0]

    return call(body, [], vmem((8, 128), jnp.int32), after=after)


def kernel_turn(windows, parts, after):
    ksize, seq_count, bins, channels = windows.shape

    def body(where, win_ref, *refs):
        out_ref = refs[len(parts)]
        for k in range(ksize):
            for q in range(seq_count):
                out_ref[k, :, q * bins : (q + 1) * bins] = win_ref[k, q].T
        for source, target in zip(refs[: len(parts)], refs[len(parts) + 1 :]):
            target[...] = source[...]

    outs = call(
        body,
        [windows, *parts],
        [vmem((ksize, channels, seq_count * bins), BF16)]
        + [struct(part.shape, BF16) for part in parts],
        after=after,
    )
    return outs[0], outs[1:]


def kernel_logit_grad(own, others, counts, mask, group, after):
    seq_count, _, wide = own.shape
    block = wide // len(group)
    inputs = [own, *others]

    def body(where, *refs):
        counts_ref, mask_ref, out_ref = refs[len(inputs) :]
        for s in range(seq_count):
            logits = refs[0][s]
            for other in refs[1 : len(inputs)]:
                logits = logits + other[s].astype(F32)
            target = jnp.concatenate(
                [counts_ref[s, :, lanes(where[1] ^ u, block)] for u in group], axis=1
            )
            mask_wide = jnp.concatenate([mask_ref[s]] * (wide // 128), axis=1)
            out_ref[s] = (mask_wide * (jnp.exp(logits) - target.astype(F32))).astype(BF16)

    return call(body, [*inputs, counts, mask], struct(own.shape, BF16), after=after)


def kernel_outer(turned, pieces, group, after):
    ksize, channels, length = turned.shape
    seq_count, rows, wide = pieces[0].shape
    owners = len(pieces)
    block = wide // len(group)
    bins = length // seq_count

    def body(where, win_ref, *refs):
        piece_refs = refs[:owners]
        grads_ref, low_ref, high_ref, kept_ref, sent_ref = refs[owners:]
        for s in range(owners):
            source = rows_of(lax.rem(where[0] - s + owners, owners), rows)
            for q in range(seq_count):
                grads_ref[q, source] = piece_refs[s][q]
        for q in range(seq_count):
            low_ref[q] = grads_ref[q, 0:1]
            high_ref[q] = grads_ref[q, bins - 1 : bins]
        grads = grads_ref[...].reshape(length, wide)
        for k in range(ksize):
            term = dot(win_ref[k], grads)
            kept_ref[k] = term[:, :block]
            sent_ref[k] = term[:, block:].astype(BF16)

    grads, low, high, kept, sent = call(
        body,
        [turned, *pieces],
        [
            vmem((seq_count, bins, wide), BF16),
            struct((seq_count, 1, wide), BF16),
            struct((seq_count, 1, wide), BF16),
            vmem((ksize, channels, block), F32),
            struct((ksize, channels, block), BF16),
        ],
        after=after,
    )
    return grads, (low, high), [kept], [sent]


def kernel_back(grads, projs, edges, slope, after):
    seq_count, positions, channels = slope.shape
    bins = positions // 2
    ksize, _, block = projs[0].shape
    slabs = len(projs)
    tiles = lane_tiles(channels)

    def body(where, *refs):
        grad_refs = refs[: len(grads)]
        proj_refs = refs[len(grads) : len(grads) + slabs]
        next_ref, prev_ref, slope_ref, out_ref, shifted, both = refs[len(grads) + slabs :]
        slab = where[1]

        def reorder(ref, q, other):
            flip = slab ^ other
            row = jnp.concatenate(
                [ref[q, :, lanes(p ^ flip, block)] for p in range(slabs)], axis=1
            )
            return jnp.broadcast_to(row.astype(F32), (16, slabs * block)).astype(BF16)

        for q in range(seq_count):
            from_next = reorder(next_ref, q, jnp.minimum(slab + 1, slabs - 1))
            from_prev = reorder(prev_ref, q, jnp.maximum(slab - 1, 0))
            grad = jnp.concatenate([g[q] for g in grad_refs], axis=1)
            stay, moved = [], []
            for k in range(ksize):
                proj = jnp.concatenate([p[k] for p in proj_refs], axis=1)
                back = dot(grad, proj, ((1,), (1,)))
                stay.append(back)
                if k == 2:
                    moved.append(None)
                    continue
                edge = dot(from_next if k < 2 else from_prev, proj, ((1,), (1,)))[:8]
                shifted[k, 8 : 8 + bins] = back
                if k < 2:
                    shifted[k, 8 + bins : 16 + bins] = edge
                    moved.append(shifted[k, 9 : 9 + bins])
                else:
                    shifted[k, 0:8] = edge
                    moved.append(shifted[k, 7 : 7 + bins])
            even = moved[0] + stay[1] + stay[2] + moved[3] + moved[4]
            odd = moved[0] + moved[1] + stay[2] + stay[3] + moved[4]
            for t, at, size in tiles:
                part = slice(at, at + size)
                fill = [jnp.zeros((bins, 128 - size), F32)] if size < 128 else []
                both[t, pl.ds(0, bins, stride=2), :] = jnp.concatenate(
                    [even[:, part], *fill], axis=1
                )
                both[t, pl.ds(1, bins, stride=2), :] = jnp.concatenate(
                    [odd[:, part], *fill], axis=1
                )
                grad_acts = both[t][:, :size]
                out_ref[q, :, part] = (grad_acts * (slope_ref[q, :, part] * 0.5)).astype(BF16)

    return call(
        body,
        [*grads, *projs, *edges, slope],
        struct(slope.shape, BF16),
        [
            pltpu.VMEM((ksize, bins + 16, channels), F32),
            pltpu.VMEM((len(tiles), positions, 128), F32),
        ],
        after,
    )


def kernel_tracks(kept, other, conv_weight, after):
    ksize, _, out_width = conv_weight.shape
    block = kept.shape[2]
    owners = lax.axis_size("chan")
    cols = out_width // owners

    def body(where, kept_ref, other_ref, w_ref, total_ref, *refs):
        out_refs, acc = refs[:-1], refs[-1]
        for k in range(ksize):
            total = (kept_ref[k] + other_ref[k].astype(F32)).astype(BF16)
            total_ref[k] = total
            term = dot(total, w_ref[k], ((0,), (0,)))
            if k:
                acc[...] += term
            else:
                acc[...] = term
        for s in range(owners):
            part = acc[:, lanes(lax.rem(where[0] + s, owners), cols)]
            out_refs[s][...] = part.astype(out_refs[s].dtype)

    outs = call(
        body,
        [kept, other, conv_weight],
        [struct(kept.shape, BF16)]
        + [struct((block, cols), BF16 if s else F32) for s in range(owners)],
        [pltpu.VMEM((block, out_width), F32)],
        after,
    )
    return outs[0], outs[1], outs[2:]


def kernel_filters(totals, parts, after):
    ksize, channels, _ = totals[0].shape
    width = parts[0].shape[1]
    count = len(totals)

    def body(where, *refs):
        right = jnp.concatenate([p[...] for p in refs[count : 2 * count]], axis=0)
        for k in range(ksize):
            left = jnp.concatenate([t[k] for t in refs[:count]], axis=1)
            refs[-1][k] = dot(left, right)

    return call(
        body, [*totals, *parts], struct((ksize, channels, width), F32), after=after
    )


def local(dna_act, conv_weight, head_weight, track_ids, bin_mask, counts):
    seq_count, positions, channels = dna_act.shape
    out_width = conv_weight.shape[2]
    slabs = lax.axis_size("seq")
    owners = lax.axis_size("chan")
    slab = lax.axis_index("seq")
    block = track_ids.shape[0] // slabs
    cols = head_weight.shape[1]
    rows = bin_mask.shape[1]
    far = slabs // 2

    tiled = (
        slabs == 4
        and block % 128 == 0
        and cols % 128 == 0
        and (out_width // slabs) % 128 == 0
        and rows % 16 == 0
        and positions % 32 == 0
        and channels % 16 == 0
    )
    mark, prepare, project, partial, turn, logit_grad, outer, back, tracks, filters = (
        (kernel_mark, kernel_prepare, kernel_project, kernel_partial, kernel_turn, kernel_logit_grad,
         kernel_outer, kernel_back, kernel_tracks, kernel_filters)
        if tiled
        else (plain_mark, plain_prepare, plain_project, plain_partial, plain_turn, plain_logit_grad,
              plain_outer, plain_back, plain_tracks, plain_filters)
    )

    my_ids = lax.dynamic_slice_in_dim(track_ids, (slab ^ far) * block, block)
    my_rows = head_weight.at[my_ids].get(mode="promise_in_bounds", wrap_negative_indices=False)
    pieces = [my_rows] + [shift_chan(my_rows, s) for s in range(1, owners)]
    head = edge_seq(dna_act[:, positions - 2 :], 1)
    tail = edge_seq(dna_act[:, :2], -1)
    windows, slope, conv_weight = prepare(dna_act, head, tail, conv_weight)
    proj, parts = project(pieces, conv_weight, slabs, [slope])

    groups = [[far + u for u in range(far)], list(range(far))]
    slots = {far: proj, 0: swap_seq(proj, far)}

    def spread(first):
        bit = far // 2
        while bit:
            for u in [v for v in slots if v & far == first]:
                slots[u ^ bit] = swap_seq(slots[u], bit)
            bit //= 2

    mask = jnp.broadcast_to(bin_mask.astype(F32)[:, :, None], (seq_count, rows, 128))
    owns, last = [], []
    for name, group in zip("ab", groups):
        if name == "b":
            slots[0], _ = lax.optimization_barrier((slots[0], sends[0]))
        spread(group[0])
        own, sends = partial(windows, [slots[u] for u in group], last)
        owns.append((own, [shift_chan(send, s + 1) for s, send in enumerate(sends)]))
        last = [own]
        if name == "a":
            turned, parts = turn(windows, parts, last)
    parts = [parts[0]] + [swap_seq(parts[t], t) for t in range(1, slabs)]
    rings = []
    for name, group, (own, others) in zip("ab", groups, owns):
        mine = logit_grad(own, others, counts, mask, group, last)
        rings.append([mine] + [shift_chan(mine, s) for s in range(1, owners)])
        last = [mine]
    grads, rims, kept, payload = [], [], {}, {}
    for name, group, ring in zip("ab", groups, rings):
        grad, rim, keeps, sent = outer(turned, ring, group, last)
        grads.append(grad)
        rims.append(rim)
        for n, u in enumerate(group[0::2]):
            received = swap_seq(sent[n], 1)
            kept[u] = keeps[n] + received.astype(F32)
            payload[u] = kept[u].astype(BF16)
        last = [payload[u] for u in group[0::2]]
        if name == "a":
            last = [mark(last)]

    edges = [
        edge_seq(jnp.concatenate([low for low, _ in rims], axis=2), -1),
        edge_seq(jnp.concatenate([high for _, high in rims], axis=2), 1),
    ]
    order = groups[0] + groups[1]

    bit = 2
    while bit < far:
        kept = {u: kept[u] + swap_seq(payload[u ^ bit], bit).astype(F32) for u in kept}
        payload = {u: k.astype(BF16) for u, k in kept.items()}
        bit *= 2
    other = {}
    for u, p in payload.items():
        other[u ^ far] = swap_seq(p, far)
    total, own_tracks, sends = tracks(kept[0], other[0], conv_weight, last)
    grad_input = back(grads, [slots[u] for u in order], edges, slope, [own_tracks])
    totals = {
        u: total if u == 0 else (kept[u] + other[u].astype(F32)).astype(BF16) for u in kept
    }
    grad_tracks = own_tracks
    arrived = [shift_chan(send, s + 1) for s, send in enumerate(sends)]
    for got in arrived:
        grad_tracks = grad_tracks + got.astype(F32)
    for u in list(totals):
        totals[u ^ 1] = swap_seq(totals[u], 1)

    grad_conv = filters(
        [totals[u] for u in order], [parts[u ^ far] for u in order], [grad_input]
    )
    return (grad_input, grad_conv, grad_tracks)


def solution(mesh):
    in_specs = (
        P("groups", "seq", "chan"),
        P(None, "chan", None),
        P(None, "chan"),
        P("groups"),
        P("groups", ("seq", "chan")),
        P("groups", ("seq", "chan"), None),
    )
    out_specs = (
        P("groups", "seq", "chan"),
        P("groups", "chan", "seq"),
        P(("groups", "seq"), "chan"),
    )

    return jax.shard_map(local, mesh=mesh, in_specs=in_specs, out_specs=out_specs, check_vma=False)
```

profile of v0, /device:TPU:0, one launch (start us, length us, event | category | flops | bytes accessed | tf_op | source)
XLA Modules:
  0.0 128.0 jit_solution(4047355841445974500)
XLA Ops:
  0.7 0.8 dynamic_slice.3
  1.5 4.3 %gather_fusion = bf16[128,384]{1,0:T(8,128)(2,1)S(1)} fusion(bf16[7611,384]{1,0:T(8,128)(2,1)} %param.8, s32[1024]{0:T(1024)S(1)} %pad_clamp_fusion), kind=kCustom, calls=%fused_computation | custom fusion | bytes 197120 | tf_op jit(solution)/shard_map/gather | solution.py:539
  5.8 3.1 %collective-permute-start.2 = (bf16[128,384]{1,0:T(8,128)(2,1)S(1)}, bf16[128,384]{1,0:T(8,128)(2,1)S(1)}, u32[]{:S(2)}, u32[]{:S(2)}) collective-permute-start(bf16[128,384]{1,0:T(8,128)(2,1)S(1)} %gather_fusion), channel_id=1, source_target_pairs={{0,1},{1,2},{2,3},{3,0},{4,5},{5,6},{6,7},{7,4},{8,9},{9,10},{10,1... | collective-permute-start | bytes 294920 | tf_op jit(solution)/shard_map/ppermute | solution.py:18
  8.9 2.6 %collective-permute-start.3 = (bf16[128,384]{1,0:T(8,128)(2,1)S(1)}, bf16[128,384]{1,0:T(8,128)(2,1)S(1)}, u32[]{:S(2)}, u32[]{:S(2)}) collective-permute-start(bf16[128,384]{1,0:T(8,128)(2,1)S(1)} %gather_fusion), channel_id=1, source_target_pairs={{0,2},{1,3},{2,0},{3,1},{4,6},{5,7},{6,4},{7,5},{8,10},{9,11},{10,... | collective-permute-start | bytes 294920 | tf_op jit(solution)/shard_map/ppermute | solution.py:18
  11.5 1.3 %collective-permute-start.4 = (bf16[128,384]{1,0:T(8,128)(2,1)S(1)}, bf16[128,384]{1,0:T(8,128)(2,1)S(1)}, u32[]{:S(2)}, u32[]{:S(2)}) collective-permute-start(bf16[128,384]{1,0:T(8,128)(2,1)S(1)} %gather_fusion), channel_id=1, source_target_pairs={{0,3},{1,0},{2,1},{3,2},{4,7},{5,4},{6,5},{7,6},{8,11},{9,8},{10,9... | collective-permute-start | bytes 294920 | tf_op jit(solution)/shard_map/ppermute | solution.py:18
  12.8 1.2 fusion.2
  14.2 1.3 %collective-permute-start = (bf16[3,2,320]{2,1,0:T(2,128)(2,1)S(1)}, bf16[3,2,320]{2,1,0:T(2,128)(2,1)S(1)}, u32[]{:S(2)}, u32[]{:S(2)}) collective-permute-start(bf16[3,2,320]{2,1,0:T(2,128)(2,1)S(1)} %copy.12), channel_id=1, source_target_pairs={{0,4},{4,8},{8,12},{1,5},{5,9},{9,13},{2,6},{6,10},{10,14},{3,7},{... | collective-permute-start | bytes 11528 | tf_op jit(solution)/shard_map/ppermute | solution.py:29
  15.6 1.3 %collective-permute-start.1 = (bf16[3,2,320]{2,1,0:T(2,128)(2,1)S(1)}, bf16[3,2,320]{2,1,0:T(2,128)(2,1)S(1)}, u32[]{:S(2)}, u32[]{:S(2)}) collective-permute-start(bf16[3,2,320]{2,1,0:T(2,128)(2,1)S(1)} %copy.13), channel_id=1, source_target_pairs={{4,0},{8,4},{12,8},{5,1},{9,5},{13,9},{6,2},{10,6},{14,10},{7,3},{... | collective-permute-start | bytes 11528 | tf_op jit(solution)/shard_map/ppermute | solution.py:29
  17.0 3.4 %collective-permute-done.1.tail_ref = bf16[3,2,320]{2,1,0:T(2,128)(2,1)S(1)} collective-permute-done((bf16[3,2,320]{2,1,0:T(2,128)(2,1)S(1)}, bf16[3,2,320]{2,1,0:T(2,128)(2,1)S(1)}, u32[]{:S(2)}, u32[]{:S(2)}) %collective-permute-start.1) | collective-permute-done | bytes 3872 | tf_op jit(solution)/shard_map/ppermute | solution.py:29
  20.5 2.4 %copy-done = bf16[5,320,1536]{2,1,0:T(8,128)(2,1)S(1)} copy-done((bf16[5,320,1536]{2,1,0:T(8,128)(2,1)S(1)}, bf16[5,320,1536]{2,1,0:T(8,128)(2,1)}, u32[]{:S(2)}) %copy-start) | copy-done | bytes 4915224
  22.9 2.7 %shard_map.85 = (bf16[5,3,256,320]{3,2,1,0:T(8,128)(2,1)S(1)}, f32[3,512,320]{2,1,0:T(8,128)S(1)}, bf16[5,320,1536]{2,1,0:T(8,128)(2,1)S(1)}) custom-call(bf16[3,320,512]{2,1,0:T(8,128)(2,1)S(1)} %bitcast.3, bf16[3,2,320]{2,1,0:T(2,128)(2,1)S(1)} %collective-permute-done.head_ref, bf16[3,2,320]{2,1,0:T(2,128)(2,1)S(1)} %collective-permute-done.1.tail_ref, ...), custom_call_target="tpu_custom_call" | custom-call | tf_op jit(solution)/shard_map/pallas_call | solution.py:233
  25.6 2.0 %shard_map.86 = (bf16[5,320,128]{2,1,0:T(8,128)(2,1)S(1)}, bf16[128,384]{1,0:T(8,128)(2,1)S(1)}, bf16[128,384]{1,0:T(8,128)(2,1)S(1)}, bf16[128,384]{1,0:T(8,128)(2,1)S(1)}, bf16[128,384]{1,0:T(8,128)(2,1)S(1)}) custom-call(s32[2]{0:T(128)S(1)} %pad_add_fusion.refs_0_, bf16[128,384]{1,0:T(8,128)(2,1)S(1)} %gather_fusion, ...), custom_call_target="tpu_custom_call" | custom-call | tf_op jit(solution)/shard_map/pallas_call | solution.py:188
  27.6 2.4 %collective-permute-start.5 = (bf16[5,320,128]{2,1,0:T(8,128)(2,1)S(1)}, bf16[5,320,128]{2,1,0:T(8,128)(2,1)S(1)}, u32[]{:S(2)}, u32[]{:S(2)}) collective-permute-start(bf16[5,320,128]{2,1,0:T(8,128)(2,1)S(1)} %get-tuple-element.47.refs_2_.refs_3_), channel_id=1, source_target_pairs={{0,4},{4,0},{8,12},{12,8},{1,5},{5,1},{9,13},{13,9},{2,6},{6,2},{1... | collective-permute-start | bytes 1228808 | tf_op jit(solution)/shard_map/ppermute | solution.py:23
  30.0 1.4 %collective-permute-done.5.refs_3_.refs_4_ = bf16[5,320,128]{2,1,0:T(8,128)(2,1)S(1)} collective-permute-done((bf16[5,320,128]{2,1,0:T(8,128)(2,1)S(1)}, bf16[5,320,128]{2,1,0:T(8,128)(2,1)S(1)}, u32[]{:S(2)}, u32[]{:S(2)}) %collective-permute-start.5) | collective-permute-done | bytes 409632 | tf_op jit(solution)/shard_map/ppermute | solution.py:23
  31.4 1.8 %shard_map.87 = (f32[3,64,256]{2,1,0:T(8,128)S(1)}, bf16[3,64,256]{2,1,0:T(8,128)(2,1)S(1)}, bf16[3,64,256]{2,1,0:T(8,128)(2,1)S(1)}, bf16[3,64,256]{2,1,0:T(8,128)(2,1)S(1)}) custom-call(s32[2]{0:T(128)S(1)} %pad_add_fusion.refs_0_, bf16[5,3,256,320]{3,2,1,0:T(8,128)(2,1)S(1)} %get-tuple-element.40.refs_1_, ...), custom_call_target="tpu_custom_call" | custom-call | tf_op jit(solution)/shard_map/pallas_call | solution.py:188
  33.2 8.3 %collective-permute-done.9.refs_2_.refs_5_ = bf16[5,320,128]{2,1,0:T(8,128)(2,1)S(1)} collective-permute-done((bf16[5,320,128]{2,1,0:T(8,128)(2,1)S(1)}, bf16[5,320,128]{2,1,0:T(8,128)(2,1)S(1)}, u32[]{:S(2)}, u32[]{:S(2)}) %collective-permute-start.9) | collective-permute-done | bytes 409632 | tf_op jit(solution)/shard_map/ppermute | solution.py:23
  42.5 2.8 %collective-permute-start.8 = (bf16[3,64,256]{2,1,0:T(8,128)(2,1)S(1)}, bf16[3,64,256]{2,1,0:T(8,128)(2,1)S(1)}, u32[]{:S(2)}, u32[]{:S(2)}) collective-permute-start(bf16[3,64,256]{2,1,0:T(8,128)(2,1)S(1)} %get-tuple-element.52), channel_id=1, source_target_pairs={{0,3},{1,0},{2,1},{3,2},{4,7},{5,4},{6,5},{7,6},{8,11},{9,8},{10,9... | collective-permute-start | bytes 294920 | tf_op jit(solution)/shard_map/ppermute | solution.py:18
  45.3 1.8 %shard_map.89 = (f32[3,64,256]{2,1,0:T(8,128)S(1)}, bf16[3,64,256]{2,1,0:T(8,128)(2,1)S(1)}, bf16[3,64,256]{2,1,0:T(8,128)(2,1)S(1)}, bf16[3,64,256]{2,1,0:T(8,128)(2,1)S(1)}) custom-call(s32[2]{0:T(128)S(1)} %pad_add_fusion.refs_0_, bf16[5,3,256,320]{3,2,1,0:T(8,128)(2,1)S(1)} %get-tuple-element.40.refs_1_, ...), custom_call_target="tpu_custom_call" | custom-call | tf_op jit(solution)/shard_map/pallas_call | solution.py:188
  47.7 1.6 %collective-permute-start.15 = (bf16[3,64,256]{2,1,0:T(8,128)(2,1)S(1)}, bf16[3,64,256]{2,1,0:T(8,128)(2,1)S(1)}, u32[]{:S(2)}, u32[]{:S(2)}) collective-permute-start(bf16[3,64,256]{2,1,0:T(8,128)(2,1)S(1)} %get-tuple-element.56), channel_id=1, source_target_pairs={{0,2},{1,3},{2,0},{3,1},{4,6},{5,7},{6,4},{7,5},{8,10},{9,11},{10,... | collective-permute-start | bytes 294920 | tf_op jit(solution)/shard_map/ppermute | solution.py:18
  49.3 2.8 %collective-permute-start.16 = (bf16[3,64,256]{2,1,0:T(8,128)(2,1)S(1)}, bf16[3,64,256]{2,1,0:T(8,128)(2,1)S(1)}, u32[]{:S(2)}, u32[]{:S(2)}) collective-permute-start(bf16[3,64,256]{2,1,0:T(8,128)(2,1)S(1)} %get-tuple-element.57), channel_id=1, source_target_pairs={{0,3},{1,0},{2,1},{3,2},{4,7},{5,4},{6,5},{7,6},{8,11},{9,8},{10,9... | collective-permute-start | bytes 294920 | tf_op jit(solution)/shard_map/ppermute | solution.py:18
  52.1 1.2 collective-permute-done.7.refs_3_
  54.0 6.9 %collective-permute-start.11 = (bf16[3,64,256]{2,1,0:T(8,128)(2,1)S(1)}, bf16[3,64,256]{2,1,0:T(8,128)(2,1)S(1)}, u32[]{:S(2)}, u32[]{:S(2)}) collective-permute-start(bf16[3,64,256]{2,1,0:T(8,128)(2,1)S(1)} %shard_map.90.refs_7_.refs_2_), channel_id=1, source_target_pairs={{0,1},{1,2},{2,3},{3,0},{4,5},{5,6},{6,7},{7,4},{8,9},{9,10},{10,1... | collective-permute-start | bytes 294920 | tf_op jit(solution)/shard_map/ppermute | solution.py:18
  61.0 2.4 %collective-permute-start.13 = (bf16[3,64,256]{2,1,0:T(8,128)(2,1)S(1)}, bf16[3,64,256]{2,1,0:T(8,128)(2,1)S(1)}, u32[]{:S(2)}, u32[]{:S(2)}) collective-permute-start(bf16[3,64,256]{2,1,0:T(8,128)(2,1)S(1)} %shard_map.90.refs_7_.refs_2_), channel_id=1, source_target_pairs={{0,3},{1,0},{2,1},{3,2},{4,7},{5,4},{6,5},{7,6},{8,11},{9,8},{10,9... | collective-permute-start | bytes 294920 | tf_op jit(solution)/shard_map/ppermute | solution.py:18
  63.4 1.3 %shard_map.88 = (bf16[5,320,768]{2,1,0:T(8,128)(2,1)S(1)}, bf16[128,384]{1,0:T(8,128)(2,1)S(1)}, bf16[128,384]{1,0:T(8,128)(2,1)S(1)}, bf16[128,384]{1,0:T(8,128)(2,1)S(1)}, bf16[128,384]{1,0:T(8,128)(2,1)S(1)}) custom-call(s32[2]{0:T(128)S(1)} %pad_add_fusion.refs_0_, bf16[5,3,256,320]{3,2,1,0:T(8,128)(2,1)S(1)} %get-tuple-element.40.refs_1_, ...), custom_call_target="tpu_custom_call" | custom-call | tf_op jit(solution)/shard_map/pallas_call | solution.py:188
  65.4 4.3 %collective-permute-done.12.refs_4_ = bf16[3,64,256]{2,1,0:T(8,128)(2,1)S(1)} collective-permute-done((bf16[3,64,256]{2,1,0:T(8,128)(2,1)S(1)}, bf16[3,64,256]{2,1,0:T(8,128)(2,1)S(1)}, u32[]{:S(2)}, u32[]{:S(2)}) %collective-permute-start.12) | collective-permute-done | bytes 98336 | tf_op jit(solution)/shard_map/ppermute | solution.py:18
  69.7 1.4 %shard_map.92 = (bf16[3,256,256]{2,1,0:T(8,128)(2,1)S(1)}, bf16[3,1,256]{2,1,0:T(2,128)(2,1)S(1)}, bf16[3,1,256]{2,1,0:T(2,128)(2,1)S(1)}, f32[5,320,128]{2,1,0:T(8,128)S(1)}, bf16[5,320,128]{2,1,0:T(8,128)(2,1)S(1)}) custom-call(s32[2]{0:T(128)S(1)} %pad_add_fusion.refs_0_, bf16[5,320,768]{2,1,0:T(8,128)(2,1)S(1)} %get-tuple-element.49.refs_1_, ...), custom_call_target="tpu_custom_call" | custom-call | tf_op jit(solution)/shard_map/pallas_call | solution.py:188
  71.1 2.1 %collective-permute-start.17 = (bf16[3,64,256]{2,1,0:T(8,128)(2,1)S(1)}, bf16[3,64,256]{2,1,0:T(8,128)(2,1)S(1)}, u32[]{:S(2)}, u32[]{:S(2)}) collective-permute-start(bf16[3,64,256]{2,1,0:T(8,128)(2,1)S(1)} %shard_map.91.refs_6_.refs_2_), channel_id=1, source_target_pairs={{0,1},{1,2},{2,3},{3,0},{4,5},{5,6},{6,7},{7,4},{8,9},{9,10},{10,1... | collective-permute-start | bytes 294920 | tf_op jit(solution)/shard_map/ppermute | solution.py:18
  73.3 0.9 collective-permute-start.18
  74.2 1.5 %collective-permute-start.19 = (bf16[3,64,256]{2,1,0:T(8,128)(2,1)S(1)}, bf16[3,64,256]{2,1,0:T(8,128)(2,1)S(1)}, u32[]{:S(2)}, u32[]{:S(2)}) collective-permute-start(bf16[3,64,256]{2,1,0:T(8,128)(2,1)S(1)} %shard_map.91.refs_6_.refs_2_), channel_id=1, source_target_pairs={{0,3},{1,0},{2,1},{3,2},{4,7},{5,4},{6,5},{7,6},{8,11},{9,8},{10,9... | collective-permute-start | bytes 294920 | tf_op jit(solution)/shard_map/ppermute | solution.py:18
  76.4 2.4 %collective-permute-done.17.refs_3_ = bf16[3,64,256]{2,1,0:T(8,128)(2,1)S(1)} collective-permute-done((bf16[3,64,256]{2,1,0:T(8,128)(2,1)S(1)}, bf16[3,64,256]{2,1,0:T(8,128)(2,1)S(1)}, u32[]{:S(2)}, u32[]{:S(2)}) %collective-permute-start.17) | collective-permute-done | bytes 98336 | tf_op jit(solution)/shard_map/ppermute | solution.py:18
  78.8 3.7 %collective-permute-done.18.refs_4_ = bf16[3,64,256]{2,1,0:T(8,128)(2,1)S(1)} collective-permute-done((bf16[3,64,256]{2,1,0:T(8,128)(2,1)S(1)}, bf16[3,64,256]{2,1,0:T(8,128)(2,1)S(1)}, u32[]{:S(2)}, u32[]{:S(2)}) %collective-permute-start.18) | collective-permute-done | bytes 98336 | tf_op jit(solution)/shard_map/ppermute | solution.py:18
  82.4 1.4 %shard_map.94 = (bf16[3,256,256]{2,1,0:T(8,128)(2,1)S(1)}, bf16[3,1,256]{2,1,0:T(2,128)(2,1)S(1)}, bf16[3,1,256]{2,1,0:T(2,128)(2,1)S(1)}, f32[5,320,128]{2,1,0:T(8,128)S(1)}, bf16[5,320,128]{2,1,0:T(8,128)(2,1)S(1)}) custom-call(s32[2]{0:T(128)S(1)} %pad_add_fusion.refs_0_, bf16[5,320,768]{2,1,0:T(8,128)(2,1)S(1)} %get-tuple-element.49.refs_1_, ...), custom_call_target="tpu_custom_call" | custom-call | tf_op jit(solution)/shard_map/pallas_call | solution.py:188
  84.3 1.3 %collective-permute-done.23 = bf16[5,320,128]{2,1,0:T(8,128)(2,1)S(1)} collective-permute-done((bf16[5,320,128]{2,1,0:T(8,128)(2,1)S(1)}, bf16[5,320,128]{2,1,0:T(8,128)(2,1)S(1)}, u32[]{:S(2)}, u32[]{:S(2)}) %collective-permute-start.23) | collective-permute-done | bytes 409632 | tf_op jit(solution)/shard_map/ppermute | solution.py:23
  86.2 2.0 %collective-permute-start.22 = (bf16[3,1,512]{2,1,0:T(2,128)(2,1)S(1)}, bf16[3,1,512]{2,1,0:T(2,128)(2,1)S(1)}, u32[]{:S(2)}, u32[]{:S(2)}) collective-permute-start(bf16[3,1,512]{2,1,0:T(2,128)(2,1)S(1)} %pad_maximum_fusion.1), channel_id=1, source_target_pairs={{0,4},{4,8},{8,12},{1,5},{5,9},{9,13},{2,6},{6,10},{10,14},{3,7},{... | collective-permute-start | bytes 9224 | tf_op jit(solution)/shard_map/ppermute | solution.py:29
  88.2 8.1 %collective-permute-done.24.refs_2_ = bf16[5,320,128]{2,1,0:T(8,128)(2,1)S(1)} collective-permute-done((bf16[5,320,128]{2,1,0:T(8,128)(2,1)S(1)}, bf16[5,320,128]{2,1,0:T(8,128)(2,1)S(1)}, u32[]{:S(2)}, u32[]{:S(2)}) %collective-permute-start.24) | collective-permute-done | bytes 409632 | tf_op jit(solution)/shard_map/ppermute | solution.py:23
  96.3 2.5 %shard_map.95 = (bf16[5,320,128]{2,1,0:T(8,128)(2,1)S(1)}, f32[128,384]{1,0:T(8,128)S(1)}, bf16[128,384]{1,0:T(8,128)(2,1)}, bf16[128,384]{1,0:T(8,128)(2,1)}, bf16[128,384]{1,0:T(8,128)(2,1)S(1)}) custom-call(s32[2]{0:T(128)S(1)} %pad_add_fusion.refs_0_, f32[5,320,128]{2,1,0:T(8,128)S(1)} %get-tuple-element.81.refs_1_, ...), custom_call_target="tpu_custom_call" | custom-call | tf_op jit(solution)/shard_map/pallas_call | solution.py:188
  98.8 5.7 %collective-permute-done.25 = bf16[5,320,128]{2,1,0:T(8,128)(2,1)S(1)} collective-permute-done((bf16[5,320,128]{2,1,0:T(8,128)(2,1)S(1)}, bf16[5,320,128]{2,1,0:T(8,128)(2,1)S(1)}, u32[]{:S(2)}, u32[]{:S(2)}) %collective-permute-start.25) | collective-permute-done | bytes 409632 | tf_op jit(solution)/shard_map/ppermute | solution.py:23
  104.8 1.3 %collective-permute-start.21 = (bf16[3,1,512]{2,1,0:T(2,128)(2,1)S(1)}, bf16[3,1,512]{2,1,0:T(2,128)(2,1)S(1)}, u32[]{:S(2)}, u32[]{:S(2)}) collective-permute-start(bf16[3,1,512]{2,1,0:T(2,128)(2,1)S(1)} %pad_maximum_fusion), channel_id=1, source_target_pairs={{4,0},{8,4},{12,8},{5,1},{9,5},{13,9},{6,2},{10,6},{14,10},{7,3},{... | collective-permute-start | bytes 9224 | tf_op jit(solution)/shard_map/ppermute | solution.py:29
  106.1 2.6 %collective-permute-start.31 = (bf16[128,384]{1,0:T(8,128)(2,1)}, bf16[128,384]{1,0:T(8,128)(2,1)}, u32[]{:S(2)}, u32[]{:S(2)}) collective-permute-start(bf16[128,384]{1,0:T(8,128)(2,1)} %get-tuple-element.74), channel_id=1, source_target_pairs={{0,1},{1,2},{2,3},{3,0},{4,5},{5,6},{6,7},{7,4},{8,9},{9,10},{10,1... | collective-permute-start | bytes 294920 | tf_op jit(solution)/shard_map/ppermute | solution.py:18
  108.7 0.9 collective-permute-start.32
  109.6 1.6 %collective-permute-start.33 = (bf16[128,384]{1,0:T(8,128)(2,1)S(1)}, bf16[128,384]{1,0:T(8,128)(2,1)}, u32[]{:S(2)}, u32[]{:S(2)}) collective-permute-start(bf16[128,384]{1,0:T(8,128)(2,1)S(1)} %get-tuple-element.76), channel_id=1, source_target_pairs={{0,3},{1,0},{2,1},{3,2},{4,7},{5,4},{6,5},{7,6},{8,11},{9,8},{10,9... | collective-permute-start | bytes 294920 | tf_op jit(solution)/shard_map/ppermute | solution.py:18
  111.2 4.3 %shard_map.96.refs_9_ = bf16[3,512,320]{2,1,0:T(8,128)(2,1)S(1)} custom-call(s32[2]{0:T(128)S(1)} %pad_add_fusion.refs_0_, bf16[3,256,256]{2,1,0:T(8,128)(2,1)S(1)} %get-tuple-element.58.refs_1_, bf16[3,256,256]{2,1,0:T(8,128)(2,1)S(1)} %get-tuple-element.61.refs_2_, bf16[5,320,128]{2,1,0:T(8,128)(2,1)S(1)} %get-tuple-element.47.refs_2_.refs_3_, ...), custom_call_target="tpu_custom_call" | custom-call | tf_op jit(solution)/shard_map/pallas_call | solution.py:188
  115.6 1.4 %copy.11 = bf16[3,512,320]{1,2,0:T(8,128)(2,1)} copy(bf16[3,512,320]{2,1,0:T(8,128)(2,1)S(1)} %shard_map.96.refs_9_) | data formatting | bytes 1966080
  116.9 2.1 %collective-permute-start.28 = (bf16[128,384]{1,0:T(8,128)(2,1)S(1)}, bf16[128,384]{1,0:T(8,128)(2,1)S(1)}, u32[]{:S(2)}, u32[]{:S(2)}) collective-permute-start(bf16[128,384]{1,0:T(8,128)(2,1)S(1)} %get-tuple-element.71), channel_id=1, source_target_pairs={{0,4},{4,0},{8,12},{12,8},{1,5},{5,1},{9,13},{13,9},{2,6},{6,2},{1... | collective-permute-start | bytes 294920 | tf_op jit(solution)/shard_map/ppermute | solution.py:23
  119.0 0.7 collective-permute-start.29
  120.5 1.7 %convert_add_fusion.2 = f32[128,384]{1,0:T(8,128)} fusion(bf16[128,384]{1,0:T(8,128)(2,1)} %collective-permute-done.33, bf16[128,384]{1,0:T(8,128)(2,1)} %collective-permute-done.32, f32[128,384]{1,0:T(8,128)S(1)} %get-tuple-element.68.refs_10_, bf16[128,384]{1,0:T(8,128)(2,1)} %collective-permute-done.31), kind=kLoop, calls=%fused_computation.5 | loop fusion | flops 294912 | bytes 688128 | tf_op jit(solution)/shard_map/add | solution.py:608
  122.2 2.5 %collective-permute-done.29.refs_7_ = bf16[128,384]{1,0:T(8,128)(2,1)S(1)} collective-permute-done((bf16[128,384]{1,0:T(8,128)(2,1)S(1)}, bf16[128,384]{1,0:T(8,128)(2,1)S(1)}, u32[]{:S(2)}, u32[]{:S(2)}) %collective-permute-start.29) | collective-permute-done | bytes 98336 | tf_op jit(solution)/shard_map/ppermute | solution.py:23
  125.0 3.0 %shard_map.97 = f32[5,320,384]{2,1,0:T(8,128)} custom-call(s32[2]{0:T(128)S(1)} %pad_add_fusion.refs_0_, bf16[5,320,128]{2,1,0:T(8,128)(2,1)S(1)} %add_convert_fusion.refs_1_, bf16[5,320,128]{2,1,0:T(8,128)(2,1)S(1)} %collective-permute-done.26.refs_2_, bf16[5,320,128]{2,1,0:T(8,128)(2,1)S(1)} %get-tuple-element.69.refs_3_, ...), custom_call_target="tpu_custom_call" | custom-call | tf_op jit(solution)/shard_map/pallas_call | solution.py:188
  (57 shorter events, 6.5 us)
Async XLA Ops:
  0.6 19.8 %copy-start.1 = (bf16[3,512,320]{1,2,0:T(8,128)(2,1)S(1)}, bf16[3,512,320]{1,2,0:T(8,128)(2,1)}, u32[]{:S(2)}) copy-start(bf16[3,512,320]{1,2,0:T(8,128)(2,1)} %param.6) | copy-start | bytes 2949124
  5.8 19.8 %collective-permute-start.2 = (bf16[128,384]{1,0:T(8,128)(2,1)S(1)}, bf16[128,384]{1,0:T(8,128)(2,1)S(1)}, u32[]{:S(2)}, u32[]{:S(2)}) collective-permute-start(bf16[128,384]{1,0:T(8,128)(2,1)S(1)} %gather_fusion), channel_id=1, source_target_pairs={{0,1},{1,2},{2,3},{3,0},{4,5},{5,6},{6,7},{7,4},{8,9},{9,10},{10,1... | collective-permute-start | bytes 294920 | tf_op jit(solution)/shard_map/ppermute | solution.py:18
  8.9 16.7 %collective-permute-start.3 = (bf16[128,384]{1,0:T(8,128)(2,1)S(1)}, bf16[128,384]{1,0:T(8,128)(2,1)S(1)}, u32[]{:S(2)}, u32[]{:S(2)}) collective-permute-start(bf16[128,384]{1,0:T(8,128)(2,1)S(1)} %gather_fusion), channel_id=1, source_target_pairs={{0,2},{1,3},{2,0},{3,1},{4,6},{5,7},{6,4},{7,5},{8,10},{9,11},{10,... | collective-permute-start | bytes 294920 | tf_op jit(solution)/shard_map/ppermute | solution.py:18
  11.5 14.1 %collective-permute-start.4 = (bf16[128,384]{1,0:T(8,128)(2,1)S(1)}, bf16[128,384]{1,0:T(8,128)(2,1)S(1)}, u32[]{:S(2)}, u32[]{:S(2)}) collective-permute-start(bf16[128,384]{1,0:T(8,128)(2,1)S(1)} %gather_fusion), channel_id=1, source_target_pairs={{0,3},{1,0},{2,1},{3,2},{4,7},{5,4},{6,5},{7,6},{8,11},{9,8},{10,9... | collective-permute-start | bytes 294920 | tf_op jit(solution)/shard_map/ppermute | solution.py:18
  14.2 2.9 %collective-permute-start = (bf16[3,2,320]{2,1,0:T(2,128)(2,1)S(1)}, bf16[3,2,320]{2,1,0:T(2,128)(2,1)S(1)}, u32[]{:S(2)}, u32[]{:S(2)}) collective-permute-start(bf16[3,2,320]{2,1,0:T(2,128)(2,1)S(1)} %copy.12), channel_id=1, source_target_pairs={{0,4},{4,8},{8,12},{1,5},{5,9},{9,13},{2,6},{6,10},{10,14},{3,7},{... | collective-permute-start | bytes 11528 | tf_op jit(solution)/shard_map/ppermute | solution.py:29
  15.6 4.8 %collective-permute-start.1 = (bf16[3,2,320]{2,1,0:T(2,128)(2,1)S(1)}, bf16[3,2,320]{2,1,0:T(2,128)(2,1)S(1)}, u32[]{:S(2)}, u32[]{:S(2)}) collective-permute-start(bf16[3,2,320]{2,1,0:T(2,128)(2,1)S(1)} %copy.13), channel_id=1, source_target_pairs={{4,0},{8,4},{12,8},{5,1},{9,5},{13,9},{6,2},{10,6},{14,10},{7,3},{... | collective-permute-start | bytes 11528 | tf_op jit(solution)/shard_map/ppermute | solution.py:29
  20.5 2.4 %copy-start = (bf16[5,320,1536]{2,1,0:T(8,128)(2,1)S(1)}, bf16[5,320,1536]{2,1,0:T(8,128)(2,1)}, u32[]{:S(2)}) copy-start(bf16[5,320,1536]{2,1,0:T(8,128)(2,1)} %w_ref.1) | copy-start | bytes 14745604
  27.6 3.8 %collective-permute-start.5 = (bf16[5,320,128]{2,1,0:T(8,128)(2,1)S(1)}, bf16[5,320,128]{2,1,0:T(8,128)(2,1)S(1)}, u32[]{:S(2)}, u32[]{:S(2)}) collective-permute-start(bf16[5,320,128]{2,1,0:T(8,128)(2,1)S(1)} %get-tuple-element.47.refs_2_.refs_3_), channel_id=1, source_target_pairs={{0,4},{4,0},{8,12},{12,8},{1,5},{5,1},{9,13},{13,9},{2,6},{6,2},{1... | collective-permute-start | bytes 1228808 | tf_op jit(solution)/shard_map/ppermute | solution.py:23
  30.0 11.4 %collective-permute-start.9 = (bf16[5,320,128]{2,1,0:T(8,128)(2,1)S(1)}, bf16[5,320,128]{2,1,0:T(8,128)(2,1)S(1)}, u32[]{:S(2)}, u32[]{:S(2)}) collective-permute-start(bf16[5,320,128]{2,1,0:T(8,128)(2,1)S(1)} %get-tuple-element.47.refs_2_.refs_3_), channel_id=1, source_target_pairs={{0,8},{4,12},{8,0},{12,4},{1,9},{5,13},{9,1},{13,5},{2,10},{6,14},... | collective-permute-start | bytes 1228808 | tf_op jit(solution)/shard_map/ppermute | solution.py:23
  31.4 16.3 %copy-start.3 = (s32[3,64]{1,0:T(4,128)S(1)}, s32[3,64]{1,0:T(4,128)}, u32[]{:S(2)}) copy-start(s32[3,64]{1,0:T(4,128)} %param.10) | copy-start | bytes 2308
  33.2 20.2 %copy-start.2 = (s32[3,64,512]{2,1,0:T(8,128)S(1)}, s32[3,64,512]{2,1,0:T(8,128)}, u32[]{:S(2)}) copy-start(s32[3,64,512]{2,1,0:T(8,128)} %refs_5_.3) | copy-start | bytes 1179652
  41.5 3.8 %collective-permute-start.10 = (bf16[5,320,128]{2,1,0:T(8,128)(2,1)S(1)}, bf16[5,320,128]{2,1,0:T(8,128)(2,1)S(1)}, u32[]{:S(2)}, u32[]{:S(2)}) collective-permute-start(bf16[5,320,128]{2,1,0:T(8,128)(2,1)S(1)} %collective-permute-done.9.refs_2_.refs_5_), channel_id=1, source_target_pairs={{0,4},{4,0},{8,12},{12,8},{1,5},{5,1},{9,13},{13,9},{2,6},{6,2},{1... | collective-permute-start | bytes 1228808 | tf_op jit(solution)/shard_map/ppermute | solution.py:23
  41.5 7.8 %collective-permute-start.6 = (bf16[3,64,256]{2,1,0:T(8,128)(2,1)S(1)}, bf16[3,64,256]{2,1,0:T(8,128)(2,1)S(1)}, u32[]{:S(2)}, u32[]{:S(2)}) collective-permute-start(bf16[3,64,256]{2,1,0:T(8,128)(2,1)S(1)} %get-tuple-element.50), channel_id=1, source_target_pairs={{0,1},{1,2},{2,3},{3,0},{4,5},{5,6},{6,7},{7,4},{8,9},{9,10},{10,1... | collective-permute-start | bytes 294920 | tf_op jit(solution)/shard_map/ppermute | solution.py:18
  42.2 11.1 %collective-permute-start.7 = (bf16[3,64,256]{2,1,0:T(8,128)(2,1)S(1)}, bf16[3,64,256]{2,1,0:T(8,128)(2,1)S(1)}, u32[]{:S(2)}, u32[]{:S(2)}) collective-permute-start(bf16[3,64,256]{2,1,0:T(8,128)(2,1)S(1)} %get-tuple-element.51), channel_id=1, source_target_pairs={{0,2},{1,3},{2,0},{3,1},{4,6},{5,7},{6,4},{7,5},{8,10},{9,11},{10,... | collective-permute-start | bytes 294920 | tf_op jit(solution)/shard_map/ppermute | solution.py:18
  42.5 10.8 %collective-permute-start.8 = (bf16[3,64,256]{2,1,0:T(8,128)(2,1)S(1)}, bf16[3,64,256]{2,1,0:T(8,128)(2,1)S(1)}, u32[]{:S(2)}, u32[]{:S(2)}) collective-permute-start(bf16[3,64,256]{2,1,0:T(8,128)(2,1)S(1)} %get-tuple-element.52), channel_id=1, source_target_pairs={{0,3},{1,0},{2,1},{3,2},{4,7},{5,4},{6,5},{7,6},{8,11},{9,8},{10,9... | collective-permute-start | bytes 294920 | tf_op jit(solution)/shard_map/ppermute | solution.py:18
  47.1 13.9 %collective-permute-start.14 = (bf16[3,64,256]{2,1,0:T(8,128)(2,1)S(1)}, bf16[3,64,256]{2,1,0:T(8,128)(2,1)S(1)}, u32[]{:S(2)}, u32[]{:S(2)}) collective-permute-start(bf16[3,64,256]{2,1,0:T(8,128)(2,1)S(1)} %get-tuple-element.55), channel_id=1, source_target_pairs={{0,1},{1,2},{2,3},{3,0},{4,5},{5,6},{6,7},{7,4},{8,9},{9,10},{10,1... | collective-permute-start | bytes 294920 | tf_op jit(solution)/shard_map/ppermute | solution.py:18
  47.7 17.0 %collective-permute-start.15 = (bf16[3,64,256]{2,1,0:T(8,128)(2,1)S(1)}, bf16[3,64,256]{2,1,0:T(8,128)(2,1)S(1)}, u32[]{:S(2)}, u32[]{:S(2)}) collective-permute-start(bf16[3,64,256]{2,1,0:T(8,128)(2,1)S(1)} %get-tuple-element.56), channel_id=1, source_target_pairs={{0,2},{1,3},{2,0},{3,1},{4,6},{5,7},{6,4},{7,5},{8,10},{9,11},{10,... | collective-permute-start | bytes 294920 | tf_op jit(solution)/shard_map/ppermute | solution.py:18
  49.3 15.5 %collective-permute-start.16 = (bf16[3,64,256]{2,1,0:T(8,128)(2,1)S(1)}, bf16[3,64,256]{2,1,0:T(8,128)(2,1)S(1)}, u32[]{:S(2)}, u32[]{:S(2)}) collective-permute-start(bf16[3,64,256]{2,1,0:T(8,128)(2,1)S(1)} %get-tuple-element.57), channel_id=1, source_target_pairs={{0,3},{1,0},{2,1},{3,2},{4,7},{5,4},{6,5},{7,6},{8,11},{9,8},{10,9... | collective-permute-start | bytes 294920 | tf_op jit(solution)/shard_map/ppermute | solution.py:18
  54.0 11.4 %collective-permute-start.11 = (bf16[3,64,256]{2,1,0:T(8,128)(2,1)S(1)}, bf16[3,64,256]{2,1,0:T(8,128)(2,1)S(1)}, u32[]{:S(2)}, u32[]{:S(2)}) collective-permute-start(bf16[3,64,256]{2,1,0:T(8,128)(2,1)S(1)} %shard_map.90.refs_7_.refs_2_), channel_id=1, source_target_pairs={{0,1},{1,2},{2,3},{3,0},{4,5},{5,6},{6,7},{7,4},{8,9},{9,10},{10,1... | collective-permute-start | bytes 294920 | tf_op jit(solution)/shard_map/ppermute | solution.py:18
  60.9 8.7 %collective-permute-start.12 = (bf16[3,64,256]{2,1,0:T(8,128)(2,1)S(1)}, bf16[3,64,256]{2,1,0:T(8,128)(2,1)S(1)}, u32[]{:S(2)}, u32[]{:S(2)}) collective-permute-start(bf16[3,64,256]{2,1,0:T(8,128)(2,1)S(1)} %shard_map.90.refs_7_.refs_2_), channel_id=1, source_target_pairs={{0,2},{1,3},{2,0},{3,1},{4,6},{5,7},{6,4},{7,5},{8,10},{9,11},{10,... | collective-permute-start | bytes 294920 | tf_op jit(solution)/shard_map/ppermute | solution.py:18
  61.0 8.7 %collective-permute-start.13 = (bf16[3,64,256]{2,1,0:T(8,128)(2,1)S(1)}, bf16[3,64,256]{2,1,0:T(8,128)(2,1)S(1)}, u32[]{:S(2)}, u32[]{:S(2)}) collective-permute-start(bf16[3,64,256]{2,1,0:T(8,128)(2,1)S(1)} %shard_map.90.refs_7_.refs_2_), channel_id=1, source_target_pairs={{0,3},{1,0},{2,1},{3,2},{4,7},{5,4},{6,5},{7,6},{8,11},{9,8},{10,9... | collective-permute-start | bytes 294920 | tf_op jit(solution)/shard_map/ppermute | solution.py:18
  71.1 4.6 %collective-permute-start.20 = (bf16[5,320,128]{2,1,0:T(8,128)(2,1)S(1)}, bf16[5,320,128]{2,1,0:T(8,128)(2,1)S(1)}, u32[]{:S(2)}, u32[]{:S(2)}) collective-permute-start(bf16[5,320,128]{2,1,0:T(8,128)(2,1)S(1)} %get-tuple-element.60), channel_id=1, source_target_pairs={{0,4},{4,0},{8,12},{12,8},{1,5},{5,1},{9,13},{13,9},{2,6},{6,2},{1... | collective-permute-start | bytes 1228808 | tf_op jit(solution)/shard_map/ppermute | solution.py:23
  71.1 7.6 %collective-permute-start.17 = (bf16[3,64,256]{2,1,0:T(8,128)(2,1)S(1)}, bf16[3,64,256]{2,1,0:T(8,128)(2,1)S(1)}, u32[]{:S(2)}, u32[]{:S(2)}) collective-permute-start(bf16[3,64,256]{2,1,0:T(8,128)(2,1)S(1)} %shard_map.91.refs_6_.refs_2_), channel_id=1, source_target_pairs={{0,1},{1,2},{2,3},{3,0},{4,5},{5,6},{6,7},{7,4},{8,9},{9,10},{10,1... | collective-permute-start | bytes 294920 | tf_op jit(solution)/shard_map/ppermute | solution.py:18
  73.3 9.2 %collective-permute-start.18 = (bf16[3,64,256]{2,1,0:T(8,128)(2,1)S(1)}, bf16[3,64,256]{2,1,0:T(8,128)(2,1)S(1)}, u32[]{:S(2)}, u32[]{:S(2)}) collective-permute-start(bf16[3,64,256]{2,1,0:T(8,128)(2,1)S(1)} %shard_map.91.refs_6_.refs_2_), channel_id=1, source_target_pairs={{0,2},{1,3},{2,0},{3,1},{4,6},{5,7},{6,4},{7,5},{8,10},{9,11},{10,... | collective-permute-start | bytes 294920 | tf_op jit(solution)/shard_map/ppermute | solution.py:18
  74.2 8.2 %collective-permute-start.19 = (bf16[3,64,256]{2,1,0:T(8,128)(2,1)S(1)}, bf16[3,64,256]{2,1,0:T(8,128)(2,1)S(1)}, u32[]{:S(2)}, u32[]{:S(2)}) collective-permute-start(bf16[3,64,256]{2,1,0:T(8,128)(2,1)S(1)} %shard_map.91.refs_6_.refs_2_), channel_id=1, source_target_pairs={{0,3},{1,0},{2,1},{3,2},{4,7},{5,4},{6,5},{7,6},{8,11},{9,8},{10,9... | collective-permute-start | bytes 294920 | tf_op jit(solution)/shard_map/ppermute | solution.py:18
  83.8 1.8 %collective-permute-start.23 = (bf16[5,320,128]{2,1,0:T(8,128)(2,1)S(1)}, bf16[5,320,128]{2,1,0:T(8,128)(2,1)S(1)}, u32[]{:S(2)}, u32[]{:S(2)}) collective-permute-start(bf16[5,320,128]{2,1,0:T(8,128)(2,1)S(1)} %get-tuple-element.67), channel_id=1, source_target_pairs={{0,4},{4,0},{8,12},{12,8},{1,5},{5,1},{9,13},{13,9},{2,6},{6,2},{1... | collective-permute-start | bytes 1228808 | tf_op jit(solution)/shard_map/ppermute | solution.py:23
  83.9 12.4 %collective-permute-start.24 = (bf16[5,320,128]{2,1,0:T(8,128)(2,1)S(1)}, bf16[5,320,128]{2,1,0:T(8,128)(2,1)S(1)}, u32[]{:S(2)}, u32[]{:S(2)}) collective-permute-start(bf16[5,320,128]{2,1,0:T(8,128)(2,1)S(1)} %fusion.refs_1_), channel_id=1, source_target_pairs={{0,8},{4,12},{8,0},{12,4},{1,9},{5,13},{9,1},{13,5},{2,10},{6,14},... | collective-permute-start | bytes 1228808 | tf_op jit(solution)/shard_map/ppermute | solution.py:23
  85.8 18.8 %collective-permute-start.25 = (bf16[5,320,128]{2,1,0:T(8,128)(2,1)S(1)}, bf16[5,320,128]{2,1,0:T(8,128)(2,1)S(1)}, u32[]{:S(2)}, u32[]{:S(2)}) collective-permute-start(bf16[5,320,128]{2,1,0:T(8,128)(2,1)S(1)} %get-tuple-element.80.refs_4_), channel_id=1, source_target_pairs={{0,8},{4,12},{8,0},{12,4},{1,9},{5,13},{9,1},{13,5},{2,10},{6,14},... | collective-permute-start | bytes 1228808 | tf_op jit(solution)/shard_map/ppermute | solution.py:23
  86.2 22.5 %collective-permute-start.22 = (bf16[3,1,512]{2,1,0:T(2,128)(2,1)S(1)}, bf16[3,1,512]{2,1,0:T(2,128)(2,1)S(1)}, u32[]{:S(2)}, u32[]{:S(2)}) collective-permute-start(bf16[3,1,512]{2,1,0:T(2,128)(2,1)S(1)} %pad_maximum_fusion.1), channel_id=1, source_target_pairs={{0,4},{4,8},{8,12},{1,5},{5,9},{9,13},{2,6},{6,10},{10,14},{3,7},{... | collective-permute-start | bytes 9224 | tf_op jit(solution)/shard_map/ppermute | solution.py:29
  98.8 26.2 %collective-permute-start.27 = (bf16[5,320,128]{2,1,0:T(8,128)(2,1)S(1)}, bf16[5,320,128]{2,1,0:T(8,128)(2,1)S(1)}, u32[]{:S(2)}, u32[]{:S(2)}) collective-permute-start(bf16[5,320,128]{2,1,0:T(8,128)(2,1)S(1)} %get-tuple-element.69.refs_3_), channel_id=1, source_target_pairs={{0,4},{4,0},{8,12},{12,8},{1,5},{5,1},{9,13},{13,9},{2,6},{6,2},{1... | collective-permute-start | bytes 1228808 | tf_op jit(solution)/shard_map/ppermute | solution.py:23
  104.7 20.3 %collective-permute-start.26 = (bf16[5,320,128]{2,1,0:T(8,128)(2,1)S(1)}, bf16[5,320,128]{2,1,0:T(8,128)(2,1)S(1)}, u32[]{:S(2)}, u32[]{:S(2)}) collective-permute-start(bf16[5,320,128]{2,1,0:T(8,128)(2,1)S(1)} %add_convert_fusion.refs_1_), channel_id=1, source_target_pairs={{0,4},{4,0},{8,12},{12,8},{1,5},{5,1},{9,13},{13,9},{2,6},{6,2},{1... | collective-permute-start | bytes 1228808 | tf_op jit(solution)/shard_map/ppermute | solution.py:23
  104.8 4.8 %collective-permute-start.21 = (bf16[3,1,512]{2,1,0:T(2,128)(2,1)S(1)}, bf16[3,1,512]{2,1,0:T(2,128)(2,1)S(1)}, u32[]{:S(2)}, u32[]{:S(2)}) collective-permute-start(bf16[3,1,512]{2,1,0:T(2,128)(2,1)S(1)} %pad_maximum_fusion), channel_id=1, source_target_pairs={{4,0},{8,4},{12,8},{5,1},{9,5},{13,9},{6,2},{10,6},{14,10},{7,3},{... | collective-permute-start | bytes 9224 | tf_op jit(solution)/shard_map/ppermute | solution.py:29
  106.1 10.8 %collective-permute-start.31 = (bf16[128,384]{1,0:T(8,128)(2,1)}, bf16[128,384]{1,0:T(8,128)(2,1)}, u32[]{:S(2)}, u32[]{:S(2)}) collective-permute-start(bf16[128,384]{1,0:T(8,128)(2,1)} %get-tuple-element.74), channel_id=1, source_target_pairs={{0,1},{1,2},{2,3},{3,0},{4,5},{5,6},{6,7},{7,4},{8,9},{9,10},{10,1... | collective-permute-start | bytes 294920 | tf_op jit(solution)/shard_map/ppermute | solution.py:18
  108.7 10.3 %collective-permute-start.32 = (bf16[128,384]{1,0:T(8,128)(2,1)}, bf16[128,384]{1,0:T(8,128)(2,1)}, u32[]{:S(2)}, u32[]{:S(2)}) collective-permute-start(bf16[128,384]{1,0:T(8,128)(2,1)} %get-tuple-element.75), channel_id=1, source_target_pairs={{0,2},{1,3},{2,0},{3,1},{4,6},{5,7},{6,4},{7,5},{8,10},{9,11},{10,... | collective-permute-start | bytes 294920 | tf_op jit(solution)/shard_map/ppermute | solution.py:18
  109.6 10.1 %collective-permute-start.33 = (bf16[128,384]{1,0:T(8,128)(2,1)S(1)}, bf16[128,384]{1,0:T(8,128)(2,1)}, u32[]{:S(2)}, u32[]{:S(2)}) collective-permute-start(bf16[128,384]{1,0:T(8,128)(2,1)S(1)} %get-tuple-element.76), channel_id=1, source_target_pairs={{0,3},{1,0},{2,1},{3,2},{4,7},{5,4},{6,5},{7,6},{8,11},{9,8},{10,9... | collective-permute-start | bytes 294920 | tf_op jit(solution)/shard_map/ppermute | solution.py:18
  116.9 5.2 %collective-permute-start.28 = (bf16[128,384]{1,0:T(8,128)(2,1)S(1)}, bf16[128,384]{1,0:T(8,128)(2,1)S(1)}, u32[]{:S(2)}, u32[]{:S(2)}) collective-permute-start(bf16[128,384]{1,0:T(8,128)(2,1)S(1)} %get-tuple-element.71), channel_id=1, source_target_pairs={{0,4},{4,0},{8,12},{12,8},{1,5},{5,1},{9,13},{13,9},{2,6},{6,2},{1... | collective-permute-start | bytes 294920 | tf_op jit(solution)/shard_map/ppermute | solution.py:23
  119.0 5.7 %collective-permute-start.29 = (bf16[128,384]{1,0:T(8,128)(2,1)S(1)}, bf16[128,384]{1,0:T(8,128)(2,1)S(1)}, u32[]{:S(2)}, u32[]{:S(2)}) collective-permute-start(bf16[128,384]{1,0:T(8,128)(2,1)S(1)} %get-tuple-element.72), channel_id=1, source_target_pairs={{0,8},{4,12},{8,0},{12,4},{1,9},{5,13},{9,1},{13,5},{2,10},{6,14},... | collective-permute-start | bytes 294920 | tf_op jit(solution)/shard_map/ppermute | solution.py:23
  119.8 5.2 %collective-permute-start.30 = (bf16[128,384]{1,0:T(8,128)(2,1)S(1)}, bf16[128,384]{1,0:T(8,128)(2,1)S(1)}, u32[]{:S(2)}, u32[]{:S(2)}) collective-permute-start(bf16[128,384]{1,0:T(8,128)(2,1)S(1)} %get-tuple-element.73), channel_id=1, source_target_pairs={{0,12},{4,8},{8,4},{12,0},{1,13},{5,9},{9,5},{13,1},{2,14},{6,10},... | collective-permute-start | bytes 294920 | tf_op jit(solution)/shard_map/ppermute | solution.py:23
where the time goes:
time: 129 us; the launch traced here: 128 us
  starting transfers between devices  47.7 us (37%)
  waiting for transfers between devices  42.6 us (33%)
  Pallas kernels  24 us (19%)
  local copies, waits for them, and re-layouts  10.5 us (8%)
  other arithmetic  2.21 us (2%)
    ppermute x18, starting transfers between devices, shift_chan(): lax.ppermute(values, 'chan', [(i, (i + step) % count) for i in range(coun...  34.9 us
    ppermute x12, waiting for transfers between devices, swap_seq(): return lax.ppermute(values, 'seq', [(i, i ^ bit) for i in range(count)])  27.7 us
    pallas_call x12, Pallas kernels, call(): pl.pallas_call(run, in_specs=specs, out_specs=local_spec if single else [...  21.4 us
    ppermute x18, waiting for transfers between devices, shift_chan(): lax.ppermute(values, 'chan', [(i, (i + step) % count) for i in range(coun...  11.5 us
    ppermute x12, starting transfers between devices, swap_seq(): return lax.ppermute(values, 'seq', [(i, i ^ bit) for i in range(count)])  7 us
    ppermute x4, starting transfers between devices, edge_seq(): return lax.ppermute(values, 'seq', pairs)  5.85 us
    gather x1, local copies, waits for them, and re-layouts, local(): head_weight.at[my_ids]  4.26 us
    unnamed x11, local copies, waits for them, and re-layouts  4.11 us
  transfers between devices with their start and end apart: 34, of which 12 were waited for; matrix products, arithmetic and copies ran while one was open for 4% of the time, Pallas kernels for 13%

commit v1 on v0

--- a/solution.py
+++ b/solution.py
@@ -51,7 +51,12 @@
     ]
 
 
-def plain_prepare(dna_act, head, tail, conv_weight):
+def plain_prepare(dna_act, conv_weight):
+    slope = jax.vjp(exact_gelu, dna_act.astype(F32))[1](jnp.ones(dna_act.shape, F32))[0]
+    return dna_act, slope, conv_weight
+
+
+def plain_patch(dna_act, first, last, head, tail, after=None):
     seq_count, positions, channels = dna_act.shape
     bins = positions // 2
     raw = jnp.concatenate([head, dna_act, tail], axis=1).astype(F32)
@@ -59,11 +64,7 @@
     even = (wide.reshape(seq_count, bins + 2, 2, channels).sum(axis=2) * 0.5).astype(BF16)
     odd = wide[:, 1:-1].reshape(seq_count, bins + 1, 2, channels).sum(axis=2) * 0.5
     odd = odd.astype(BF16)
-    windows = jnp.stack(
-        [even[:, :bins], odd[:, :bins], even[:, 1:-1], odd[:, 1:], even[:, 2:]]
-    )
-    slope = jax.vjp(exact_gelu, dna_act.astype(F32))[1](jnp.ones(dna_act.shape, F32))[0]
-    return windows, slope, conv_weight
+    return jnp.stack([even[:, :bins], odd[:, :bins], even[:, 1:-1], odd[:, 1:], even[:, 2:]])
 
 
 def plain_project(pieces, conv_weight, slabs, after=None):
@@ -144,13 +145,14 @@
     return total, parts[0], [p.astype(BF16) for p in parts[1:]]
 
 
-def plain_filters(totals, parts, after=None):
-    return jnp.einsum(
+def plain_filters(totals, parts, shares):
+    grad_conv = jnp.einsum(
         "kim,mo->kio",
         jnp.concatenate(totals, 2),
         jnp.concatenate(parts, 0),
         preferred_element_type=F32,
     )
+    return grad_conv, sum(share.astype(F32) for share in shares)
 
 
 def dot(lhs, rhs, dims=((1,), (0,))):
@@ -199,15 +201,12 @@
     return [(t, at, min(128, channels - at)) for t, at in enumerate(range(0, channels, 128))]
 
 
-def kernel_prepare(dna_act, head, tail, conv_weight):
+def kernel_prepare(dna_act, conv_weight):
     seq_count, positions, channels = dna_act.shape
     bins = positions // 2
     tiles = lane_tiles(channels)
 
-    def rounded_gelu(x):
-        return (0.5 * x * (1.0 + lax.erf(x * 0.7071067811865476))).astype(BF16).astype(F32)
-
-    def body(x_ref, head_ref, tail_ref, w_ref, win_ref, slope_ref, held_ref, wide, done):
+    def body(x_ref, w_ref, win_ref, slope_ref, held_ref, wide, done):
         fetch = pltpu.make_async_copy(w_ref, held_ref, done)
         fetch.start()
         for q in range(seq_count):
@@ -215,13 +214,11 @@
             cdf = 0.5 * (1.0 + lax.erf(x * 0.7071067811865476))
             slope_ref[q] = cdf + x * jnp.exp(-0.5 * x * x) * 0.3989422804014327
             acts = (x * cdf).astype(BF16).astype(F32)
-            first = rounded_gelu(head_ref[q].astype(F32))
-            last = rounded_gelu(tail_ref[q].astype(F32))
             for t, at, size in tiles:
                 part = slice(at, at + size)
                 wide[t, 8 : 8 + positions, :size] = acts[:, part]
-                wide[t, 6:8, :size] = first[:, part]
-                wide[t, 8 + positions : 10 + positions, :size] = last[:, part]
+                wide[t, 0:8] = jnp.zeros((8, 128), F32)
+                wide[t, 8 + positions : 16 + positions] = jnp.zeros((8, 128), F32)
                 reads = [
                     wide[t, pl.ds(6 + r, bins, stride=2), :][:, :size] for r in range(KSIZE + 1)
                 ]
@@ -232,7 +229,7 @@
     local_spec = pl.BlockSpec(memory_space=pltpu.VMEM)
     return pl.pallas_call(
         body,
-        in_specs=[local_spec] * 3 + [pl.BlockSpec(memory_space=pltpu.HBM)],
+        in_specs=[local_spec, pl.BlockSpec(memory_space=pltpu.HBM)],
         out_specs=[local_spec] * 3,
         out_shape=[
             vmem((KSIZE, seq_count, bins, channels), BF16),
@@ -244,7 +241,42 @@
             pltpu.SemaphoreType.DMA(()),
         ],
         compiler_params=pltpu.CompilerParams(vmem_limit_bytes=VMEM_LIMIT),
-    )(jnp.swapaxes(dna_act, 1, 2), head, tail, conv_weight)
+    )(
+        jnp.swapaxes(dna_act, 1, 2),
+        pltpu.with_memory_space_constraint(conv_weight, pltpu.HBM),
+    )
+
+
+def kernel_patch(windows, first, last, head, tail, after):
+    _, seq_count, bins, _ = windows.shape
+
+    def rounded_gelu(ref, q):
+        x = ref[q].astype(F32)
+        return (0.5 * x * (1.0 + lax.erf(x * 0.7071067811865476))).astype(BF16).astype(F32)
+
+    def body(_, first_ref, last_ref, head_ref, tail_ref, *refs):
+        win_ref = refs[-1]
+
+        def put(k, n, one, two):
+            win_ref[k, q, n : n + 1] = ((one + two) * 0.5).astype(BF16)
+
+        for q in range(seq_count):
+            before = rounded_gelu(head_ref, q)
+            behind = rounded_gelu(tail_ref, q)
+            put(0, 0, before[0:1], before[1:2])
+            put(1, 0, before[1:2], rounded_gelu(first_ref, q)[0:1])
+            put(3, bins - 1, rounded_gelu(last_ref, q)[1:2], behind[0:1])
+            put(4, bins - 1, behind[0:1], behind[1:2])
+
+    local_spec = pl.BlockSpec(memory_space=pltpu.VMEM)
+    return pl.pallas_call(
+        body,
+        in_specs=[local_spec] * 5 + [pl.BlockSpec(memory_space=pl.ANY)] * len(after),
+        out_specs=local_spec,
+        out_shape=vmem(windows.shape, BF16),
+        input_output_aliases={0: 0},
+        compiler_params=pltpu.CompilerParams(vmem_limit_bytes=VMEM_LIMIT),
+    )(windows, first, last, head, tail, *after)
 
 
 def kernel_project(pieces, conv_weight, slabs, after):
@@ -445,19 +477,20 @@
                 both[t, pl.ds(1, bins, stride=2), :] = jnp.concatenate(
                     [odd[:, part], *fill], axis=1
                 )
-                grad_acts = both[t][:, :size]
-                out_ref[q, :, part] = (grad_acts * (slope_ref[q, :, part] * 0.5)).astype(BF16)
-
-    return call(
+                grad_acts = both[t][:, :size] * (slope_ref[q, :, part] * 0.5)
+                out_ref[q, part] = grad_acts.astype(BF16).T
+
+    turned = call(
         body,
         [*grads, *projs, *edges, slope],
-        struct(slope.shape, BF16),
+        struct((seq_count, channels, positions), BF16),
         [
             pltpu.VMEM((ksize, bins + 16, channels), F32),
             pltpu.VMEM((len(tiles), positions, 128), F32),
         ],
         after,
     )
+    return jnp.swapaxes(turned, 1, 2)
 
 
 def kernel_tracks(kept, other, conv_weight, after):
@@ -491,20 +524,44 @@
     return outs[0], outs[1], outs[2:]
 
 
-def kernel_filters(totals, parts, after):
+def kernel_filters(totals, parts, shares):
     ksize, channels, _ = totals[0].shape
     width = parts[0].shape[1]
     count = len(totals)
-
-    def body(where, *refs):
-        right = jnp.concatenate([p[...] for p in refs[count : 2 * count]], axis=0)
+    split = [count, 2 * count, 2 * count + len(shares)]
+
+    def body(*refs):
+        total_refs, part_refs, share_refs = (
+            refs[: split[0]], refs[split[0] : split[1]], refs[split[1] : split[2]]
+        )
+        conv_ref, tracks_ref, held, done = refs[split[2] :]
+        right = jnp.concatenate([p[...] for p in part_refs], axis=0)
+        copies = []
         for k in range(ksize):
-            left = jnp.concatenate([t[k] for t in refs[:count]], axis=1)
-            refs[-1][k] = dot(left, right)
-
-    return call(
-        body, [*totals, *parts], struct((ksize, channels, width), F32), after=after
-    )
+            left = jnp.concatenate([t[k] for t in total_refs], axis=1)
+            held[k] = dot(left, right)
+            copies.append(pltpu.make_async_copy(held.at[k], conv_ref.at[k], done.at[k]))
+            copies[-1].start()
+        tracks = share_refs[0][...]
+        for share in share_refs[1:]:
+            tracks = tracks + share[...].astype(F32)
+        tracks_ref[...] = tracks
+        for copy in copies:
+            copy.wait()
+
+    local_spec = pl.BlockSpec(memory_space=pltpu.VMEM)
+    arrays = [*totals, *parts, *shares]
+    return pl.pallas_call(
+        body,
+        in_specs=[local_spec] * len(arrays),
+        out_specs=[pl.BlockSpec(memory_space=pl.ANY), local_spec],
+        out_shape=[struct((ksize, channels, width), F32), struct(shares[0].shape, F32)],
+        scratch_shapes=[
+            pltpu.VMEM((ksize, channels, width), F32),
+            pltpu.SemaphoreType.DMA((ksize,)),
+        ],
+        compiler_params=pltpu.CompilerParams(vmem_limit_bytes=VMEM_LIMIT),
+    )(*arrays)
 
 
 def local(dna_act, conv_weight, head_weight, track_ids, bin_mask, counts):
@@ -527,21 +584,22 @@
         and positions % 32 == 0
         and channels % 16 == 0
     )
-    mark, prepare, project, partial, turn, logit_grad, outer, back, tracks, filters = (
-        (kernel_mark, kernel_prepare, kernel_project, kernel_partial, kernel_turn, kernel_logit_grad,
+    mark, prepare, patch, project, partial, turn, logit_grad, outer, back, tracks, filters = (
+        (kernel_mark, kernel_prepare, kernel_patch, kernel_project, kernel_partial, kernel_turn, kernel_logit_grad,
          kernel_outer, kernel_back, kernel_tracks, kernel_filters)
         if tiled
-        else (plain_mark, plain_prepare, plain_project, plain_partial, plain_turn, plain_logit_grad,
+        else (plain_mark, plain_prepare, plain_patch, plain_project, plain_partial, plain_turn, plain_logit_grad,
               plain_outer, plain_back, plain_tracks, plain_filters)
     )
 
     my_ids = lax.dynamic_slice_in_dim(track_ids, (slab ^ far) * block, block)
     my_rows = head_weight.at[my_ids].get(mode="promise_in_bounds", wrap_negative_indices=False)
     pieces = [my_rows] + [shift_chan(my_rows, s) for s in range(1, owners)]
-    head = edge_seq(dna_act[:, positions - 2 :], 1)
-    tail = edge_seq(dna_act[:, :2], -1)
-    windows, slope, conv_weight = prepare(dna_act, head, tail, conv_weight)
+    first, end = dna_act[:, :2], dna_act[:, positions - 2 :]
+    head, tail = edge_seq(end, 1), edge_seq(first, -1)
+    windows, slope, conv_weight = prepare(dna_act, conv_weight)
     proj, parts = project(pieces, conv_weight, slabs, [slope])
+    windows = patch(windows, first, end, head, tail, [proj])
 
     groups = [[far + u for u in range(far)], list(range(far))]
     slots = {far: proj, 0: swap_seq(proj, far)}
@@ -597,20 +655,17 @@
     other = {}
     for u, p in payload.items():
         other[u ^ far] = swap_seq(p, far)
-    total, own_tracks, sends = tracks(kept[0], other[0], conv_weight, last)
-    grad_input = back(grads, [slots[u] for u in order], edges, slope, [own_tracks])
+    grad_input = back(grads, [slots[u] for u in order], edges, slope, last)
+    total, own_tracks, sends = tracks(kept[0], other[0], conv_weight, [grad_input])
     totals = {
         u: total if u == 0 else (kept[u] + other[u].astype(F32)).astype(BF16) for u in kept
     }
-    grad_tracks = own_tracks
     arrived = [shift_chan(send, s + 1) for s, send in enumerate(sends)]
-    for got in arrived:
-        grad_tracks = grad_tracks + got.astype(F32)
     for u in list(totals):
         totals[u ^ 1] = swap_seq(totals[u], 1)
 
-    grad_conv = filters(
-        [totals[u] for u in order], [parts[u ^ far] for u in order], [grad_input]
+    grad_conv, grad_tracks = filters(
+        [totals[u] for u in order], [parts[u ^ far] for u in order], [own_tracks, *arrived]
     )
     return (grad_input, grad_conv, grad_tracks)
 

time: 129 us -> 134 us (1.039)
  waiting for transfers between devices: 42.6 us -> 22.1 us
  starting transfers between devices: 47.7 us -> 62.1 us
  local copies, waits for them, and re-layouts: 10.5 us -> 18.9 us
  Pallas kernels: 24 us -> 25.7 us
    ppermute x12, waiting for transfers between devices: 27.7 us -> 2.12 us  [swap_seq(): return lax.ppermute(values, 'seq', [(i, i ^ bit) for i in range(count)])]
    ppermute x12, starting transfers between devices: 7 us -> 20.6 us  [swap_seq(): return lax.ppermute(values, 'seq', [(i, i ^ bit) for i in range(count)])]
    unnamed x11 -> x60, local copies, waits for them, and re-layouts: 4.11 us -> 11.2 us
    ppermute x18, waiting for transfers between devices: 11.5 us -> 16.1 us  [shift_chan(): lax.ppermute(values, 'chan', [(i, (i + step) % count) for i in range(coun...]
    pallas_call x1 -> x3, Pallas kernels: 2.68 us -> 5 us  [the longest x1 2.53 us: kernel_filters(): pl.pallas_call(body, in_specs=[local_spec] * len(arrays), out_specs=[pl.B...]
    add x1 -> x0, other arithmetic: 1.7 us -> none  [local(): grad_tracks = grad_tracks + got.astype(F32)]
    pallas_call x0 -> x1, local copies, waits for them, and re-layouts: none -> 1.66 us  [call(): pl.pallas_call(run, in_specs=specs, out_specs=local_spec if single else [...]
    convert_element_type x2, other arithmetic: 0.23 us -> 1.79 us  [local(): payload[u] = kept[u].astype(BF16)]
  transfers between devices with their start and end apart: 34 -> 34, of which waited for: 12 -> 11; matrix products, arithmetic and copies ran while one was open for 4% -> 6% of each run, Pallas kernels for 13% -> 14%
where the time goes in v1:
time: 134 us; the launch traced here: 133 us
  starting transfers between devices  62.1 us (46%)
  Pallas kernels  25.7 us (19%)
  waiting for transfers between devices  22.1 us (16%)
  local copies, waits for them, and re-layouts  18.9 us (14%)
  other arithmetic  3.06 us (2%)
    ppermute x18, starting transfers between devices, shift_chan(): lax.ppermute(values, 'chan', [(i, (i + step) % count) for i in range(coun...  34.9 us
    pallas_call x11, Pallas kernels, call(): pl.pallas_call(run, in_specs=specs, out_specs=local_spec if single else [...  20.7 us
    ppermute x12, starting transfers between devices, swap_seq(): return lax.ppermute(values, 'seq', [(i, i ^ bit) for i in range(count)])  20.6 us
    ppermute x18, waiting for transfers between devices, shift_chan(): lax.ppermute(values, 'chan', [(i, (i + step) % count) for i in range(coun...  16.1 us
    unnamed x60, local copies, waits for them, and re-layouts  11.2 us
    ppermute x4, starting transfers between devices, edge_seq(): return lax.ppermute(values, 'seq', pairs)  6.59 us
    gather x1, local copies, waits for them, and re-layouts, local(): head_weight.at[my_ids]  4.26 us
    ppermute x4, waiting for transfers between devices, edge_seq(): return lax.ppermute(values, 'seq', pairs)  3.89 us
  transfers between devices with their start and end apart: 34, of which 11 were waited for; matrix products, arithmetic and copies ran while one was open for 6% of the time, Pallas kernels for 14%

profile of v1, /device:TPU:0, one launch (start us, length us, event | category | flops | bytes accessed | tf_op | source)
XLA Modules:
  0.0 133.1 jit_solution(12102282815521438430)
XLA Ops:
  1.4 4.3 %gather_fusion = bf16[128,384]{1,0:T(8,128)(2,1)S(1)} fusion(bf16[7611,384]{1,0:T(8,128)(2,1)} %param.8, s32[1024]{0:T(1024)S(1)} %pad_clamp_fusion), kind=kCustom, calls=%fused_computation | custom fusion | bytes 197120 | tf_op jit(solution)/shard_map/gather | solution.py:596
  5.7 3.1 %collective-permute-start.2 = (bf16[128,384]{1,0:T(8,128)(2,1)S(1)}, bf16[128,384]{1,0:T(8,128)(2,1)S(1)}, u32[]{:S(2)}, u32[]{:S(2)}) collective-permute-start(bf16[128,384]{1,0:T(8,128)(2,1)S(1)} %gather_fusion), channel_id=1, source_target_pairs={{0,1},{1,2},{2,3},{3,0},{4,5},{5,6},{6,7},{7,4},{8,9},{9,10},{10,1... | collective-permute-start | bytes 294920 | tf_op jit(solution)/shard_map/ppermute | solution.py:18
  8.8 2.6 %collective-permute-start.3 = (bf16[128,384]{1,0:T(8,128)(2,1)S(1)}, bf16[128,384]{1,0:T(8,128)(2,1)S(1)}, u32[]{:S(2)}, u32[]{:S(2)}) collective-permute-start(bf16[128,384]{1,0:T(8,128)(2,1)S(1)} %gather_fusion), channel_id=1, source_target_pairs={{0,2},{1,3},{2,0},{3,1},{4,6},{5,7},{6,4},{7,5},{8,10},{9,11},{10,... | collective-permute-start | bytes 294920 | tf_op jit(solution)/shard_map/ppermute | solution.py:18
  11.4 1.3 %collective-permute-start.4 = (bf16[128,384]{1,0:T(8,128)(2,1)S(1)}, bf16[128,384]{1,0:T(8,128)(2,1)S(1)}, u32[]{:S(2)}, u32[]{:S(2)}) collective-permute-start(bf16[128,384]{1,0:T(8,128)(2,1)S(1)} %gather_fusion), channel_id=1, source_target_pairs={{0,3},{1,0},{2,1},{3,2},{4,7},{5,4},{6,5},{7,6},{8,11},{9,8},{10,9... | collective-permute-start | bytes 294920 | tf_op jit(solution)/shard_map/ppermute | solution.py:18
  12.7 1.2 copy-done.4
  13.9 2.4 %shard_map.85 = (bf16[5,3,256,320]{3,2,1,0:T(8,128)(2,1)S(1)}, f32[3,512,320]{2,1,0:T(8,128)S(1)}, bf16[5,320,1536]{2,1,0:T(8,128)(2,1)S(1)}) custom-call(bf16[3,320,512]{2,1,0:T(8,128)(2,1)S(1)} %bitcast.6, bf16[5,320,1536]{2,1,0:T(8,128)(2,1)} %w_ref.1), custom_call_target="tpu_custom_call" | custom-call | tf_op jit(solution)/shard_map/pallas_call | solution.py:230
  16.4 1.5 %collective-permute-done.3.refs_3_ = bf16[128,384]{1,0:T(8,128)(2,1)S(1)} collective-permute-done((bf16[128,384]{1,0:T(8,128)(2,1)S(1)}, bf16[128,384]{1,0:T(8,128)(2,1)S(1)}, u32[]{:S(2)}, u32[]{:S(2)}) %collective-permute-start.3) | collective-permute-done | bytes 98336 | tf_op jit(solution)/shard_map/ppermute | solution.py:18
  17.9 1.3 copy-done.6
  21.7 2.0 %shard_map.86 = (bf16[5,320,128]{2,1,0:T(8,128)(2,1)S(1)}, bf16[128,384]{1,0:T(8,128)(2,1)S(1)}, bf16[128,384]{1,0:T(8,128)(2,1)S(1)}, bf16[128,384]{1,0:T(8,128)(2,1)S(1)}, bf16[128,384]{1,0:T(8,128)(2,1)S(1)}) custom-call(s32[2]{0:T(128)S(1)} %pad_add_fusion.refs_0_, bf16[128,384]{1,0:T(8,128)(2,1)S(1)} %gather_fusion, ...), custom_call_target="tpu_custom_call" | custom-call | tf_op jit(solution)/shard_map/pallas_call | solution.py:190
  24.3 1.6 %collective-permute-start.9 = (bf16[5,320,128]{2,1,0:T(8,128)(2,1)S(1)}, bf16[5,320,128]{2,1,0:T(8,128)(2,1)}, u32[]{:S(2)}, u32[]{:S(2)}) collective-permute-start(bf16[5,320,128]{2,1,0:T(8,128)(2,1)S(1)} %get-tuple-element.45.refs_0_.refs_2_.refs_3_), channel_id=1, source_target_pairs={{0,8},{4,12},{8,0},{12,4},{1,9},{5,13},{9,1},{13,5},{2,10},{6,14},... | collective-permute-start | bytes 1228808 | tf_op jit(solution)/shard_map/ppermute | solution.py:23
  27.9 2.1 %collective-permute-start = (bf16[3,2,320]{2,1,0:T(2,128)(2,1)S(1)}, bf16[3,2,320]{2,1,0:T(2,128)(2,1)S(1)}, u32[]{:S(2)}, u32[]{:S(2)}) collective-permute-start(bf16[3,2,320]{2,1,0:T(2,128)(2,1)S(1)} %copy.16.last_ref), channel_id=1, source_target_pairs={{0,4},{4,8},{8,12},{1,5},{5,9},{9,13},{2,6},{6,10},{10,14},{3,7},{... | collective-permute-start | bytes 11528 | tf_op jit(solution)/shard_map/ppermute | solution.py:29
  31.1 1.3 collective-permute-start.1
  32.4 1.8 %collective-permute-done.1.tail_ref = bf16[3,2,320]{2,1,0:T(2,128)(2,1)S(1)} collective-permute-done((bf16[3,2,320]{2,1,0:T(2,128)(2,1)S(1)}, bf16[3,2,320]{2,1,0:T(2,128)(2,1)S(1)}, u32[]{:S(2)}, u32[]{:S(2)}) %collective-permute-start.1) | collective-permute-done | bytes 3872 | tf_op jit(solution)/shard_map/ppermute | solution.py:29
  34.7 2.2 %shard_map.88 = (f32[3,64,256]{2,1,0:T(8,128)S(1)}, bf16[3,64,256]{2,1,0:T(8,128)(2,1)S(1)}, bf16[3,64,256]{2,1,0:T(8,128)(2,1)S(1)}, bf16[3,64,256]{2,1,0:T(8,128)(2,1)S(1)}) custom-call(s32[2]{0:T(128)S(1)} %copy-done.19, bf16[5,3,256,320]{3,2,1,0:T(8,128)(2,1)S(1)} %shard_map.87.refs_1_, ...), custom_call_target="tpu_custom_call" | custom-call | tf_op jit(solution)/shard_map/pallas_call | solution.py:190
  37.0 2.4 %collective-permute-start.10 = (bf16[5,320,128]{2,1,0:T(8,128)(2,1)}, bf16[5,320,128]{2,1,0:T(8,128)(2,1)S(1)}, u32[]{:S(2)}, u32[]{:S(2)}) collective-permute-start(bf16[5,320,128]{2,1,0:T(8,128)(2,1)} %collective-permute-done.9.refs_2_.refs_5_), channel_id=1, source_target_pairs={{0,4},{4,0},{8,12},{12,8},{1,5},{5,1},{9,13},{13,9},{2,6},{6,2},{1... | collective-permute-start | bytes 1228808 | tf_op jit(solution)/shard_map/ppermute | solution.py:23
  39.5 1.3 collective-permute-start.6
  40.7 2.3 %collective-permute-start.7 = (bf16[3,64,256]{2,1,0:T(8,128)(2,1)S(1)}, bf16[3,64,256]{2,1,0:T(8,128)(2,1)S(1)}, u32[]{:S(2)}, u32[]{:S(2)}) collective-permute-start(bf16[3,64,256]{2,1,0:T(8,128)(2,1)S(1)} %get-tuple-element.53), channel_id=1, source_target_pairs={{0,2},{1,3},{2,0},{3,1},{4,6},{5,7},{6,4},{7,5},{8,10},{9,11},{10,... | collective-permute-start | bytes 294920 | tf_op jit(solution)/shard_map/ppermute | solution.py:18
  43.4 2.2 %shard_map.90 = (f32[3,64,256]{2,1,0:T(8,128)S(1)}, bf16[3,64,256]{2,1,0:T(8,128)(2,1)S(1)}, bf16[3,64,256]{2,1,0:T(8,128)(2,1)S(1)}, bf16[3,64,256]{2,1,0:T(8,128)(2,1)S(1)}) custom-call(s32[2]{0:T(128)S(1)} %copy-done.19, bf16[5,3,256,320]{3,2,1,0:T(8,128)(2,1)S(1)} %shard_map.87.refs_1_, bf16[5,320,128]{2,1,0:T(8,128)(2,1)} %collective-permute-done.9.refs_2_.refs_5_, ...), custom_call_target="tpu_custom_call" | custom-call | tf_op jit(solution)/shard_map/pallas_call | solution.py:190
  45.6 1.7 %collective-permute-start.14 = (bf16[3,64,256]{2,1,0:T(8,128)(2,1)S(1)}, bf16[3,64,256]{2,1,0:T(8,128)(2,1)S(1)}, u32[]{:S(2)}, u32[]{:S(2)}) collective-permute-start(bf16[3,64,256]{2,1,0:T(8,128)(2,1)S(1)} %get-tuple-element.57), channel_id=1, source_target_pairs={{0,1},{1,2},{2,3},{3,0},{4,5},{5,6},{6,7},{7,4},{8,9},{9,10},{10,1... | collective-permute-start | bytes 294920 | tf_op jit(solution)/shard_map/ppermute | solution.py:18
  48.0 2.6 %collective-permute-start.16 = (bf16[3,64,256]{2,1,0:T(8,128)(2,1)S(1)}, bf16[3,64,256]{2,1,0:T(8,128)(2,1)S(1)}, u32[]{:S(2)}, u32[]{:S(2)}) collective-permute-start(bf16[3,64,256]{2,1,0:T(8,128)(2,1)S(1)} %get-tuple-element.59), channel_id=1, source_target_pairs={{0,3},{1,0},{2,1},{3,2},{4,7},{5,4},{6,5},{7,6},{8,11},{9,8},{10,9... | collective-permute-start | bytes 294920 | tf_op jit(solution)/shard_map/ppermute | solution.py:18
  50.5 3.2 %collective-permute-done.7.refs_3_ = bf16[3,64,256]{2,1,0:T(8,128)(2,1)S(1)} collective-permute-done((bf16[3,64,256]{2,1,0:T(8,128)(2,1)S(1)}, bf16[3,64,256]{2,1,0:T(8,128)(2,1)S(1)}, u32[]{:S(2)}, u32[]{:S(2)}) %collective-permute-start.7) | collective-permute-done | bytes 98336 | tf_op jit(solution)/shard_map/ppermute | solution.py:18
  54.5 4.0 %collective-permute-start.11 = (bf16[3,64,256]{2,1,0:T(8,128)(2,1)S(1)}, bf16[3,64,256]{2,1,0:T(8,128)(2,1)S(1)}, u32[]{:S(2)}, u32[]{:S(2)}) collective-permute-start(bf16[3,64,256]{2,1,0:T(8,128)(2,1)S(1)} %shard_map.91.refs_7_.refs_2_), channel_id=1, source_target_pairs={{0,1},{1,2},{2,3},{3,0},{4,5},{5,6},{6,7},{7,4},{8,9},{9,10},{10,1... | collective-permute-start | bytes 294920 | tf_op jit(solution)/shard_map/ppermute | solution.py:18
  59.3 1.7 %collective-permute-start.13 = (bf16[3,64,256]{2,1,0:T(8,128)(2,1)S(1)}, bf16[3,64,256]{2,1,0:T(8,128)(2,1)S(1)}, u32[]{:S(2)}, u32[]{:S(2)}) collective-permute-start(bf16[3,64,256]{2,1,0:T(8,128)(2,1)S(1)} %shard_map.91.refs_7_.refs_2_), channel_id=1, source_target_pairs={{0,3},{1,0},{2,1},{3,2},{4,7},{5,4},{6,5},{7,6},{8,11},{9,8},{10,9... | collective-permute-start | bytes 294920 | tf_op jit(solution)/shard_map/ppermute | solution.py:18
  61.0 1.4 %shard_map.89 = (bf16[5,320,768]{2,1,0:T(8,128)(2,1)S(1)}, bf16[128,384]{1,0:T(8,128)(2,1)S(1)}, bf16[128,384]{1,0:T(8,128)(2,1)S(1)}, bf16[128,384]{1,0:T(8,128)(2,1)S(1)}, bf16[128,384]{1,0:T(8,128)(2,1)S(1)}) custom-call(s32[2]{0:T(128)S(1)} %copy-done.19, bf16[5,3,256,320]{3,2,1,0:T(8,128)(2,1)S(1)} %shard_map.87.refs_1_, ...), custom_call_target="tpu_custom_call" | custom-call | tf_op jit(solution)/shard_map/pallas_call | solution.py:190
  63.6 3.5 %collective-permute-done.12.refs_4_ = bf16[3,64,256]{2,1,0:T(8,128)(2,1)S(1)} collective-permute-done((bf16[3,64,256]{2,1,0:T(8,128)(2,1)S(1)}, bf16[3,64,256]{2,1,0:T(8,128)(2,1)S(1)}, u32[]{:S(2)}, u32[]{:S(2)}) %collective-permute-start.12) | collective-permute-done | bytes 98336 | tf_op jit(solution)/shard_map/ppermute | solution.py:18
  67.2 1.4 %shard_map.93 = (bf16[3,256,256]{2,1,0:T(8,128)(2,1)S(1)}, bf16[3,1,256]{2,1,0:T(2,128)(2,1)S(1)}, bf16[3,1,256]{2,1,0:T(2,128)(2,1)S(1)}, f32[5,320,128]{2,1,0:T(8,128)S(1)}, bf16[5,320,128]{2,1,0:T(8,128)(2,1)S(1)}) custom-call(s32[2]{0:T(128)S(1)} %copy-done.19, bf16[5,320,768]{2,1,0:T(8,128)(2,1)S(1)} %get-tuple-element.51.refs_1_, ...), custom_call_target="tpu_custom_call" | custom-call | tf_op jit(solution)/shard_map/pallas_call | solution.py:190
  68.7 2.6 %collective-permute-start.17 = (bf16[3,64,256]{2,1,0:T(8,128)(2,1)S(1)}, bf16[3,64,256]{2,1,0:T(8,128)(2,1)S(1)}, u32[]{:S(2)}, u32[]{:S(2)}) collective-permute-start(bf16[3,64,256]{2,1,0:T(8,128)(2,1)S(1)} %shard_map.92.refs_6_.refs_2_), channel_id=1, source_target_pairs={{0,1},{1,2},{2,3},{3,0},{4,5},{5,6},{6,7},{7,4},{8,9},{9,10},{10,1... | collective-permute-start | bytes 294920 | tf_op jit(solution)/shard_map/ppermute | solution.py:18
  72.0 1.7 %collective-permute-start.19 = (bf16[3,64,256]{2,1,0:T(8,128)(2,1)S(1)}, bf16[3,64,256]{2,1,0:T(8,128)(2,1)S(1)}, u32[]{:S(2)}, u32[]{:S(2)}) collective-permute-start(bf16[3,64,256]{2,1,0:T(8,128)(2,1)S(1)} %shard_map.92.refs_6_.refs_2_), channel_id=1, source_target_pairs={{0,3},{1,0},{2,1},{3,2},{4,7},{5,4},{6,5},{7,6},{8,11},{9,8},{10,9... | collective-permute-start | bytes 294920 | tf_op jit(solution)/shard_map/ppermute | solution.py:18
  76.3 3.7 %collective-permute-done.18.refs_4_ = bf16[3,64,256]{2,1,0:T(8,128)(2,1)S(1)} collective-permute-done((bf16[3,64,256]{2,1,0:T(8,128)(2,1)S(1)}, bf16[3,64,256]{2,1,0:T(8,128)(2,1)S(1)}, u32[]{:S(2)}, u32[]{:S(2)}) %collective-permute-start.18) | collective-permute-done | bytes 98336 | tf_op jit(solution)/shard_map/ppermute | solution.py:18
  79.9 1.4 %shard_map.95 = (bf16[3,256,256]{2,1,0:T(8,128)(2,1)S(1)}, bf16[3,1,256]{2,1,0:T(2,128)(2,1)S(1)}, bf16[3,1,256]{2,1,0:T(2,128)(2,1)S(1)}, f32[5,320,128]{2,1,0:T(8,128)S(1)}, bf16[5,320,128]{2,1,0:T(8,128)(2,1)S(1)}) custom-call(s32[2]{0:T(128)S(1)} %copy-done.19, bf16[5,320,768]{2,1,0:T(8,128)(2,1)S(1)} %get-tuple-element.51.refs_1_, ...), custom_call_target="tpu_custom_call" | custom-call | tf_op jit(solution)/shard_map/pallas_call | solution.py:190
  81.4 1.3 collective-permute-start.26
  84.0 1.2 collective-permute-start.24
  85.2 1.8 %collective-permute-start.22 = (bf16[3,1,512]{2,1,0:T(2,128)(2,1)S(1)}, bf16[3,1,512]{2,1,0:T(2,128)(2,1)S(1)}, u32[]{:S(2)}, u32[]{:S(2)}) collective-permute-start(bf16[3,1,512]{2,1,0:T(2,128)(2,1)S(1)} %pad_maximum_fusion.1), channel_id=1, source_target_pairs={{0,4},{4,8},{8,12},{1,5},{5,9},{9,13},{2,6},{6,10},{10,14},{3,7},{... | collective-permute-start | bytes 9224 | tf_op jit(solution)/shard_map/ppermute | solution.py:29
  87.0 1.5 %collective-permute-start.21 = (bf16[3,1,512]{2,1,0:T(2,128)(2,1)S(1)}, bf16[3,1,512]{2,1,0:T(2,128)(2,1)S(1)}, u32[]{:S(2)}, u32[]{:S(2)}) collective-permute-start(bf16[3,1,512]{2,1,0:T(2,128)(2,1)S(1)} %pad_maximum_fusion), channel_id=1, source_target_pairs={{4,0},{8,4},{12,8},{5,1},{9,5},{13,9},{6,2},{10,6},{14,10},{7,3},{... | collective-permute-start | bytes 9224 | tf_op jit(solution)/shard_map/ppermute | solution.py:29
  88.5 2.1 %collective-permute-done.21.refs_7_ = bf16[3,1,512]{2,1,0:T(2,128)(2,1)S(1)} collective-permute-done((bf16[3,1,512]{2,1,0:T(2,128)(2,1)S(1)}, bf16[3,1,512]{2,1,0:T(2,128)(2,1)S(1)}, u32[]{:S(2)}, u32[]{:S(2)}) %collective-permute-start.21) | collective-permute-done | bytes 3104 | tf_op jit(solution)/shard_map/ppermute | solution.py:29
  90.7 5.9 %shard_map.96 = bf16[3,320,512]{2,1,0:T(8,128)(2,1)} custom-call(s32[2]{0:T(128)S(1)} %copy-done.19, bf16[3,256,256]{2,1,0:T(8,128)(2,1)S(1)} %get-tuple-element.60.refs_1_, bf16[3,256,256]{2,1,0:T(8,128)(2,1)S(1)} %get-tuple-element.63.refs_2_, bf16[5,320,128]{2,1,0:T(8,128)(2,1)S(1)} %get-tuple-element.45.refs_0_.refs_2_.refs_3_, ...), custom_call_target="tpu_custom_call" | custom-call | tf_op jit(solution)/shard_map/pallas_call | solution.py:190
  96.6 1.7 %copy.12 = bf16[3,320,512]{1,2,0:T(8,128)(2,1)S(1)} copy(bf16[3,320,512]{2,1,0:T(8,128)(2,1)} %shard_map.96) | data formatting | bytes 1966080 | tf_op jit(solution)/shard_map/pallas_call | solution.py:190
  98.3 2.4 %copy-done.1 = bf16[5,320,1536]{2,1,0:T(8,128)(2,1)S(1)} copy-done((bf16[5,320,1536]{2,1,0:T(8,128)(2,1)S(1)}, bf16[5,320,1536]{2,1,0:T(8,128)(2,1)}, u32[]{:S(2)}) %copy-start.1) | copy-done | bytes 4915224
  100.7 2.4 %shard_map.97 = (bf16[5,320,128]{2,1,0:T(8,128)(2,1)S(1)}, f32[128,384]{1,0:T(8,128)S(1)}, bf16[128,384]{1,0:T(8,128)(2,1)S(1)}, bf16[128,384]{1,0:T(8,128)(2,1)S(1)}, bf16[128,384]{1,0:T(8,128)(2,1)S(1)}) custom-call(s32[2]{0:T(128)S(1)} %copy-done.19, f32[5,320,128]{2,1,0:T(8,128)S(1)} %get-tuple-element.85.refs_1_, ...), custom_call_target="tpu_custom_call" | custom-call | tf_op jit(solution)/shard_map/pallas_call | solution.py:190
  103.1 11.9 %collective-permute-start.27 = (bf16[5,320,128]{2,1,0:T(8,128)(2,1)S(1)}, bf16[5,320,128]{2,1,0:T(8,128)(2,1)S(1)}, u32[]{:S(2)}, u32[]{:S(2)}) collective-permute-start(bf16[5,320,128]{2,1,0:T(8,128)(2,1)S(1)} %get-tuple-element.70.refs_2_), channel_id=1, source_target_pairs={{0,4},{4,0},{8,12},{12,8},{1,5},{5,1},{9,13},{13,9},{2,6},{6,2},{1... | collective-permute-start | bytes 1228808 | tf_op jit(solution)/shard_map/ppermute | solution.py:23
  115.0 1.2 add_convert_fusion.refs_0_
  118.2 2.6 %collective-permute-start.31 = (bf16[128,384]{1,0:T(8,128)(2,1)S(1)}, bf16[128,384]{1,0:T(8,128)(2,1)S(1)}, u32[]{:S(2)}, u32[]{:S(2)}) collective-permute-start(bf16[128,384]{1,0:T(8,128)(2,1)S(1)} %get-tuple-element.76), channel_id=1, source_target_pairs={{0,1},{1,2},{2,3},{3,0},{4,5},{5,6},{6,7},{7,4},{8,9},{9,10},{10,1... | collective-permute-start | bytes 294920 | tf_op jit(solution)/shard_map/ppermute | solution.py:18
  120.7 1.7 %collective-permute-done.29.refs_6_ = bf16[128,384]{1,0:T(8,128)(2,1)S(1)} collective-permute-done((bf16[128,384]{1,0:T(8,128)(2,1)S(1)}, bf16[128,384]{1,0:T(8,128)(2,1)S(1)}, u32[]{:S(2)}, u32[]{:S(2)}) %collective-permute-start.29) | collective-permute-done | bytes 98336 | tf_op jit(solution)/shard_map/ppermute | solution.py:23
  122.4 1.6 %collective-permute-start.32 = (bf16[128,384]{1,0:T(8,128)(2,1)S(1)}, bf16[128,384]{1,0:T(8,128)(2,1)S(1)}, u32[]{:S(2)}, u32[]{:S(2)}) collective-permute-start(bf16[128,384]{1,0:T(8,128)(2,1)S(1)} %get-tuple-element.77), channel_id=1, source_target_pairs={{0,2},{1,3},{2,0},{3,1},{4,6},{5,7},{6,4},{7,5},{8,10},{9,11},{10,... | collective-permute-start | bytes 294920 | tf_op jit(solution)/shard_map/ppermute | solution.py:18
  124.0 3.3 %collective-permute-start.33 = (bf16[128,384]{1,0:T(8,128)(2,1)S(1)}, bf16[128,384]{1,0:T(8,128)(2,1)S(1)}, u32[]{:S(2)}, u32[]{:S(2)}) collective-permute-start(bf16[128,384]{1,0:T(8,128)(2,1)S(1)} %get-tuple-element.78), channel_id=1, source_target_pairs={{0,3},{1,0},{2,1},{3,2},{4,7},{5,4},{6,5},{7,6},{8,11},{9,8},{10,9... | collective-permute-start | bytes 294920 | tf_op jit(solution)/shard_map/ppermute | solution.py:18
  127.3 1.4 %collective-permute-done.32.refs_10_ = bf16[128,384]{1,0:T(8,128)(2,1)S(1)} collective-permute-done((bf16[128,384]{1,0:T(8,128)(2,1)S(1)}, bf16[128,384]{1,0:T(8,128)(2,1)S(1)}, u32[]{:S(2)}, u32[]{:S(2)}) %collective-permute-start.32) | collective-permute-done | bytes 98336 | tf_op jit(solution)/shard_map/ppermute | solution.py:18
  128.7 1.7 %collective-permute-done.33.refs_11_ = bf16[128,384]{1,0:T(8,128)(2,1)S(1)} collective-permute-done((bf16[128,384]{1,0:T(8,128)(2,1)S(1)}, bf16[128,384]{1,0:T(8,128)(2,1)S(1)}, u32[]{:S(2)}, u32[]{:S(2)}) %collective-permute-start.33) | collective-permute-done | bytes 98336 | tf_op jit(solution)/shard_map/ppermute | solution.py:18
  130.4 2.5 %shard_map.98 = (f32[5,320,384]{2,1,0:T(8,128)}, f32[128,384]{1,0:T(8,128)}) custom-call(bf16[5,320,128]{2,1,0:T(8,128)(2,1)S(1)} %add_convert_fusion.refs_0_, bf16[5,320,128]{2,1,0:T(8,128)(2,1)S(1)} %collective-permute-done.25.refs_1_, bf16[5,320,128]{2,1,0:T(8,128)(2,1)S(1)} %get-tuple-element.70.refs_2_, ...), custom_call_target="tpu_custom_call" | custom-call | tf_op jit(solution)/shard_map/pallas_call | solution.py:554
  (107 shorter events, 18.2 us)
Async XLA Ops:
  5.7 10.8 %collective-permute-start.2 = (bf16[128,384]{1,0:T(8,128)(2,1)S(1)}, bf16[128,384]{1,0:T(8,128)(2,1)S(1)}, u32[]{:S(2)}, u32[]{:S(2)}) collective-permute-start(bf16[128,384]{1,0:T(8,128)(2,1)S(1)} %gather_fusion), channel_id=1, source_target_pairs={{0,1},{1,2},{2,3},{3,0},{4,5},{5,6},{6,7},{7,4},{8,9},{9,10},{10,1... | collective-permute-start | bytes 294920 | tf_op jit(solution)/shard_map/ppermute | solution.py:18
  8.8 9.2 %collective-permute-start.3 = (bf16[128,384]{1,0:T(8,128)(2,1)S(1)}, bf16[128,384]{1,0:T(8,128)(2,1)S(1)}, u32[]{:S(2)}, u32[]{:S(2)}) collective-permute-start(bf16[128,384]{1,0:T(8,128)(2,1)S(1)} %gather_fusion), channel_id=1, source_target_pairs={{0,2},{1,3},{2,0},{3,1},{4,6},{5,7},{6,4},{7,5},{8,10},{9,11},{10,... | collective-permute-start | bytes 294920 | tf_op jit(solution)/shard_map/ppermute | solution.py:18
  11.4 7.9 %collective-permute-start.4 = (bf16[128,384]{1,0:T(8,128)(2,1)S(1)}, bf16[128,384]{1,0:T(8,128)(2,1)S(1)}, u32[]{:S(2)}, u32[]{:S(2)}) collective-permute-start(bf16[128,384]{1,0:T(8,128)(2,1)S(1)} %gather_fusion), channel_id=1, source_target_pairs={{0,3},{1,0},{2,1},{3,2},{4,7},{5,4},{6,5},{7,6},{8,11},{9,8},{10,9... | collective-permute-start | bytes 294920 | tf_op jit(solution)/shard_map/ppermute | solution.py:18
  24.3 10.0 %collective-permute-start.5 = (bf16[5,320,128]{2,1,0:T(8,128)(2,1)S(1)}, bf16[5,320,128]{2,1,0:T(8,128)(2,1)}, u32[]{:S(2)}, u32[]{:S(2)}) collective-permute-start(bf16[5,320,128]{2,1,0:T(8,128)(2,1)S(1)} %get-tuple-element.45.refs_0_.refs_2_.refs_3_), channel_id=1, source_target_pairs={{0,4},{4,0},{8,12},{12,8},{1,5},{5,1},{9,13},{13,9},{2,6},{6,2},{1... | collective-permute-start | bytes 1228808 | tf_op jit(solution)/shard_map/ppermute | solution.py:23
  24.3 12.7 %collective-permute-start.9 = (bf16[5,320,128]{2,1,0:T(8,128)(2,1)S(1)}, bf16[5,320,128]{2,1,0:T(8,128)(2,1)}, u32[]{:S(2)}, u32[]{:S(2)}) collective-permute-start(bf16[5,320,128]{2,1,0:T(8,128)(2,1)S(1)} %get-tuple-element.45.refs_0_.refs_2_.refs_3_), channel_id=1, source_target_pairs={{0,8},{4,12},{8,0},{12,4},{1,9},{5,13},{9,1},{13,5},{2,10},{6,14},... | collective-permute-start | bytes 1228808 | tf_op jit(solution)/shard_map/ppermute | solution.py:23
  27.9 4.5 %collective-permute-start = (bf16[3,2,320]{2,1,0:T(2,128)(2,1)S(1)}, bf16[3,2,320]{2,1,0:T(2,128)(2,1)S(1)}, u32[]{:S(2)}, u32[]{:S(2)}) collective-permute-start(bf16[3,2,320]{2,1,0:T(2,128)(2,1)S(1)} %copy.16.last_ref), channel_id=1, source_target_pairs={{0,4},{4,8},{8,12},{1,5},{5,9},{9,13},{2,6},{6,10},{10,14},{3,7},{... | collective-permute-start | bytes 11528 | tf_op jit(solution)/shard_map/ppermute | solution.py:29
  31.1 3.1 %collective-permute-start.1 = (bf16[3,2,320]{2,1,0:T(2,128)(2,1)S(1)}, bf16[3,2,320]{2,1,0:T(2,128)(2,1)S(1)}, u32[]{:S(2)}, u32[]{:S(2)}) collective-permute-start(bf16[3,2,320]{2,1,0:T(2,128)(2,1)S(1)} %copy.15.first_ref), channel_id=1, source_target_pairs={{4,0},{8,4},{12,8},{5,1},{9,5},{13,9},{6,2},{10,6},{14,10},{7,3},{... | collective-permute-start | bytes 11528 | tf_op jit(solution)/shard_map/ppermute | solution.py:29
  34.2 13.1 %copy-start.28 = (s32[3,64]{1,0:T(4,128)S(1)}, s32[3,64]{1,0:T(4,128)}, u32[]{:S(2)}) copy-start(s32[3,64]{1,0:T(4,128)} %param.10) | copy-start | bytes 2308
  37.0 16.9 %copy-start.5 = (s32[3,64,512]{2,1,0:T(8,128)S(1)}, s32[3,64,512]{2,1,0:T(8,128)}, u32[]{:S(2)}) copy-start(s32[3,64,512]{2,1,0:T(8,128)} %refs_5_.3) | copy-start | bytes 1179652
  37.0 24.0 %copy-start.11 = (bf16[128,384]{1,0:T(8,128)(2,1)S(1)}, bf16[128,384]{1,0:T(8,128)(2,1)}, u32[]{:S(2)}) copy-start(bf16[128,384]{1,0:T(8,128)(2,1)} %copy-done.10) | copy-start | bytes 294916
  37.0 24.0 %copy-start.13 = (bf16[128,384]{1,0:T(8,128)(2,1)S(1)}, bf16[128,384]{1,0:T(8,128)(2,1)}, u32[]{:S(2)}) copy-start(bf16[128,384]{1,0:T(8,128)(2,1)} %copy-done.12) | copy-start | bytes 294916
  37.0 24.0 %copy-start.15 = (bf16[128,384]{1,0:T(8,128)(2,1)S(1)}, bf16[128,384]{1,0:T(8,128)(2,1)}, u32[]{:S(2)}) copy-start(bf16[128,384]{1,0:T(8,128)(2,1)} %copy-done.14) | copy-start | bytes 294916
  37.0 23.9 %copy-start.17 = (bf16[128,384]{1,0:T(8,128)(2,1)S(1)}, bf16[128,384]{1,0:T(8,128)(2,1)}, u32[]{:S(2)}) copy-start(bf16[128,384]{1,0:T(8,128)(2,1)} %copy-done.16) | copy-start | bytes 294916
  37.0 6.3 %collective-permute-start.10 = (bf16[5,320,128]{2,1,0:T(8,128)(2,1)}, bf16[5,320,128]{2,1,0:T(8,128)(2,1)S(1)}, u32[]{:S(2)}, u32[]{:S(2)}) collective-permute-start(bf16[5,320,128]{2,1,0:T(8,128)(2,1)} %collective-permute-done.9.refs_2_.refs_5_), channel_id=1, source_target_pairs={{0,4},{4,0},{8,12},{12,8},{1,5},{5,1},{9,13},{13,9},{2,6},{6,2},{1... | collective-permute-start | bytes 1228808 | tf_op jit(solution)/shard_map/ppermute | solution.py:23
  39.5 8.5 %collective-permute-start.6 = (bf16[3,64,256]{2,1,0:T(8,128)(2,1)S(1)}, bf16[3,64,256]{2,1,0:T(8,128)(2,1)S(1)}, u32[]{:S(2)}, u32[]{:S(2)}) collective-permute-start(bf16[3,64,256]{2,1,0:T(8,128)(2,1)S(1)} %get-tuple-element.52), channel_id=1, source_target_pairs={{0,1},{1,2},{2,3},{3,0},{4,5},{5,6},{6,7},{7,4},{8,9},{9,10},{10,1... | collective-permute-start | bytes 294920 | tf_op jit(solution)/shard_map/ppermute | solution.py:18
  40.7 13.1 %collective-permute-start.7 = (bf16[3,64,256]{2,1,0:T(8,128)(2,1)S(1)}, bf16[3,64,256]{2,1,0:T(8,128)(2,1)S(1)}, u32[]{:S(2)}, u32[]{:S(2)}) collective-permute-start(bf16[3,64,256]{2,1,0:T(8,128)(2,1)S(1)} %get-tuple-element.53), channel_id=1, source_target_pairs={{0,2},{1,3},{2,0},{3,1},{4,6},{5,7},{6,4},{7,5},{8,10},{9,11},{10,... | collective-permute-start | bytes 294920 | tf_op jit(solution)/shard_map/ppermute | solution.py:18
  43.0 10.8 %collective-permute-start.8 = (bf16[3,64,256]{2,1,0:T(8,128)(2,1)S(1)}, bf16[3,64,256]{2,1,0:T(8,128)(2,1)S(1)}, u32[]{:S(2)}, u32[]{:S(2)}) collective-permute-start(bf16[3,64,256]{2,1,0:T(8,128)(2,1)S(1)} %get-tuple-element.54), channel_id=1, source_target_pairs={{0,3},{1,0},{2,1},{3,2},{4,7},{5,4},{6,5},{7,6},{8,11},{9,8},{10,9... | collective-permute-start | bytes 294920 | tf_op jit(solution)/shard_map/ppermute | solution.py:18
  45.6 13.7 %collective-permute-start.14 = (bf16[3,64,256]{2,1,0:T(8,128)(2,1)S(1)}, bf16[3,64,256]{2,1,0:T(8,128)(2,1)S(1)}, u32[]{:S(2)}, u32[]{:S(2)}) collective-permute-start(bf16[3,64,256]{2,1,0:T(8,128)(2,1)S(1)} %get-tuple-element.57), channel_id=1, source_target_pairs={{0,1},{1,2},{2,3},{3,0},{4,5},{5,6},{6,7},{7,4},{8,9},{9,10},{10,1... | collective-permute-start | bytes 294920 | tf_op jit(solution)/shard_map/ppermute | solution.py:18
  47.3 15.7 %collective-permute-start.15 = (bf16[3,64,256]{2,1,0:T(8,128)(2,1)S(1)}, bf16[3,64,256]{2,1,0:T(8,128)(2,1)S(1)}, u32[]{:S(2)}, u32[]{:S(2)}) collective-permute-start(bf16[3,64,256]{2,1,0:T(8,128)(2,1)S(1)} %get-tuple-element.58), channel_id=1, source_target_pairs={{0,2},{1,3},{2,0},{3,1},{4,6},{5,7},{6,4},{7,5},{8,10},{9,11},{10,... | collective-permute-start | bytes 294920 | tf_op jit(solution)/shard_map/ppermute | solution.py:18
  48.0 15.0 %collective-permute-start.16 = (bf16[3,64,256]{2,1,0:T(8,128)(2,1)S(1)}, bf16[3,64,256]{2,1,0:T(8,128)(2,1)S(1)}, u32[]{:S(2)}, u32[]{:S(2)}) collective-permute-start(bf16[3,64,256]{2,1,0:T(8,128)(2,1)S(1)} %get-tuple-element.59), channel_id=1, source_target_pairs={{0,3},{1,0},{2,1},{3,2},{4,7},{5,4},{6,5},{7,6},{8,11},{9,8},{10,9... | collective-permute-start | bytes 294920 | tf_op jit(solution)/shard_map/ppermute | solution.py:18
  54.5 9.1 %collective-permute-start.11 = (bf16[3,64,256]{2,1,0:T(8,128)(2,1)S(1)}, bf16[3,64,256]{2,1,0:T(8,128)(2,1)S(1)}, u32[]{:S(2)}, u32[]{:S(2)}) collective-permute-start(bf16[3,64,256]{2,1,0:T(8,128)(2,1)S(1)} %shard_map.91.refs_7_.refs_2_), channel_id=1, source_target_pairs={{0,1},{1,2},{2,3},{3,0},{4,5},{5,6},{6,7},{7,4},{8,9},{9,10},{10,1... | collective-permute-start | bytes 294920 | tf_op jit(solution)/shard_map/ppermute | solution.py:18
  58.5 8.7 %collective-permute-start.12 = (bf16[3,64,256]{2,1,0:T(8,128)(2,1)S(1)}, bf16[3,64,256]{2,1,0:T(8,128)(2,1)S(1)}, u32[]{:S(2)}, u32[]{:S(2)}) collective-permute-start(bf16[3,64,256]{2,1,0:T(8,128)(2,1)S(1)} %shard_map.91.refs_7_.refs_2_), channel_id=1, source_target_pairs={{0,2},{1,3},{2,0},{3,1},{4,6},{5,7},{6,4},{7,5},{8,10},{9,11},{10,... | collective-permute-start | bytes 294920 | tf_op jit(solution)/shard_map/ppermute | solution.py:18
  59.3 7.9 %collective-permute-start.13 = (bf16[3,64,256]{2,1,0:T(8,128)(2,1)S(1)}, bf16[3,64,256]{2,1,0:T(8,128)(2,1)S(1)}, u32[]{:S(2)}, u32[]{:S(2)}) collective-permute-start(bf16[3,64,256]{2,1,0:T(8,128)(2,1)S(1)} %shard_map.91.refs_7_.refs_2_), channel_id=1, source_target_pairs={{0,3},{1,0},{2,1},{3,2},{4,7},{5,4},{6,5},{7,6},{8,11},{9,8},{10,9... | collective-permute-start | bytes 294920 | tf_op jit(solution)/shard_map/ppermute | solution.py:18
  63.0 12.2 %copy-start.20 = (bf16[128,384]{1,0:T(8,128)(2,1)}, bf16[128,384]{1,0:T(8,128)(2,1)S(1)}, u32[]{:S(2)}) copy-start(bf16[128,384]{1,0:T(8,128)(2,1)S(1)} %get-tuple-element.74) | copy-start | bytes 294916
  63.0 12.2 %copy-start.22 = (bf16[128,384]{1,0:T(8,128)(2,1)}, bf16[128,384]{1,0:T(8,128)(2,1)S(1)}, u32[]{:S(2)}) copy-start(bf16[128,384]{1,0:T(8,128)(2,1)S(1)} %get-tuple-element.73) | copy-start | bytes 294916
  68.6 5.1 %collective-permute-start.20 = (bf16[5,320,128]{2,1,0:T(8,128)(2,1)S(1)}, bf16[5,320,128]{2,1,0:T(8,128)(2,1)S(1)}, u32[]{:S(2)}, u32[]{:S(2)}) collective-permute-start(bf16[5,320,128]{2,1,0:T(8,128)(2,1)S(1)} %get-tuple-element.62), channel_id=1, source_target_pairs={{0,4},{4,0},{8,12},{12,8},{1,5},{5,1},{9,13},{13,9},{2,6},{6,2},{1... | collective-permute-start | bytes 1228808 | tf_op jit(solution)/shard_map/ppermute | solution.py:23
  68.7 7.6 %collective-permute-start.17 = (bf16[3,64,256]{2,1,0:T(8,128)(2,1)S(1)}, bf16[3,64,256]{2,1,0:T(8,128)(2,1)S(1)}, u32[]{:S(2)}, u32[]{:S(2)}) collective-permute-start(bf16[3,64,256]{2,1,0:T(8,128)(2,1)S(1)} %shard_map.92.refs_6_.refs_2_), channel_id=1, source_target_pairs={{0,1},{1,2},{2,3},{3,0},{4,5},{5,6},{6,7},{7,4},{8,9},{9,10},{10,1... | collective-permute-start | bytes 294920 | tf_op jit(solution)/shard_map/ppermute | solution.py:18
  71.3 8.7 %collective-permute-start.18 = (bf16[3,64,256]{2,1,0:T(8,128)(2,1)S(1)}, bf16[3,64,256]{2,1,0:T(8,128)(2,1)S(1)}, u32[]{:S(2)}, u32[]{:S(2)}) collective-permute-start(bf16[3,64,256]{2,1,0:T(8,128)(2,1)S(1)} %shard_map.92.refs_6_.refs_2_), channel_id=1, source_target_pairs={{0,2},{1,3},{2,0},{3,1},{4,6},{5,7},{6,4},{7,5},{8,10},{9,11},{10,... | collective-permute-start | bytes 294920 | tf_op jit(solution)/shard_map/ppermute | solution.py:18
  72.0 7.9 %collective-permute-start.19 = (bf16[3,64,256]{2,1,0:T(8,128)(2,1)S(1)}, bf16[3,64,256]{2,1,0:T(8,128)(2,1)S(1)}, u32[]{:S(2)}, u32[]{:S(2)}) collective-permute-start(bf16[3,64,256]{2,1,0:T(8,128)(2,1)S(1)} %shard_map.92.refs_6_.refs_2_), channel_id=1, source_target_pairs={{0,3},{1,0},{2,1},{3,2},{4,7},{5,4},{6,5},{7,6},{8,11},{9,8},{10,9... | collective-permute-start | bytes 294920 | tf_op jit(solution)/shard_map/ppermute | solution.py:18
  73.7 9.4 %copy-start.26 = (bf16[5,320,128]{2,1,0:T(8,128)(2,1)}, bf16[5,320,128]{2,1,0:T(8,128)(2,1)S(1)}, u32[]{:S(2)}) copy-start(bf16[5,320,128]{2,1,0:T(8,128)(2,1)S(1)} %collective-permute-done.20) | copy-start | bytes 1228804
  74.6 16.0 %copy-start.3 = (f32[3,512,320]{2,1,0:T(8,128)S(1)}, f32[3,512,320]{2,1,0:T(8,128)}, u32[]{:S(2)}) copy-start(f32[3,512,320]{2,1,0:T(8,128)} %copy-done.2) | copy-start | bytes 5898244
  81.3 1.8 %collective-permute-start.23 = (bf16[5,320,128]{2,1,0:T(8,128)(2,1)S(1)}, bf16[5,320,128]{2,1,0:T(8,128)(2,1)S(1)}, u32[]{:S(2)}, u32[]{:S(2)}) collective-permute-start(bf16[5,320,128]{2,1,0:T(8,128)(2,1)S(1)} %get-tuple-element.69), channel_id=1, source_target_pairs={{0,4},{4,0},{8,12},{12,8},{1,5},{5,1},{9,13},{13,9},{2,6},{6,2},{1... | collective-permute-start | bytes 1228808 | tf_op jit(solution)/shard_map/ppermute | solution.py:23
  81.4 16.9 %collective-permute-start.26 = (bf16[5,320,128]{2,1,0:T(8,128)(2,1)}, bf16[5,320,128]{2,1,0:T(8,128)(2,1)}, u32[]{:S(2)}, u32[]{:S(2)}) collective-permute-start(bf16[5,320,128]{2,1,0:T(8,128)(2,1)} %fusion.refs_1_), channel_id=1, source_target_pairs={{0,8},{4,12},{8,0},{12,4},{1,9},{5,13},{9,1},{13,5},{2,10},{6,14},... | collective-permute-start | bytes 1228808 | tf_op jit(solution)/shard_map/ppermute | solution.py:23
  84.0 31.0 %collective-permute-start.24 = (bf16[5,320,128]{2,1,0:T(8,128)(2,1)}, bf16[5,320,128]{2,1,0:T(8,128)(2,1)}, u32[]{:S(2)}, u32[]{:S(2)}) collective-permute-start(bf16[5,320,128]{2,1,0:T(8,128)(2,1)} %get-tuple-element.84.refs_10_), channel_id=1, source_target_pairs={{0,8},{4,12},{8,0},{12,4},{1,9},{5,13},{9,1},{13,5},{2,10},{6,14},... | collective-permute-start | bytes 1228808 | tf_op jit(solution)/shard_map/ppermute | solution.py:23
  85.2 3.3 %collective-permute-start.22 = (bf16[3,1,512]{2,1,0:T(2,128)(2,1)S(1)}, bf16[3,1,512]{2,1,0:T(2,128)(2,1)S(1)}, u32[]{:S(2)}, u32[]{:S(2)}) collective-permute-start(bf16[3,1,512]{2,1,0:T(2,128)(2,1)S(1)} %pad_maximum_fusion.1), channel_id=1, source_target_pairs={{0,4},{4,8},{8,12},{1,5},{5,9},{9,13},{2,6},{6,10},{10,14},{3,7},{... | collective-permute-start | bytes 9224 | tf_op jit(solution)/shard_map/ppermute | solution.py:29
  87.0 3.6 %collective-permute-start.21 = (bf16[3,1,512]{2,1,0:T(2,128)(2,1)S(1)}, bf16[3,1,512]{2,1,0:T(2,128)(2,1)S(1)}, u32[]{:S(2)}, u32[]{:S(2)}) collective-permute-start(bf16[3,1,512]{2,1,0:T(2,128)(2,1)S(1)} %pad_maximum_fusion), channel_id=1, source_target_pairs={{4,0},{8,4},{12,8},{5,1},{9,5},{13,9},{6,2},{10,6},{14,10},{7,3},{... | collective-permute-start | bytes 9224 | tf_op jit(solution)/shard_map/ppermute | solution.py:29
  100.7 14.3 %copy-start.27 = (bf16[5,320,128]{2,1,0:T(8,128)(2,1)S(1)}, bf16[5,320,128]{2,1,0:T(8,128)(2,1)}, u32[]{:S(2)}) copy-start(bf16[5,320,128]{2,1,0:T(8,128)(2,1)} %copy-done.26) | copy-start | bytes 1228804
  100.7 15.5 %copy-start.25 = (bf16[128,384]{1,0:T(8,128)(2,1)S(1)}, bf16[128,384]{1,0:T(8,128)(2,1)}, u32[]{:S(2)}) copy-start(bf16[128,384]{1,0:T(8,128)(2,1)} %copy-done.24) | copy-start | bytes 294916
  100.7 16.0 %copy-start.23 = (bf16[128,384]{1,0:T(8,128)(2,1)S(1)}, bf16[128,384]{1,0:T(8,128)(2,1)}, u32[]{:S(2)}) copy-start(bf16[128,384]{1,0:T(8,128)(2,1)} %copy-done.22) | copy-start | bytes 294916
  100.7 16.7 %copy-start.21 = (bf16[128,384]{1,0:T(8,128)(2,1)S(1)}, bf16[128,384]{1,0:T(8,128)(2,1)}, u32[]{:S(2)}) copy-start(bf16[128,384]{1,0:T(8,128)(2,1)} %copy-done.20) | copy-start | bytes 294916
  103.1 27.3 %collective-permute-start.27 = (bf16[5,320,128]{2,1,0:T(8,128)(2,1)S(1)}, bf16[5,320,128]{2,1,0:T(8,128)(2,1)S(1)}, u32[]{:S(2)}, u32[]{:S(2)}) collective-permute-start(bf16[5,320,128]{2,1,0:T(8,128)(2,1)S(1)} %get-tuple-element.70.refs_2_), channel_id=1, source_target_pairs={{0,4},{4,0},{8,12},{12,8},{1,5},{5,1},{9,13},{13,9},{2,6},{6,2},{1... | collective-permute-start | bytes 1228808 | tf_op jit(solution)/shard_map/ppermute | solution.py:23
  116.1 14.3 %collective-permute-start.25 = (bf16[5,320,128]{2,1,0:T(8,128)(2,1)S(1)}, bf16[5,320,128]{2,1,0:T(8,128)(2,1)S(1)}, u32[]{:S(2)}, u32[]{:S(2)}) collective-permute-start(bf16[5,320,128]{2,1,0:T(8,128)(2,1)S(1)} %add_convert_fusion.refs_0_), channel_id=1, source_target_pairs={{0,4},{4,0},{8,12},{12,8},{1,5},{5,1},{9,13},{13,9},{2,6},{6,2},{1... | collective-permute-start | bytes 1228808 | tf_op jit(solution)/shard_map/ppermute | solution.py:23
  116.2 1.9 %collective-permute-start.28 = (bf16[128,384]{1,0:T(8,128)(2,1)S(1)}, bf16[128,384]{1,0:T(8,128)(2,1)S(1)}, u32[]{:S(2)}, u32[]{:S(2)}) collective-permute-start(bf16[128,384]{1,0:T(8,128)(2,1)S(1)} %copy-done.25), channel_id=1, source_target_pairs={{0,4},{4,0},{8,12},{12,8},{1,5},{5,1},{9,13},{13,9},{2,6},{6,2},{1... | collective-permute-start | bytes 294920 | tf_op jit(solution)/shard_map/ppermute | solution.py:23
  116.7 5.7 %collective-permute-start.29 = (bf16[128,384]{1,0:T(8,128)(2,1)S(1)}, bf16[128,384]{1,0:T(8,128)(2,1)S(1)}, u32[]{:S(2)}, u32[]{:S(2)}) collective-permute-start(bf16[128,384]{1,0:T(8,128)(2,1)S(1)} %copy-done.23), channel_id=1, source_target_pairs={{0,8},{4,12},{8,0},{12,4},{1,9},{5,13},{9,1},{13,5},{2,10},{6,14},... | collective-permute-start | bytes 294920 | tf_op jit(solution)/shard_map/ppermute | solution.py:23
  117.4 6.6 %collective-permute-start.30 = (bf16[128,384]{1,0:T(8,128)(2,1)S(1)}, bf16[128,384]{1,0:T(8,128)(2,1)S(1)}, u32[]{:S(2)}, u32[]{:S(2)}) collective-permute-start(bf16[128,384]{1,0:T(8,128)(2,1)S(1)} %copy-done.21), channel_id=1, source_target_pairs={{0,12},{4,8},{8,4},{12,0},{1,13},{5,9},{9,5},{13,1},{2,14},{6,10},... | collective-permute-start | bytes 294920 | tf_op jit(solution)/shard_map/ppermute | solution.py:23
  118.2 9.2 %collective-permute-start.31 = (bf16[128,384]{1,0:T(8,128)(2,1)S(1)}, bf16[128,384]{1,0:T(8,128)(2,1)S(1)}, u32[]{:S(2)}, u32[]{:S(2)}) collective-permute-start(bf16[128,384]{1,0:T(8,128)(2,1)S(1)} %get-tuple-element.76), channel_id=1, source_target_pairs={{0,1},{1,2},{2,3},{3,0},{4,5},{5,6},{6,7},{7,4},{8,9},{9,10},{10,1... | collective-permute-start | bytes 294920 | tf_op jit(solution)/shard_map/ppermute | solution.py:18
  122.4 6.3 %collective-permute-start.32 = (bf16[128,384]{1,0:T(8,128)(2,1)S(1)}, bf16[128,384]{1,0:T(8,128)(2,1)S(1)}, u32[]{:S(2)}, u32[]{:S(2)}) collective-permute-start(bf16[128,384]{1,0:T(8,128)(2,1)S(1)} %get-tuple-element.77), channel_id=1, source_target_pairs={{0,2},{1,3},{2,0},{3,1},{4,6},{5,7},{6,4},{7,5},{8,10},{9,11},{10,... | collective-permute-start | bytes 294920 | tf_op jit(solution)/shard_map/ppermute | solution.py:18
  124.0 6.4 %collective-permute-start.33 = (bf16[128,384]{1,0:T(8,128)(2,1)S(1)}, bf16[128,384]{1,0:T(8,128)(2,1)S(1)}, u32[]{:S(2)}, u32[]{:S(2)}) collective-permute-start(bf16[128,384]{1,0:T(8,128)(2,1)S(1)} %get-tuple-element.78), channel_id=1, source_target_pairs={{0,3},{1,0},{2,1},{3,2},{4,7},{5,4},{6,5},{7,6},{8,11},{9,8},{10,9... | collective-permute-start | bytes 294920 | tf_op jit(solution)/shard_map/ppermute | solution.py:18
  (15 other events, 34.1 us)

commit v2 on v1

--- a/solution.py
+++ b/solution.py
@@ -477,20 +477,19 @@
                 both[t, pl.ds(1, bins, stride=2), :] = jnp.concatenate(
                     [odd[:, part], *fill], axis=1
                 )
-                grad_acts = both[t][:, :size] * (slope_ref[q, :, part] * 0.5)
-                out_ref[q, part] = grad_acts.astype(BF16).T
-
-    turned = call(
+                grad_acts = both[t][:, :size]
+                out_ref[q, :, part] = (grad_acts * (slope_ref[q, :, part] * 0.5)).astype(BF16)
+
+    return call(
         body,
         [*grads, *projs, *edges, slope],
-        struct((seq_count, channels, positions), BF16),
+        struct(slope.shape, BF16),
         [
             pltpu.VMEM((ksize, bins + 16, channels), F32),
             pltpu.VMEM((len(tiles), positions, 128), F32),
         ],
         after,
     )
-    return jnp.swapaxes(turned, 1, 2)
 
 
 def kernel_tracks(kept, other, conv_weight, after):
@@ -655,8 +654,8 @@
     other = {}
     for u, p in payload.items():
         other[u ^ far] = swap_seq(p, far)
-    grad_input = back(grads, [slots[u] for u in order], edges, slope, last)
-    total, own_tracks, sends = tracks(kept[0], other[0], conv_weight, [grad_input])
+    total, own_tracks, sends = tracks(kept[0], other[0], conv_weight, last)
+    grad_input = back(grads, [slots[u] for u in order], edges, slope, [own_tracks])
     totals = {
         u: total if u == 0 else (kept[u] + other[u].astype(F32)).astype(BF16) for u in kept
     }

time: 134 us -> 126 us (0.940)
  starting transfers between devices: 62.1 us -> 48.6 us
  waiting for transfers between devices: 22.1 us -> 33.5 us
  local copies, waits for them, and re-layouts: 18.9 us -> 15.7 us
  other arithmetic: 3.06 us -> 0.46 us
    ppermute x12, waiting for transfers between devices: 2.12 us -> 16.6 us  [swap_seq(): return lax.ppermute(values, 'seq', [(i, i ^ bit) for i in range(count)])]
    ppermute x12, starting transfers between devices: 20.6 us -> 8.8 us  [swap_seq(): return lax.ppermute(values, 'seq', [(i, i ^ bit) for i in range(count)])]
    ppermute x18, starting transfers between devices: 34.9 us -> 32.6 us  [shift_chan(): lax.ppermute(values, 'chan', [(i, (i + step) % count) for i in range(coun...]
    ppermute x4, waiting for transfers between devices: 3.89 us -> 1.76 us  [edge_seq(): return lax.ppermute(values, 'seq', pairs)]
    pallas_call x1 -> x0, local copies, waits for them, and re-layouts: 1.66 us -> none  [call(): pl.pallas_call(run, in_specs=specs, out_specs=local_spec if single else [...]
    convert_element_type x2, other arithmetic: 1.79 us -> 0.21 us  [local(): payload[u] = kept[u].astype(BF16)]
    unnamed x60 -> x47, local copies, waits for them, and re-layouts: 11.2 us -> 9.74 us
  transfers between devices with their start and end apart: 34 -> 34, of which waited for: 11 -> 11; matrix products, arithmetic and copies ran while one was open for 6% -> 4% of each run, Pallas kernels for 14% -> 14%
where the time goes in v2:
time: 126 us; the launch traced here: 125 us
  starting transfers between devices  48.6 us (39%)
  waiting for transfers between devices  33.5 us (27%)
  Pallas kernels  25.9 us (21%)
  local copies, waits for them, and re-layouts  15.7 us (12%)
    ppermute x18, starting transfers between devices, shift_chan(): lax.ppermute(values, 'chan', [(i, (i + step) % count) for i in range(coun...  32.6 us
    pallas_call x11, Pallas kernels, call(): pl.pallas_call(run, in_specs=specs, out_specs=local_spec if single else [...  19.8 us
    ppermute x12, waiting for transfers between devices, swap_seq(): return lax.ppermute(values, 'seq', [(i, i ^ bit) for i in range(count)])  16.6 us
    ppermute x18, waiting for transfers between devices, shift_chan(): lax.ppermute(values, 'chan', [(i, (i + step) % count) for i in range(coun...  15.1 us
    unnamed x47, local copies, waits for them, and re-layouts  9.74 us
    ppermute x12, starting transfers between devices, swap_seq(): return lax.ppermute(values, 'seq', [(i, i ^ bit) for i in range(count)])  8.8 us
    ppermute x4, starting transfers between devices, edge_seq(): return lax.ppermute(values, 'seq', pairs)  7.26 us
    gather x1, local copies, waits for them, and re-layouts, local(): head_weight.at[my_ids]  4.26 us
  transfers between devices with their start and end apart: 34, of which 11 were waited for; matrix products, arithmetic and copies ran while one was open for 4% of the time, Pallas kernels for 14%

profile of v2, /device:TPU:0, one launch (start us, length us, event | category | flops | bytes accessed | tf_op | source)
XLA Modules:
  0.0 125.4 jit_solution(1398388396830392025)
XLA Ops:
  1.4 4.3 %gather_fusion = bf16[128,384]{1,0:T(8,128)(2,1)S(1)} fusion(bf16[7611,384]{1,0:T(8,128)(2,1)} %param.8, s32[1024]{0:T(1024)S(1)} %pad_clamp_fusion), kind=kCustom, calls=%fused_computation | custom fusion | bytes 197120 | tf_op jit(solution)/shard_map/gather | solution.py:595
  5.7 3.1 %collective-permute-start.2 = (bf16[128,384]{1,0:T(8,128)(2,1)S(1)}, bf16[128,384]{1,0:T(8,128)(2,1)S(1)}, u32[]{:S(2)}, u32[]{:S(2)}) collective-permute-start(bf16[128,384]{1,0:T(8,128)(2,1)S(1)} %gather_fusion), channel_id=1, source_target_pairs={{0,1},{1,2},{2,3},{3,0},{4,5},{5,6},{6,7},{7,4},{8,9},{9,10},{10,1... | collective-permute-start | bytes 294920 | tf_op jit(solution)/shard_map/ppermute | solution.py:18
  8.8 2.6 %collective-permute-start.3 = (bf16[128,384]{1,0:T(8,128)(2,1)S(1)}, bf16[128,384]{1,0:T(8,128)(2,1)S(1)}, u32[]{:S(2)}, u32[]{:S(2)}) collective-permute-start(bf16[128,384]{1,0:T(8,128)(2,1)S(1)} %gather_fusion), channel_id=1, source_target_pairs={{0,2},{1,3},{2,0},{3,1},{4,6},{5,7},{6,4},{7,5},{8,10},{9,11},{10,... | collective-permute-start | bytes 294920 | tf_op jit(solution)/shard_map/ppermute | solution.py:18
  11.4 1.3 %collective-permute-start.4 = (bf16[128,384]{1,0:T(8,128)(2,1)S(1)}, bf16[128,384]{1,0:T(8,128)(2,1)S(1)}, u32[]{:S(2)}, u32[]{:S(2)}) collective-permute-start(bf16[128,384]{1,0:T(8,128)(2,1)S(1)} %gather_fusion), channel_id=1, source_target_pairs={{0,3},{1,0},{2,1},{3,2},{4,7},{5,4},{6,5},{7,6},{8,11},{9,8},{10,9... | collective-permute-start | bytes 294920 | tf_op jit(solution)/shard_map/ppermute | solution.py:18
  12.7 1.2 copy-done.3
  13.9 2.4 %shard_map.85 = (bf16[5,3,256,320]{3,2,1,0:T(8,128)(2,1)S(1)}, f32[3,512,320]{2,1,0:T(8,128)S(1)}, bf16[5,320,1536]{2,1,0:T(8,128)(2,1)S(1)}) custom-call(bf16[3,320,512]{2,1,0:T(8,128)(2,1)S(1)} %bitcast.5, bf16[5,320,1536]{2,1,0:T(8,128)(2,1)} %w_ref.1), custom_call_target="tpu_custom_call" | custom-call | tf_op jit(solution)/shard_map/pallas_call | solution.py:230
  16.4 1.5 %collective-permute-done.3.refs_3_ = bf16[128,384]{1,0:T(8,128)(2,1)S(1)} collective-permute-done((bf16[128,384]{1,0:T(8,128)(2,1)S(1)}, bf16[128,384]{1,0:T(8,128)(2,1)S(1)}, u32[]{:S(2)}, u32[]{:S(2)}) %collective-permute-start.3) | collective-permute-done | bytes 98336 | tf_op jit(solution)/shard_map/ppermute | solution.py:18
  17.9 1.3 %copy-done.5 = bf16[128,384]{1,0:T(8,128)(2,1)} copy-done((bf16[128,384]{1,0:T(8,128)(2,1)}, bf16[128,384]{1,0:T(8,128)(2,1)S(1)}, u32[]{:S(2)}) %copy-start.5) | copy-done | bytes 98328
  21.7 2.0 %shard_map.86 = (bf16[5,320,128]{2,1,0:T(8,128)(2,1)S(1)}, bf16[128,384]{1,0:T(8,128)(2,1)S(1)}, bf16[128,384]{1,0:T(8,128)(2,1)S(1)}, bf16[128,384]{1,0:T(8,128)(2,1)S(1)}, bf16[128,384]{1,0:T(8,128)(2,1)S(1)}) custom-call(s32[2]{0:T(128)S(1)} %pad_add_fusion.refs_0_, bf16[128,384]{1,0:T(8,128)(2,1)S(1)} %gather_fusion, ...), custom_call_target="tpu_custom_call" | custom-call | tf_op jit(solution)/shard_map/pallas_call | solution.py:190
  24.4 1.6 %collective-permute-start.9 = (bf16[5,320,128]{2,1,0:T(8,128)(2,1)S(1)}, bf16[5,320,128]{2,1,0:T(8,128)(2,1)}, u32[]{:S(2)}, u32[]{:S(2)}) collective-permute-start(bf16[5,320,128]{2,1,0:T(8,128)(2,1)S(1)} %get-tuple-element.45.refs_0_.refs_2_.refs_3_), channel_id=1, source_target_pairs={{0,8},{4,12},{8,0},{12,4},{1,9},{5,13},{9,1},{13,5},{2,10},{6,14},... | collective-permute-start | bytes 1228808 | tf_op jit(solution)/shard_map/ppermute | solution.py:23
  26.9 1.1 copy.14.last_ref
  28.0 2.1 %collective-permute-start = (bf16[3,2,320]{2,1,0:T(2,128)(2,1)S(1)}, bf16[3,2,320]{2,1,0:T(2,128)(2,1)S(1)}, u32[]{:S(2)}, u32[]{:S(2)}) collective-permute-start(bf16[3,2,320]{2,1,0:T(2,128)(2,1)S(1)} %copy.14.last_ref), channel_id=1, source_target_pairs={{0,4},{4,8},{8,12},{1,5},{5,9},{9,13},{2,6},{6,10},{10,14},{3,7},{... | collective-permute-start | bytes 11528 | tf_op jit(solution)/shard_map/ppermute | solution.py:29
  30.1 1.1 copy.13.first_ref
  31.2 1.3 %collective-permute-start.1 = (bf16[3,2,320]{2,1,0:T(2,128)(2,1)S(1)}, bf16[3,2,320]{2,1,0:T(2,128)(2,1)S(1)}, u32[]{:S(2)}, u32[]{:S(2)}) collective-permute-start(bf16[3,2,320]{2,1,0:T(2,128)(2,1)S(1)} %copy.13.first_ref), channel_id=1, source_target_pairs={{4,0},{8,4},{12,8},{5,1},{9,5},{13,9},{6,2},{10,6},{14,10},{7,3},{... | collective-permute-start | bytes 11528 | tf_op jit(solution)/shard_map/ppermute | solution.py:29
  32.5 1.8 %collective-permute-done.1.tail_ref = bf16[3,2,320]{2,1,0:T(2,128)(2,1)S(1)} collective-permute-done((bf16[3,2,320]{2,1,0:T(2,128)(2,1)S(1)}, bf16[3,2,320]{2,1,0:T(2,128)(2,1)S(1)}, u32[]{:S(2)}, u32[]{:S(2)}) %collective-permute-start.1) | collective-permute-done | bytes 3872 | tf_op jit(solution)/shard_map/ppermute | solution.py:29
  34.9 2.2 %shard_map.88 = (f32[3,64,256]{2,1,0:T(8,128)S(1)}, bf16[3,64,256]{2,1,0:T(8,128)(2,1)S(1)}, bf16[3,64,256]{2,1,0:T(8,128)(2,1)S(1)}, bf16[3,64,256]{2,1,0:T(8,128)(2,1)S(1)}) custom-call(s32[2]{0:T(128)S(1)} %copy-done.18, bf16[5,3,256,320]{3,2,1,0:T(8,128)(2,1)S(1)} %shard_map.87.refs_1_, ...), custom_call_target="tpu_custom_call" | custom-call | tf_op jit(solution)/shard_map/pallas_call | solution.py:190
  37.2 2.4 %collective-permute-start.10 = (bf16[5,320,128]{2,1,0:T(8,128)(2,1)}, bf16[5,320,128]{2,1,0:T(8,128)(2,1)S(1)}, u32[]{:S(2)}, u32[]{:S(2)}) collective-permute-start(bf16[5,320,128]{2,1,0:T(8,128)(2,1)} %collective-permute-done.9.refs_2_.refs_5_), channel_id=1, source_target_pairs={{0,4},{4,0},{8,12},{12,8},{1,5},{5,1},{9,13},{13,9},{2,6},{6,2},{1... | collective-permute-start | bytes 1228808 | tf_op jit(solution)/shard_map/ppermute | solution.py:23
  39.6 1.3 %collective-permute-start.6 = (bf16[3,64,256]{2,1,0:T(8,128)(2,1)S(1)}, bf16[3,64,256]{2,1,0:T(8,128)(2,1)S(1)}, u32[]{:S(2)}, u32[]{:S(2)}) collective-permute-start(bf16[3,64,256]{2,1,0:T(8,128)(2,1)S(1)} %get-tuple-element.52), channel_id=1, source_target_pairs={{0,1},{1,2},{2,3},{3,0},{4,5},{5,6},{6,7},{7,4},{8,9},{9,10},{10,1... | collective-permute-start | bytes 294920 | tf_op jit(solution)/shard_map/ppermute | solution.py:18
  40.9 2.3 %collective-permute-start.7 = (bf16[3,64,256]{2,1,0:T(8,128)(2,1)S(1)}, bf16[3,64,256]{2,1,0:T(8,128)(2,1)S(1)}, u32[]{:S(2)}, u32[]{:S(2)}) collective-permute-start(bf16[3,64,256]{2,1,0:T(8,128)(2,1)S(1)} %get-tuple-element.53), channel_id=1, source_target_pairs={{0,2},{1,3},{2,0},{3,1},{4,6},{5,7},{6,4},{7,5},{8,10},{9,11},{10,... | collective-permute-start | bytes 294920 | tf_op jit(solution)/shard_map/ppermute | solution.py:18
  43.5 2.2 %shard_map.90 = (f32[3,64,256]{2,1,0:T(8,128)S(1)}, bf16[3,64,256]{2,1,0:T(8,128)(2,1)S(1)}, bf16[3,64,256]{2,1,0:T(8,128)(2,1)S(1)}, bf16[3,64,256]{2,1,0:T(8,128)(2,1)S(1)}) custom-call(s32[2]{0:T(128)S(1)} %copy-done.18, bf16[5,3,256,320]{3,2,1,0:T(8,128)(2,1)S(1)} %shard_map.87.refs_1_, bf16[5,320,128]{2,1,0:T(8,128)(2,1)} %collective-permute-done.9.refs_2_.refs_5_, ...), custom_call_target="tpu_custom_call" | custom-call | tf_op jit(solution)/shard_map/pallas_call | solution.py:190
  45.8 1.7 %collective-permute-start.14 = (bf16[3,64,256]{2,1,0:T(8,128)(2,1)S(1)}, bf16[3,64,256]{2,1,0:T(8,128)(2,1)S(1)}, u32[]{:S(2)}, u32[]{:S(2)}) collective-permute-start(bf16[3,64,256]{2,1,0:T(8,128)(2,1)S(1)} %get-tuple-element.57), channel_id=1, source_target_pairs={{0,1},{1,2},{2,3},{3,0},{4,5},{5,6},{6,7},{7,4},{8,9},{9,10},{10,1... | collective-permute-start | bytes 294920 | tf_op jit(solution)/shard_map/ppermute | solution.py:18
  48.1 2.6 %collective-permute-start.16 = (bf16[3,64,256]{2,1,0:T(8,128)(2,1)S(1)}, bf16[3,64,256]{2,1,0:T(8,128)(2,1)S(1)}, u32[]{:S(2)}, u32[]{:S(2)}) collective-permute-start(bf16[3,64,256]{2,1,0:T(8,128)(2,1)S(1)} %get-tuple-element.59), channel_id=1, source_target_pairs={{0,3},{1,0},{2,1},{3,2},{4,7},{5,4},{6,5},{7,6},{8,11},{9,8},{10,9... | collective-permute-start | bytes 294920 | tf_op jit(solution)/shard_map/ppermute | solution.py:18
  50.7 3.2 %collective-permute-done.7.refs_3_ = bf16[3,64,256]{2,1,0:T(8,128)(2,1)S(1)} collective-permute-done((bf16[3,64,256]{2,1,0:T(8,128)(2,1)S(1)}, bf16[3,64,256]{2,1,0:T(8,128)(2,1)S(1)}, u32[]{:S(2)}, u32[]{:S(2)}) %collective-permute-start.7) | collective-permute-done | bytes 98336 | tf_op jit(solution)/shard_map/ppermute | solution.py:18
  54.7 4.0 %collective-permute-start.11 = (bf16[3,64,256]{2,1,0:T(8,128)(2,1)S(1)}, bf16[3,64,256]{2,1,0:T(8,128)(2,1)S(1)}, u32[]{:S(2)}, u32[]{:S(2)}) collective-permute-start(bf16[3,64,256]{2,1,0:T(8,128)(2,1)S(1)} %shard_map.91.refs_7_.refs_2_), channel_id=1, source_target_pairs={{0,1},{1,2},{2,3},{3,0},{4,5},{5,6},{6,7},{7,4},{8,9},{9,10},{10,1... | collective-permute-start | bytes 294920 | tf_op jit(solution)/shard_map/ppermute | solution.py:18
  59.5 1.7 %collective-permute-start.13 = (bf16[3,64,256]{2,1,0:T(8,128)(2,1)S(1)}, bf16[3,64,256]{2,1,0:T(8,128)(2,1)S(1)}, u32[]{:S(2)}, u32[]{:S(2)}) collective-permute-start(bf16[3,64,256]{2,1,0:T(8,128)(2,1)S(1)} %shard_map.91.refs_7_.refs_2_), channel_id=1, source_target_pairs={{0,3},{1,0},{2,1},{3,2},{4,7},{5,4},{6,5},{7,6},{8,11},{9,8},{10,9... | collective-permute-start | bytes 294920 | tf_op jit(solution)/shard_map/ppermute | solution.py:18
  61.1 1.4 %shard_map.89 = (bf16[5,320,768]{2,1,0:T(8,128)(2,1)S(1)}, bf16[128,384]{1,0:T(8,128)(2,1)S(1)}, bf16[128,384]{1,0:T(8,128)(2,1)S(1)}, bf16[128,384]{1,0:T(8,128)(2,1)S(1)}, bf16[128,384]{1,0:T(8,128)(2,1)S(1)}) custom-call(s32[2]{0:T(128)S(1)} %copy-done.18, bf16[5,3,256,320]{3,2,1,0:T(8,128)(2,1)S(1)} %shard_map.87.refs_1_, ...), custom_call_target="tpu_custom_call" | custom-call | tf_op jit(solution)/shard_map/pallas_call | solution.py:190
  63.2 4.2 %collective-permute-done.12.refs_4_ = bf16[3,64,256]{2,1,0:T(8,128)(2,1)S(1)} collective-permute-done((bf16[3,64,256]{2,1,0:T(8,128)(2,1)S(1)}, bf16[3,64,256]{2,1,0:T(8,128)(2,1)S(1)}, u32[]{:S(2)}, u32[]{:S(2)}) %collective-permute-start.12) | collective-permute-done | bytes 98336 | tf_op jit(solution)/shard_map/ppermute | solution.py:18
  67.3 1.4 %shard_map.93 = (bf16[3,256,256]{2,1,0:T(8,128)(2,1)S(1)}, bf16[3,1,256]{2,1,0:T(2,128)(2,1)S(1)}, bf16[3,1,256]{2,1,0:T(2,128)(2,1)S(1)}, f32[5,320,128]{2,1,0:T(8,128)S(1)}, bf16[5,320,128]{2,1,0:T(8,128)(2,1)S(1)}) custom-call(s32[2]{0:T(128)S(1)} %copy-done.18, bf16[5,320,768]{2,1,0:T(8,128)(2,1)S(1)} %get-tuple-element.51.refs_1_, ...), custom_call_target="tpu_custom_call" | custom-call | tf_op jit(solution)/shard_map/pallas_call | solution.py:190
  68.8 2.6 %collective-permute-start.17 = (bf16[3,64,256]{2,1,0:T(8,128)(2,1)S(1)}, bf16[3,64,256]{2,1,0:T(8,128)(2,1)S(1)}, u32[]{:S(2)}, u32[]{:S(2)}) collective-permute-start(bf16[3,64,256]{2,1,0:T(8,128)(2,1)S(1)} %shard_map.92.refs_6_.refs_2_), channel_id=1, source_target_pairs={{0,1},{1,2},{2,3},{3,0},{4,5},{5,6},{6,7},{7,4},{8,9},{9,10},{10,1... | collective-permute-start | bytes 294920 | tf_op jit(solution)/shard_map/ppermute | solution.py:18
  72.2 1.7 %collective-permute-start.19 = (bf16[3,64,256]{2,1,0:T(8,128)(2,1)S(1)}, bf16[3,64,256]{2,1,0:T(8,128)(2,1)S(1)}, u32[]{:S(2)}, u32[]{:S(2)}) collective-permute-start(bf16[3,64,256]{2,1,0:T(8,128)(2,1)S(1)} %shard_map.92.refs_6_.refs_2_), channel_id=1, source_target_pairs={{0,3},{1,0},{2,1},{3,2},{4,7},{5,4},{6,5},{7,6},{8,11},{9,8},{10,9... | collective-permute-start | bytes 294920 | tf_op jit(solution)/shard_map/ppermute | solution.py:18
  74.5 1.9 %collective-permute-done.17.refs_3_ = bf16[3,64,256]{2,1,0:T(8,128)(2,1)S(1)} collective-permute-done((bf16[3,64,256]{2,1,0:T(8,128)(2,1)S(1)}, bf16[3,64,256]{2,1,0:T(8,128)(2,1)S(1)}, u32[]{:S(2)}, u32[]{:S(2)}) %collective-permute-start.17) | collective-permute-done | bytes 98336 | tf_op jit(solution)/shard_map/ppermute | solution.py:18
  76.4 3.7 %collective-permute-done.18.refs_4_ = bf16[3,64,256]{2,1,0:T(8,128)(2,1)S(1)} collective-permute-done((bf16[3,64,256]{2,1,0:T(8,128)(2,1)S(1)}, bf16[3,64,256]{2,1,0:T(8,128)(2,1)S(1)}, u32[]{:S(2)}, u32[]{:S(2)}) %collective-permute-start.18) | collective-permute-done | bytes 98336 | tf_op jit(solution)/shard_map/ppermute | solution.py:18
  80.1 1.4 %shard_map.95 = (bf16[3,256,256]{2,1,0:T(8,128)(2,1)S(1)}, bf16[3,1,256]{2,1,0:T(2,128)(2,1)S(1)}, bf16[3,1,256]{2,1,0:T(2,128)(2,1)S(1)}, f32[5,320,128]{2,1,0:T(8,128)S(1)}, bf16[5,320,128]{2,1,0:T(8,128)(2,1)S(1)}) custom-call(s32[2]{0:T(128)S(1)} %copy-done.18, bf16[5,320,768]{2,1,0:T(8,128)(2,1)S(1)} %get-tuple-element.51.refs_1_, ...), custom_call_target="tpu_custom_call" | custom-call | tf_op jit(solution)/shard_map/pallas_call | solution.py:190
  81.6 1.3 %collective-permute-start.24 = (bf16[5,320,128]{2,1,0:T(8,128)(2,1)S(1)}, bf16[5,320,128]{2,1,0:T(8,128)(2,1)S(1)}, u32[]{:S(2)}, u32[]{:S(2)}) collective-permute-start(bf16[5,320,128]{2,1,0:T(8,128)(2,1)S(1)} %fusion.refs_1_), channel_id=1, source_target_pairs={{0,8},{4,12},{8,0},{12,4},{1,9},{5,13},{9,1},{13,5},{2,10},{6,14},... | collective-permute-start | bytes 1228808 | tf_op jit(solution)/shard_map/ppermute | solution.py:23
  83.4 1.3 %collective-permute-start.25 = (bf16[5,320,128]{2,1,0:T(8,128)(2,1)S(1)}, bf16[5,320,128]{2,1,0:T(8,128)(2,1)S(1)}, u32[]{:S(2)}, u32[]{:S(2)}) collective-permute-start(bf16[5,320,128]{2,1,0:T(8,128)(2,1)S(1)} %get-tuple-element.84.refs_4_), channel_id=1, source_target_pairs={{0,8},{4,12},{8,0},{12,4},{1,9},{5,13},{9,1},{13,5},{2,10},{6,14},... | collective-permute-start | bytes 1228808 | tf_op jit(solution)/shard_map/ppermute | solution.py:23
  84.7 9.2 %collective-permute-done.24.refs_2_ = bf16[5,320,128]{2,1,0:T(8,128)(2,1)S(1)} collective-permute-done((bf16[5,320,128]{2,1,0:T(8,128)(2,1)S(1)}, bf16[5,320,128]{2,1,0:T(8,128)(2,1)S(1)}, u32[]{:S(2)}, u32[]{:S(2)}) %collective-permute-start.24) | collective-permute-done | bytes 409632 | tf_op jit(solution)/shard_map/ppermute | solution.py:23
  94.0 2.6 %shard_map.96 = (bf16[5,320,128]{2,1,0:T(8,128)(2,1)S(1)}, f32[128,384]{1,0:T(8,128)S(1)}, bf16[128,384]{1,0:T(8,128)(2,1)}, bf16[128,384]{1,0:T(8,128)(2,1)}, bf16[128,384]{1,0:T(8,128)(2,1)}) custom-call(s32[2]{0:T(128)S(1)} %copy-done.18, f32[5,320,128]{2,1,0:T(8,128)S(1)} %get-tuple-element.85.refs_1_, ...), custom_call_target="tpu_custom_call" | custom-call | tf_op jit(solution)/shard_map/pallas_call | solution.py:190
  96.6 5.6 %collective-permute-done.25 = bf16[5,320,128]{2,1,0:T(8,128)(2,1)S(1)} collective-permute-done((bf16[5,320,128]{2,1,0:T(8,128)(2,1)S(1)}, bf16[5,320,128]{2,1,0:T(8,128)(2,1)S(1)}, u32[]{:S(2)}, u32[]{:S(2)}) %collective-permute-start.25) | collective-permute-done | bytes 409632 | tf_op jit(solution)/shard_map/ppermute | solution.py:23
  102.9 1.2 collective-permute-start.29
  104.4 2.6 %collective-permute-start.22 = (bf16[3,1,512]{2,1,0:T(2,128)(2,1)S(1)}, bf16[3,1,512]{2,1,0:T(2,128)(2,1)S(1)}, u32[]{:S(2)}, u32[]{:S(2)}) collective-permute-start(bf16[3,1,512]{2,1,0:T(2,128)(2,1)S(1)} %pad_maximum_fusion.1), channel_id=1, source_target_pairs={{0,4},{4,8},{8,12},{1,5},{5,9},{9,13},{2,6},{6,10},{10,14},{3,7},{... | collective-permute-start | bytes 9224 | tf_op jit(solution)/shard_map/ppermute | solution.py:29
  107.0 1.2 collective-permute-done.29.refs_6_
  108.3 1.3 %collective-permute-start.21 = (bf16[3,1,512]{2,1,0:T(2,128)(2,1)S(1)}, bf16[3,1,512]{2,1,0:T(2,128)(2,1)S(1)}, u32[]{:S(2)}, u32[]{:S(2)}) collective-permute-start(bf16[3,1,512]{2,1,0:T(2,128)(2,1)S(1)} %pad_maximum_fusion), channel_id=1, source_target_pairs={{4,0},{8,4},{12,8},{5,1},{9,5},{13,9},{6,2},{10,6},{14,10},{7,3},{... | collective-permute-start | bytes 9224 | tf_op jit(solution)/shard_map/ppermute | solution.py:29
  109.6 2.6 %collective-permute-start.31 = (bf16[128,384]{1,0:T(8,128)(2,1)}, bf16[128,384]{1,0:T(8,128)(2,1)S(1)}, u32[]{:S(2)}, u32[]{:S(2)}) collective-permute-start(bf16[128,384]{1,0:T(8,128)(2,1)} %get-tuple-element.76), channel_id=1, source_target_pairs={{0,1},{1,2},{2,3},{3,0},{4,5},{5,6},{6,7},{7,4},{8,9},{9,10},{10,1... | collective-permute-start | bytes 294920 | tf_op jit(solution)/shard_map/ppermute | solution.py:18
  112.2 1.4 %collective-permute-start.32 = (bf16[128,384]{1,0:T(8,128)(2,1)}, bf16[128,384]{1,0:T(8,128)(2,1)}, u32[]{:S(2)}, u32[]{:S(2)}) collective-permute-start(bf16[128,384]{1,0:T(8,128)(2,1)} %get-tuple-element.77), channel_id=1, source_target_pairs={{0,2},{1,3},{2,0},{3,1},{4,6},{5,7},{6,4},{7,5},{8,10},{9,11},{10,... | collective-permute-start | bytes 294920 | tf_op jit(solution)/shard_map/ppermute | solution.py:18
  113.6 1.1 collective-permute-start.33
  114.8 4.8 %shard_map.97 = bf16[3,512,320]{2,1,0:T(8,128)(2,1)S(1)} custom-call(s32[2]{0:T(128)S(1)} %copy-done.18, bf16[3,256,256]{2,1,0:T(8,128)(2,1)S(1)} %get-tuple-element.60.refs_1_, bf16[3,256,256]{2,1,0:T(8,128)(2,1)S(1)} %get-tuple-element.63.refs_2_, bf16[5,320,128]{2,1,0:T(8,128)(2,1)S(1)} %get-tuple-element.45.refs_0_.refs_2_.refs_3_, ...), custom_call_target="tpu_custom_call" | custom-call | tf_op jit(solution)/shard_map/pallas_call | solution.py:190
  119.6 1.4 %copy.12 = bf16[3,512,320]{1,2,0:T(8,128)(2,1)} copy(bf16[3,512,320]{2,1,0:T(8,128)(2,1)S(1)} %shard_map.97) | data formatting | bytes 1966080
  121.6 3.6 %shard_map.98 = (f32[5,320,384]{2,1,0:T(8,128)}, f32[128,384]{1,0:T(8,128)}) custom-call(bf16[5,320,128]{2,1,0:T(8,128)(2,1)S(1)} %add_convert_fusion.refs_0_, bf16[5,320,128]{2,1,0:T(8,128)(2,1)} %collective-permute-done.26.refs_1_, bf16[5,320,128]{2,1,0:T(8,128)(2,1)S(1)} %get-tuple-element.71.refs_2_, ...), custom_call_target="tpu_custom_call" | custom-call | tf_op jit(solution)/shard_map/pallas_call | solution.py:553
  (94 shorter events, 12.4 us)
Async XLA Ops:
  5.7 10.8 %collective-permute-start.2 = (bf16[128,384]{1,0:T(8,128)(2,1)S(1)}, bf16[128,384]{1,0:T(8,128)(2,1)S(1)}, u32[]{:S(2)}, u32[]{:S(2)}) collective-permute-start(bf16[128,384]{1,0:T(8,128)(2,1)S(1)} %gather_fusion), channel_id=1, source_target_pairs={{0,1},{1,2},{2,3},{3,0},{4,5},{5,6},{6,7},{7,4},{8,9},{9,10},{10,1... | collective-permute-start | bytes 294920 | tf_op jit(solution)/shard_map/ppermute | solution.py:18
  8.8 9.2 %collective-permute-start.3 = (bf16[128,384]{1,0:T(8,128)(2,1)S(1)}, bf16[128,384]{1,0:T(8,128)(2,1)S(1)}, u32[]{:S(2)}, u32[]{:S(2)}) collective-permute-start(bf16[128,384]{1,0:T(8,128)(2,1)S(1)} %gather_fusion), channel_id=1, source_target_pairs={{0,2},{1,3},{2,0},{3,1},{4,6},{5,7},{6,4},{7,5},{8,10},{9,11},{10,... | collective-permute-start | bytes 294920 | tf_op jit(solution)/shard_map/ppermute | solution.py:18
  11.4 7.9 %collective-permute-start.4 = (bf16[128,384]{1,0:T(8,128)(2,1)S(1)}, bf16[128,384]{1,0:T(8,128)(2,1)S(1)}, u32[]{:S(2)}, u32[]{:S(2)}) collective-permute-start(bf16[128,384]{1,0:T(8,128)(2,1)S(1)} %gather_fusion), channel_id=1, source_target_pairs={{0,3},{1,0},{2,1},{3,2},{4,7},{5,4},{6,5},{7,6},{8,11},{9,8},{10,9... | collective-permute-start | bytes 294920 | tf_op jit(solution)/shard_map/ppermute | solution.py:18
  16.3 7.4 %copy-start = (bf16[5,320,1536]{2,1,0:T(8,128)(2,1)}, bf16[5,320,1536]{2,1,0:T(8,128)(2,1)S(1)}, u32[]{:S(2)}) copy-start(bf16[5,320,1536]{2,1,0:T(8,128)(2,1)S(1)} %get-tuple-element.43.refs_5_.refs_3_) | copy-start | bytes 14745604
  16.3 7.4 %copy-start.1 = (f32[3,512,320]{2,1,0:T(8,128)}, f32[3,512,320]{2,1,0:T(8,128)S(1)}, u32[]{:S(2)}) copy-start(f32[3,512,320]{2,1,0:T(8,128)S(1)} %get-tuple-element.44.refs_6_.refs_9_) | copy-start | bytes 5898244
  24.3 2.6 %copy-start.11 = (bf16[128,384]{1,0:T(8,128)(2,1)}, bf16[128,384]{1,0:T(8,128)(2,1)S(1)}, u32[]{:S(2)}) copy-start(bf16[128,384]{1,0:T(8,128)(2,1)S(1)} %get-tuple-element.47.refs_3_) | copy-start | bytes 294916
  24.3 2.6 %copy-start.13 = (bf16[128,384]{1,0:T(8,128)(2,1)}, bf16[128,384]{1,0:T(8,128)(2,1)S(1)}, u32[]{:S(2)}) copy-start(bf16[128,384]{1,0:T(8,128)(2,1)S(1)} %get-tuple-element.48.refs_4_) | copy-start | bytes 294916
  24.3 2.6 %copy-start.15 = (bf16[128,384]{1,0:T(8,128)(2,1)}, bf16[128,384]{1,0:T(8,128)(2,1)S(1)}, u32[]{:S(2)}) copy-start(bf16[128,384]{1,0:T(8,128)(2,1)S(1)} %get-tuple-element.49.refs_5_) | copy-start | bytes 294916
  24.3 10.0 %collective-permute-start.5 = (bf16[5,320,128]{2,1,0:T(8,128)(2,1)S(1)}, bf16[5,320,128]{2,1,0:T(8,128)(2,1)}, u32[]{:S(2)}, u32[]{:S(2)}) collective-permute-start(bf16[5,320,128]{2,1,0:T(8,128)(2,1)S(1)} %get-tuple-element.45.refs_0_.refs_2_.refs_3_), channel_id=1, source_target_pairs={{0,4},{4,0},{8,12},{12,8},{1,5},{5,1},{9,13},{13,9},{2,6},{6,2},{1... | collective-permute-start | bytes 1228808 | tf_op jit(solution)/shard_map/ppermute | solution.py:23
  24.4 12.8 %collective-permute-start.9 = (bf16[5,320,128]{2,1,0:T(8,128)(2,1)S(1)}, bf16[5,320,128]{2,1,0:T(8,128)(2,1)}, u32[]{:S(2)}, u32[]{:S(2)}) collective-permute-start(bf16[5,320,128]{2,1,0:T(8,128)(2,1)S(1)} %get-tuple-element.45.refs_0_.refs_2_.refs_3_), channel_id=1, source_target_pairs={{0,8},{4,12},{8,0},{12,4},{1,9},{5,13},{9,1},{13,5},{2,10},{6,14},... | collective-permute-start | bytes 1228808 | tf_op jit(solution)/shard_map/ppermute | solution.py:23
  28.0 4.5 %collective-permute-start = (bf16[3,2,320]{2,1,0:T(2,128)(2,1)S(1)}, bf16[3,2,320]{2,1,0:T(2,128)(2,1)S(1)}, u32[]{:S(2)}, u32[]{:S(2)}) collective-permute-start(bf16[3,2,320]{2,1,0:T(2,128)(2,1)S(1)} %copy.14.last_ref), channel_id=1, source_target_pairs={{0,4},{4,8},{8,12},{1,5},{5,9},{9,13},{2,6},{6,10},{10,14},{3,7},{... | collective-permute-start | bytes 11528 | tf_op jit(solution)/shard_map/ppermute | solution.py:29
  31.2 3.1 %collective-permute-start.1 = (bf16[3,2,320]{2,1,0:T(2,128)(2,1)S(1)}, bf16[3,2,320]{2,1,0:T(2,128)(2,1)S(1)}, u32[]{:S(2)}, u32[]{:S(2)}) collective-permute-start(bf16[3,2,320]{2,1,0:T(2,128)(2,1)S(1)} %copy.13.first_ref), channel_id=1, source_target_pairs={{4,0},{8,4},{12,8},{5,1},{9,5},{13,9},{6,2},{10,6},{14,10},{7,3},{... | collective-permute-start | bytes 11528 | tf_op jit(solution)/shard_map/ppermute | solution.py:29
  34.3 13.2 %copy-start.19 = (s32[3,64]{1,0:T(4,128)S(1)}, s32[3,64]{1,0:T(4,128)}, u32[]{:S(2)}) copy-start(s32[3,64]{1,0:T(4,128)} %param.10) | copy-start | bytes 2308
  37.1 16.9 %copy-start.4 = (s32[3,64,512]{2,1,0:T(8,128)S(1)}, s32[3,64,512]{2,1,0:T(8,128)}, u32[]{:S(2)}) copy-start(s32[3,64,512]{2,1,0:T(8,128)} %refs_5_.3) | copy-start | bytes 1179652
  37.2 24.0 %copy-start.10 = (bf16[128,384]{1,0:T(8,128)(2,1)S(1)}, bf16[128,384]{1,0:T(8,128)(2,1)}, u32[]{:S(2)}) copy-start(bf16[128,384]{1,0:T(8,128)(2,1)} %copy-done.9) | copy-start | bytes 294916
  37.2 24.0 %copy-start.12 = (bf16[128,384]{1,0:T(8,128)(2,1)S(1)}, bf16[128,384]{1,0:T(8,128)(2,1)}, u32[]{:S(2)}) copy-start(bf16[128,384]{1,0:T(8,128)(2,1)} %copy-done.11) | copy-start | bytes 294916
  37.2 24.0 %copy-start.14 = (bf16[128,384]{1,0:T(8,128)(2,1)S(1)}, bf16[128,384]{1,0:T(8,128)(2,1)}, u32[]{:S(2)}) copy-start(bf16[128,384]{1,0:T(8,128)(2,1)} %copy-done.13) | copy-start | bytes 294916
  37.2 23.9 %copy-start.16 = (bf16[128,384]{1,0:T(8,128)(2,1)S(1)}, bf16[128,384]{1,0:T(8,128)(2,1)}, u32[]{:S(2)}) copy-start(bf16[128,384]{1,0:T(8,128)(2,1)} %copy-done.15) | copy-start | bytes 294916
  37.2 6.3 %collective-permute-start.10 = (bf16[5,320,128]{2,1,0:T(8,128)(2,1)}, bf16[5,320,128]{2,1,0:T(8,128)(2,1)S(1)}, u32[]{:S(2)}, u32[]{:S(2)}) collective-permute-start(bf16[5,320,128]{2,1,0:T(8,128)(2,1)} %collective-permute-done.9.refs_2_.refs_5_), channel_id=1, source_target_pairs={{0,4},{4,0},{8,12},{12,8},{1,5},{5,1},{9,13},{13,9},{2,6},{6,2},{1... | collective-permute-start | bytes 1228808 | tf_op jit(solution)/shard_map/ppermute | solution.py:23
  39.6 8.5 %collective-permute-start.6 = (bf16[3,64,256]{2,1,0:T(8,128)(2,1)S(1)}, bf16[3,64,256]{2,1,0:T(8,128)(2,1)S(1)}, u32[]{:S(2)}, u32[]{:S(2)}) collective-permute-start(bf16[3,64,256]{2,1,0:T(8,128)(2,1)S(1)} %get-tuple-element.52), channel_id=1, source_target_pairs={{0,1},{1,2},{2,3},{3,0},{4,5},{5,6},{6,7},{7,4},{8,9},{9,10},{10,1... | collective-permute-start | bytes 294920 | tf_op jit(solution)/shard_map/ppermute | solution.py:18
  40.9 13.1 %collective-permute-start.7 = (bf16[3,64,256]{2,1,0:T(8,128)(2,1)S(1)}, bf16[3,64,256]{2,1,0:T(8,128)(2,1)S(1)}, u32[]{:S(2)}, u32[]{:S(2)}) collective-permute-start(bf16[3,64,256]{2,1,0:T(8,128)(2,1)S(1)} %get-tuple-element.53), channel_id=1, source_target_pairs={{0,2},{1,3},{2,0},{3,1},{4,6},{5,7},{6,4},{7,5},{8,10},{9,11},{10,... | collective-permute-start | bytes 294920 | tf_op jit(solution)/shard_map/ppermute | solution.py:18
  43.1 10.8 %collective-permute-start.8 = (bf16[3,64,256]{2,1,0:T(8,128)(2,1)S(1)}, bf16[3,64,256]{2,1,0:T(8,128)(2,1)S(1)}, u32[]{:S(2)}, u32[]{:S(2)}) collective-permute-start(bf16[3,64,256]{2,1,0:T(8,128)(2,1)S(1)} %get-tuple-element.54), channel_id=1, source_target_pairs={{0,3},{1,0},{2,1},{3,2},{4,7},{5,4},{6,5},{7,6},{8,11},{9,8},{10,9... | collective-permute-start | bytes 294920 | tf_op jit(solution)/shard_map/ppermute | solution.py:18
  45.8 13.7 %collective-permute-start.14 = (bf16[3,64,256]{2,1,0:T(8,128)(2,1)S(1)}, bf16[3,64,256]{2,1,0:T(8,128)(2,1)S(1)}, u32[]{:S(2)}, u32[]{:S(2)}) collective-permute-start(bf16[3,64,256]{2,1,0:T(8,128)(2,1)S(1)} %get-tuple-element.57), channel_id=1, source_target_pairs={{0,1},{1,2},{2,3},{3,0},{4,5},{5,6},{6,7},{7,4},{8,9},{9,10},{10,1... | collective-permute-start | bytes 294920 | tf_op jit(solution)/shard_map/ppermute | solution.py:18
  47.5 15.0 %collective-permute-start.15 = (bf16[3,64,256]{2,1,0:T(8,128)(2,1)S(1)}, bf16[3,64,256]{2,1,0:T(8,128)(2,1)S(1)}, u32[]{:S(2)}, u32[]{:S(2)}) collective-permute-start(bf16[3,64,256]{2,1,0:T(8,128)(2,1)S(1)} %get-tuple-element.58), channel_id=1, source_target_pairs={{0,2},{1,3},{2,0},{3,1},{4,6},{5,7},{6,4},{7,5},{8,10},{9,11},{10,... | collective-permute-start | bytes 294920 | tf_op jit(solution)/shard_map/ppermute | solution.py:18
  48.1 14.4 %collective-permute-start.16 = (bf16[3,64,256]{2,1,0:T(8,128)(2,1)S(1)}, bf16[3,64,256]{2,1,0:T(8,128)(2,1)S(1)}, u32[]{:S(2)}, u32[]{:S(2)}) collective-permute-start(bf16[3,64,256]{2,1,0:T(8,128)(2,1)S(1)} %get-tuple-element.59), channel_id=1, source_target_pairs={{0,3},{1,0},{2,1},{3,2},{4,7},{5,4},{6,5},{7,6},{8,11},{9,8},{10,9... | collective-permute-start | bytes 294920 | tf_op jit(solution)/shard_map/ppermute | solution.py:18
  54.7 8.5 %collective-permute-start.11 = (bf16[3,64,256]{2,1,0:T(8,128)(2,1)S(1)}, bf16[3,64,256]{2,1,0:T(8,128)(2,1)S(1)}, u32[]{:S(2)}, u32[]{:S(2)}) collective-permute-start(bf16[3,64,256]{2,1,0:T(8,128)(2,1)S(1)} %shard_map.91.refs_7_.refs_2_), channel_id=1, source_target_pairs={{0,1},{1,2},{2,3},{3,0},{4,5},{5,6},{6,7},{7,4},{8,9},{9,10},{10,1... | collective-permute-start | bytes 294920 | tf_op jit(solution)/shard_map/ppermute | solution.py:18
  58.7 8.7 %collective-permute-start.12 = (bf16[3,64,256]{2,1,0:T(8,128)(2,1)S(1)}, bf16[3,64,256]{2,1,0:T(8,128)(2,1)S(1)}, u32[]{:S(2)}, u32[]{:S(2)}) collective-permute-start(bf16[3,64,256]{2,1,0:T(8,128)(2,1)S(1)} %shard_map.91.refs_7_.refs_2_), channel_id=1, source_target_pairs={{0,2},{1,3},{2,0},{3,1},{4,6},{5,7},{6,4},{7,5},{8,10},{9,11},{10,... | collective-permute-start | bytes 294920 | tf_op jit(solution)/shard_map/ppermute | solution.py:18
  59.5 7.9 %collective-permute-start.13 = (bf16[3,64,256]{2,1,0:T(8,128)(2,1)S(1)}, bf16[3,64,256]{2,1,0:T(8,128)(2,1)S(1)}, u32[]{:S(2)}, u32[]{:S(2)}) collective-permute-start(bf16[3,64,256]{2,1,0:T(8,128)(2,1)S(1)} %shard_map.91.refs_7_.refs_2_), channel_id=1, source_target_pairs={{0,3},{1,0},{2,1},{3,2},{4,7},{5,4},{6,5},{7,6},{8,11},{9,8},{10,9... | collective-permute-start | bytes 294920 | tf_op jit(solution)/shard_map/ppermute | solution.py:18
  61.1 32.8 %slice-start = ((s8[4915200]{0:T(1024)(128)(4,1)}), s8[4194304]{0:T(1024)(128)(4,1)S(1)}, s32[]{:S(2)}) async-start(s8[4915200]{0:T(1024)(128)(4,1)} %bitcast.3), calls=%async_computation | async-start | bytes 8388608
  67.3 26.6 %slice-start.1 = ((s8[4915200]{0:T(1024)(128)(4,1)}), s8[720896]{0:T(1024)(128)(4,1)S(1)}, s32[]{:S(2)}) async-start(s8[4915200]{0:T(1024)(128)(4,1)} %bitcast.3), calls=%async_computation.1 | async-start | bytes 1441792
  68.7 5.2 %collective-permute-start.20 = (bf16[5,320,128]{2,1,0:T(8,128)(2,1)S(1)}, bf16[5,320,128]{2,1,0:T(8,128)(2,1)S(1)}, u32[]{:S(2)}, u32[]{:S(2)}) collective-permute-start(bf16[5,320,128]{2,1,0:T(8,128)(2,1)S(1)} %get-tuple-element.62), channel_id=1, source_target_pairs={{0,4},{4,0},{8,12},{12,8},{1,5},{5,1},{9,13},{13,9},{2,6},{6,2},{1... | collective-permute-start | bytes 1228808 | tf_op jit(solution)/shard_map/ppermute | solution.py:23
  68.8 7.6 %collective-permute-start.17 = (bf16[3,64,256]{2,1,0:T(8,128)(2,1)S(1)}, bf16[3,64,256]{2,1,0:T(8,128)(2,1)S(1)}, u32[]{:S(2)}, u32[]{:S(2)}) collective-permute-start(bf16[3,64,256]{2,1,0:T(8,128)(2,1)S(1)} %shard_map.92.refs_6_.refs_2_), channel_id=1, source_target_pairs={{0,1},{1,2},{2,3},{3,0},{4,5},{5,6},{6,7},{7,4},{8,9},{9,10},{10,1... | collective-permute-start | bytes 294920 | tf_op jit(solution)/shard_map/ppermute | solution.py:18
  71.4 8.6 %collective-permute-start.18 = (bf16[3,64,256]{2,1,0:T(8,128)(2,1)S(1)}, bf16[3,64,256]{2,1,0:T(8,128)(2,1)S(1)}, u32[]{:S(2)}, u32[]{:S(2)}) collective-permute-start(bf16[3,64,256]{2,1,0:T(8,128)(2,1)S(1)} %shard_map.92.refs_6_.refs_2_), channel_id=1, source_target_pairs={{0,2},{1,3},{2,0},{3,1},{4,6},{5,7},{6,4},{7,5},{8,10},{9,11},{10,... | collective-permute-start | bytes 294920 | tf_op jit(solution)/shard_map/ppermute | solution.py:18
  72.2 7.9 %collective-permute-start.19 = (bf16[3,64,256]{2,1,0:T(8,128)(2,1)S(1)}, bf16[3,64,256]{2,1,0:T(8,128)(2,1)S(1)}, u32[]{:S(2)}, u32[]{:S(2)}) collective-permute-start(bf16[3,64,256]{2,1,0:T(8,128)(2,1)S(1)} %shard_map.92.refs_6_.refs_2_), channel_id=1, source_target_pairs={{0,3},{1,0},{2,1},{3,2},{4,7},{5,4},{6,5},{7,6},{8,11},{9,8},{10,9... | collective-permute-start | bytes 294920 | tf_op jit(solution)/shard_map/ppermute | solution.py:18
  81.5 1.8 %collective-permute-start.23 = (bf16[5,320,128]{2,1,0:T(8,128)(2,1)S(1)}, bf16[5,320,128]{2,1,0:T(8,128)(2,1)S(1)}, u32[]{:S(2)}, u32[]{:S(2)}) collective-permute-start(bf16[5,320,128]{2,1,0:T(8,128)(2,1)S(1)} %get-tuple-element.69), channel_id=1, source_target_pairs={{0,4},{4,0},{8,12},{12,8},{1,5},{5,1},{9,13},{13,9},{2,6},{6,2},{1... | collective-permute-start | bytes 1228808 | tf_op jit(solution)/shard_map/ppermute | solution.py:23
  81.6 12.4 %collective-permute-start.24 = (bf16[5,320,128]{2,1,0:T(8,128)(2,1)S(1)}, bf16[5,320,128]{2,1,0:T(8,128)(2,1)S(1)}, u32[]{:S(2)}, u32[]{:S(2)}) collective-permute-start(bf16[5,320,128]{2,1,0:T(8,128)(2,1)S(1)} %fusion.refs_1_), channel_id=1, source_target_pairs={{0,8},{4,12},{8,0},{12,4},{1,9},{5,13},{9,1},{13,5},{2,10},{6,14},... | collective-permute-start | bytes 1228808 | tf_op jit(solution)/shard_map/ppermute | solution.py:23
  83.4 18.8 %collective-permute-start.25 = (bf16[5,320,128]{2,1,0:T(8,128)(2,1)S(1)}, bf16[5,320,128]{2,1,0:T(8,128)(2,1)S(1)}, u32[]{:S(2)}, u32[]{:S(2)}) collective-permute-start(bf16[5,320,128]{2,1,0:T(8,128)(2,1)S(1)} %get-tuple-element.84.refs_4_), channel_id=1, source_target_pairs={{0,8},{4,12},{8,0},{12,4},{1,9},{5,13},{9,1},{13,5},{2,10},{6,14},... | collective-permute-start | bytes 1228808 | tf_op jit(solution)/shard_map/ppermute | solution.py:23
  94.0 20.8 %copy-start.2 = (f32[3,512,320]{2,1,0:T(8,128)S(1)}, f32[3,512,320]{2,1,0:T(8,128)}, u32[]{:S(2)}) copy-start(f32[3,512,320]{2,1,0:T(8,128)} %copy-done.1) | copy-start | bytes 5898244
  96.6 25.1 %collective-permute-start.27 = (bf16[5,320,128]{2,1,0:T(8,128)(2,1)S(1)}, bf16[5,320,128]{2,1,0:T(8,128)(2,1)S(1)}, u32[]{:S(2)}, u32[]{:S(2)}) collective-permute-start(bf16[5,320,128]{2,1,0:T(8,128)(2,1)S(1)} %get-tuple-element.71.refs_2_), channel_id=1, source_target_pairs={{0,4},{4,0},{8,12},{12,8},{1,5},{5,1},{9,13},{13,9},{2,6},{6,2},{1... | collective-permute-start | bytes 1228808 | tf_op jit(solution)/shard_map/ppermute | solution.py:23
  102.3 19.3 %collective-permute-start.26 = (bf16[5,320,128]{2,1,0:T(8,128)(2,1)S(1)}, bf16[5,320,128]{2,1,0:T(8,128)(2,1)}, u32[]{:S(2)}, u32[]{:S(2)}) collective-permute-start(bf16[5,320,128]{2,1,0:T(8,128)(2,1)S(1)} %add_convert_fusion.refs_0_), channel_id=1, source_target_pairs={{0,4},{4,0},{8,12},{12,8},{1,5},{5,1},{9,13},{13,9},{2,6},{6,2},{1... | collective-permute-start | bytes 1228808 | tf_op jit(solution)/shard_map/ppermute | solution.py:23
  102.4 1.9 %collective-permute-start.28 = (bf16[128,384]{1,0:T(8,128)(2,1)S(1)}, bf16[128,384]{1,0:T(8,128)(2,1)S(1)}, u32[]{:S(2)}, u32[]{:S(2)}) collective-permute-start(bf16[128,384]{1,0:T(8,128)(2,1)S(1)} %get-tuple-element.73), channel_id=1, source_target_pairs={{0,4},{4,0},{8,12},{12,8},{1,5},{5,1},{9,13},{13,9},{2,6},{6,2},{1... | collective-permute-start | bytes 294920 | tf_op jit(solution)/shard_map/ppermute | solution.py:23
  102.9 5.3 %collective-permute-start.29 = (bf16[128,384]{1,0:T(8,128)(2,1)S(1)}, bf16[128,384]{1,0:T(8,128)(2,1)S(1)}, u32[]{:S(2)}, u32[]{:S(2)}) collective-permute-start(bf16[128,384]{1,0:T(8,128)(2,1)S(1)} %get-tuple-element.74), channel_id=1, source_target_pairs={{0,8},{4,12},{8,0},{12,4},{1,9},{5,13},{9,1},{13,5},{2,10},{6,14},... | collective-permute-start | bytes 294920 | tf_op jit(solution)/shard_map/ppermute | solution.py:23
  104.2 5.4 %collective-permute-start.30 = (bf16[128,384]{1,0:T(8,128)(2,1)S(1)}, bf16[128,384]{1,0:T(8,128)(2,1)S(1)}, u32[]{:S(2)}, u32[]{:S(2)}) collective-permute-start(bf16[128,384]{1,0:T(8,128)(2,1)S(1)} %get-tuple-element.75), channel_id=1, source_target_pairs={{0,12},{4,8},{8,4},{12,0},{1,13},{5,9},{9,5},{13,1},{2,14},{6,10},... | collective-permute-start | bytes 294920 | tf_op jit(solution)/shard_map/ppermute | solution.py:23
  104.4 7.8 %collective-permute-start.22 = (bf16[3,1,512]{2,1,0:T(2,128)(2,1)S(1)}, bf16[3,1,512]{2,1,0:T(2,128)(2,1)S(1)}, u32[]{:S(2)}, u32[]{:S(2)}) collective-permute-start(bf16[3,1,512]{2,1,0:T(2,128)(2,1)S(1)} %pad_maximum_fusion.1), channel_id=1, source_target_pairs={{0,4},{4,8},{8,12},{1,5},{5,9},{9,13},{2,6},{6,10},{10,14},{3,7},{... | collective-permute-start | bytes 9224 | tf_op jit(solution)/shard_map/ppermute | solution.py:29
  108.3 5.4 %collective-permute-start.21 = (bf16[3,1,512]{2,1,0:T(2,128)(2,1)S(1)}, bf16[3,1,512]{2,1,0:T(2,128)(2,1)S(1)}, u32[]{:S(2)}, u32[]{:S(2)}) collective-permute-start(bf16[3,1,512]{2,1,0:T(2,128)(2,1)S(1)} %pad_maximum_fusion), channel_id=1, source_target_pairs={{4,0},{8,4},{12,8},{5,1},{9,5},{13,9},{6,2},{10,6},{14,10},{7,3},{... | collective-permute-start | bytes 9224 | tf_op jit(solution)/shard_map/ppermute | solution.py:29
  109.6 11.4 %collective-permute-start.31 = (bf16[128,384]{1,0:T(8,128)(2,1)}, bf16[128,384]{1,0:T(8,128)(2,1)S(1)}, u32[]{:S(2)}, u32[]{:S(2)}) collective-permute-start(bf16[128,384]{1,0:T(8,128)(2,1)} %get-tuple-element.76), channel_id=1, source_target_pairs={{0,1},{1,2},{2,3},{3,0},{4,5},{5,6},{6,7},{7,4},{8,9},{9,10},{10,1... | collective-permute-start | bytes 294920 | tf_op jit(solution)/shard_map/ppermute | solution.py:18
  112.2 9.4 %collective-permute-start.32 = (bf16[128,384]{1,0:T(8,128)(2,1)}, bf16[128,384]{1,0:T(8,128)(2,1)}, u32[]{:S(2)}, u32[]{:S(2)}) collective-permute-start(bf16[128,384]{1,0:T(8,128)(2,1)} %get-tuple-element.77), channel_id=1, source_target_pairs={{0,2},{1,3},{2,0},{3,1},{4,6},{5,7},{6,4},{7,5},{8,10},{9,11},{10,... | collective-permute-start | bytes 294920 | tf_op jit(solution)/shard_map/ppermute | solution.py:18
  113.6 8.0 %collective-permute-start.33 = (bf16[128,384]{1,0:T(8,128)(2,1)}, bf16[128,384]{1,0:T(8,128)(2,1)}, u32[]{:S(2)}, u32[]{:S(2)}) collective-permute-start(bf16[128,384]{1,0:T(8,128)(2,1)} %get-tuple-element.78), channel_id=1, source_target_pairs={{0,3},{1,0},{2,1},{3,2},{4,7},{5,4},{6,5},{7,6},{8,11},{9,8},{10,9... | collective-permute-start | bytes 294920 | tf_op jit(solution)/shard_map/ppermute | solution.py:18
  (8 other events, 8.7 us)
